TPU v7x, 32 devices: a whole 2x2x4 slice. The times are simulated.
32 devices in a mesh: row: 4 (over y, x), col: 8 (over z, core).
Axes of the slice: x: 2, y: 2, z: 4, core: 2. Of those that a mesh axis runs over, the one named last changes fastest.
Arguments:
- tokens_in: bfloat16 [192, 8192], P('col', 'row'), may hold values from -6 to 6
- grad_out: bfloat16 [192, 8192], P('col', 'row'), may hold values from -6 to 6
- gate_weight: bfloat16 [8192, 28672], P('row', 'col'), may hold values from -0.09375 to 0.09375
- up_weight: bfloat16 [8192, 28672], P('row', 'col'), may hold values from -0.09375 to 0.09375
- down_weight: bfloat16 [28672, 8192], P('col', 'row'), may hold values from -0.046875 to 0.046875
- gate_mask: int32 [128, 448], P('row', 'col'), may hold values 0 or 1
- up_mask: int32 [128, 448], P('row', 'col'), may hold values 0 or 1
- down_mask: int32 [448, 128], P('col', 'row'), may hold values 0 or 1
Outputs:
- layer_out: bfloat16 [192, 8192], P('col', 'row')
- grad_in: bfloat16 [192, 8192], P('col', 'row')
- grad_gate: bfloat16 [8192, 28672], P('row', 'col')
- grad_up: bfloat16 [8192, 28672], P('row', 'col')
- grad_down: bfloat16 [28672, 8192], P('col', 'row')
Inputs may be any that keep to these rules, and one draw needn't show every extreme that they name: gate_mask holds only 0 and 1. up_mask holds only 0 and 1. down_mask holds only 0 and 1.
All inputs are finite; a program needn't handle non-finite values. No bound on the sum of `gate_mask` or of `up_mask` or of `down_mask` on one device may be relied on, other than what follows from the above.
Results may differ from a plain program's by a relative error of at most 0.0051.
Values may be sent and summed in bfloat16 or wider, within the bound.
No kernel may reach another device: no remote copies, remote signals or barrier semaphores. Data moves between devices by JAX's collectives and lax.ppermute only.
A program may use at most 448 MiB of HBM per device.

v0:
```python
import jax
import jax.numpy as jnp
from jax import lax
from jax.sharding import PartitionSpec as P


def expand_blocks(weight, blocks):
    rows_blk, cols_blk = blocks.shape
    height, width = weight.shape
    shaped = weight.reshape(rows_blk, height // rows_blk, cols_blk, width // cols_blk)
    return (shaped * blocks.astype(weight.dtype)[:, None, :, None]).reshape(height, width)


def contract(left_side, right_side, left_dim, right_dim):
    return lax.dot_general(
        left_side,
        right_side,
        (((left_dim,), (right_dim,)), ((), ())),
        preferred_element_type=jnp.float32,
    )


def local(tokens_in, grad_out, gate_weight, up_weight, down_weight, gate_mask, up_mask, down_mask):
    gate_kept = expand_blocks(gate_weight, gate_mask)
    up_kept = expand_blocks(up_weight, up_mask)
    down_kept = expand_blocks(down_weight, down_mask)
    all_tokens, all_grads = (
        lax.all_gather(tokens_in, "col", axis=0, tiled=True),
        lax.all_gather(grad_out, "col", axis=0, tiled=True),
    )
    gate_part = jnp.dot(all_tokens, gate_kept, preferred_element_type=jnp.float32)
    up_part = jnp.dot(all_tokens, up_kept, preferred_element_type=jnp.float32)
    gate_pre, up_pre = lax.psum((gate_part, up_part), "row")
    sig_gate = jax.nn.sigmoid(gate_pre)
    silu_gate = gate_pre * sig_gate
    hidden = (silu_gate * up_pre).astype(jnp.bfloat16)
    out_term = jnp.dot(hidden, down_kept, preferred_element_type=jnp.float32)
    layer_out = lax.psum_scatter(out_term, "col", scatter_dimension=0, tiled=True).astype(
        jnp.bfloat16
    )
    hidden_term = contract(all_grads, down_kept, 1, 1)
    grad_down = expand_blocks(contract(hidden, all_grads, 0, 0), down_mask).astype(jnp.bfloat16)
    grad_hidden = lax.psum(hidden_term, "row")
    grad_gate_pre = (grad_hidden * up_pre * sig_gate * (1.0 + gate_pre * (1.0 - sig_gate))).astype(
        jnp.bfloat16
    )
    grad_up_pre = (grad_hidden * silu_gate).astype(jnp.bfloat16)
    input_term = contract(grad_gate_pre, gate_kept, 1, 1) + contract(grad_up_pre, up_kept, 1, 1)
    grad_gate = expand_blocks(contract(all_tokens, grad_gate_pre, 0, 0), gate_mask).astype(
        jnp.bfloat16
    )
    grad_up = expand_blocks(contract(all_tokens, grad_up_pre, 0, 0), up_mask).astype(jnp.bfloat16)
    grad_in = lax.psum_scatter(input_term, "col", scatter_dimension=0, tiled=True).astype(
        jnp.bfloat16
    )
    return (layer_out, grad_in, grad_gate, grad_up, grad_down)


def solution(mesh):
    placed = (
        P("col", "row"),
        P("col", "row"),
        P("row", "col"),
        P("row", "col"),
        P("col", "row"),
        P("row", "col"),
        P("row", "col"),
        P("col", "row"),
    )
    return jax.shard_map(
        local,
        mesh=mesh,
        in_specs=placed,
        out_specs=(
            P("col", "row"),
            P("col", "row"),
            P("row", "col"),
            P("row", "col"),
            P("col", "row"),
        ),
        check_vma=False,
    )
```

profile of v0, /device:TPU:0, one launch (start us, length us, event | category | flops | bytes accessed | tf_op | source)
XLA Modules:
  0.0 587.5 jit_solution(8498510842173035679)
XLA Ops:
  7.2 0.8 fusion.22
  9.7 17.4 %all_gather.6 = bf16[192,2048]{1,0:T(8,128)(2,1)S(1)} all-gather(bf16[24,2048]{1,0:T(8,128)(2,1)} %param.8), channel_id=1, replica_groups=mesh['row'=4,'col'=8] {'col'}, dimensions={0}, use_global_device_ids=true | all-gather | bytes 884736 | tf_op jit(solution)/shard_map/all_gather | solution.py:28
  27.1 15.9 %all_gather.7 = bf16[192,2048]{1,0:T(8,128)(2,1)S(1)} all-gather(bf16[24,2048]{1,0:T(8,128)(2,1)} %param.9), channel_id=1, replica_groups=mesh['row'=4,'col'=8] {'col'}, dimensions={0}, use_global_device_ids=true | all-gather | bytes 884736 | tf_op jit(solution)/shard_map/all_gather | solution.py:29
  43.0 9.9 %mul.95 = bf16[56,64,32,64]{3,2,1,0:T(8,128)(2,1)} broadcast(bf16[56,32]{1,0:T(8,128)(2,1)S(1)} %copy.13), dimensions={0,2} | broadcast | bytes 14683648 | tf_op jit(solution)/shard_map/mul | solution.py:11
  52.9 40.3 %mul.96 = bf16[3584,2048]{1,0:T(8,128)(2,1)} reshape(bf16[56,64,32,64]{3,2,1,0:T(8,128)(2,1)} %mul.95) | data formatting | bytes 29360128 | tf_op jit(solution)/shard_map/mul | solution.py:11
  93.2 10.0 %mul.91 = bf16[32,64,56,64]{3,2,1,0:T(8,128)(2,1)} broadcast(bf16[32,56]{1,0:T(8,128)(2,1)S(1)} %get-tuple-element.19), dimensions={0,2} | broadcast | bytes 14683648 | tf_op jit(solution)/shard_map/mul | solution.py:11
  103.2 36.1 %mul.92 = bf16[2048,3584]{1,0:T(8,128)(2,1)} reshape(bf16[32,64,56,64]{3,2,1,0:T(8,128)(2,1)} %mul.91) | data formatting | bytes 29360128 | tf_op jit(solution)/shard_map/mul | solution.py:11
  139.3 10.0 %mul.87 = bf16[32,64,56,64]{3,2,1,0:T(8,128)(2,1)} broadcast(bf16[32,56]{1,0:T(8,128)(2,1)S(1)} %get-tuple-element.21), dimensions={0,2} | broadcast | bytes 14683648 | tf_op jit(solution)/shard_map/mul | solution.py:11
  149.3 36.1 %mul.88 = bf16[2048,3584]{1,0:T(8,128)(2,1)} reshape(bf16[32,64,56,64]{3,2,1,0:T(8,128)(2,1)} %mul.87) | data formatting | bytes 29360128 | tf_op jit(solution)/shard_map/mul | solution.py:11
  185.5 12.0 %mul.89 = bf16[2048,3584]{1,0:T(8,128)(2,1)S(1)} multiply(bf16[2048,3584]{1,0:T(8,128)(2,1)} %param.10, bf16[2048,3584]{1,0:T(8,128)(2,1)} %mul.88) | non-fusion elementwise | flops 7340032 | bytes 44040192 | tf_op jit(solution)/shard_map/mul | solution.py:11
  197.5 5.5 copy-done
  203.0 4.7 convolution_bitcast_fusion
  207.7 14.7 %fusion.10 = f32[192,3584]{1,0:T(8,128)} fusion(bf16[192,2048]{1,0:T(8,128)(2,1)S(1)} %all_gather.6, bf16[2048,3584]{1,0:T(8,128)(2,1)} %param.11, bf16[2048,3584]{1,0:T(8,128)(2,1)} %mul.92), kind=kOutput, calls=%fused_computation.13 | convolution fusion | flops 2825912320 | bytes 32899072 | tf_op jit(solution)/shard_map/dot_general | solution.py:32
  222.3 15.8 %fusion.13 = f32[192,3584]{1,0:T(8,128)} fusion(bf16[192,2048]{1,0:T(8,128)(2,1)S(1)} %all_gather.7, bf16[3584,2048]{1,0:T(8,128)(2,1)} %param.12, bf16[3584,2048]{1,0:T(8,128)(2,1)} %mul.96), kind=kOutput, calls=%fused_computation.14 | convolution fusion | flops 2825912320 | bytes 32899072 | tf_op jit(solution)/shard_map/dot_general | solution.py:15
  238.4 20.4 %mul.109 = f32[56,64,32,64]{3,2,1,0:T(8,128)} broadcast(f32[56,32]{1,0:T(8,128)S(1)} %copy.16), dimensions={0,2} | broadcast | bytes 29367296 | tf_op jit(solution)/shard_map/mul | solution.py:11
  258.8 48.1 %mul.110 = f32[3584,2048]{1,0:T(8,128)} reshape(f32[56,64,32,64]{3,2,1,0:T(8,128)} %mul.109) | data formatting | bytes 58720256 | tf_op jit(solution)/shard_map/mul | solution.py:11
  306.9 19.6 %mul.106 = f32[32,64,56,64]{1,0,3,2:T(8,128)} broadcast(f32[32,56]{0,1:T(8,128)S(1)} %copy.15), dimensions={0,2} | broadcast | bytes 29367296 | tf_op jit(solution)/shard_map/mul | solution.py:11
  326.5 50.9 %mul.107 = f32[2048,3584]{0,1:T(8,128)} reshape(f32[32,64,56,64]{1,0,3,2:T(8,128)} %mul.106) | data formatting | bytes 58720256 | tf_op jit(solution)/shard_map/mul | solution.py:11
  377.3 20.2 %mul.103 = f32[32,64,56,64]{1,0,3,2:T(8,128)} broadcast(f32[32,56]{0,1:T(8,128)S(1)} %copy.14), dimensions={0,2} | broadcast | bytes 29367296 | tf_op jit(solution)/shard_map/mul | solution.py:11
  397.5 49.8 %mul.104 = f32[2048,3584]{0,1:T(8,128)} reshape(f32[32,64,56,64]{1,0,3,2:T(8,128)} %mul.103) | data formatting | bytes 58720256 | tf_op jit(solution)/shard_map/mul | solution.py:11
  447.3 4.1 multiply_convert_fusion.1
  451.4 1.1 copy-done.3
  452.5 8.2 %fusion.23 = f32[192,2048]{1,0:T(8,128)S(1)} fusion(bf16[192,3584]{1,0:T(8,128)(2,1)S(1)} %get-tuple-element.14, bf16[2048,3584]{1,0:T(8,128)(2,1)} %copy-done), kind=kOutput, calls=%fused_computation.25 | convolution fusion | flops 2818572288 | bytes 17629184 | tf_op jit(solution)/shard_map/dot_general | solution.py:15
  460.7 13.4 %fusion.17 = f32[192,2048]{1,0:T(8,128)} fusion(f32[192,2048]{1,0:T(8,128)S(1)} %fusion.23, bf16[192,3584]{1,0:T(8,128)(2,1)S(1)} %get-tuple-element.13, bf16[2048,3584]{1,0:T(8,128)(2,1)} %param.11, bf16[2048,3584]{1,0:T(8,128)(2,1)} %mul.92), kind=kOutput, calls=%fused_computation.21 | convolution fusion | flops 2826305536 | bytes 33882112 | tf_op jit(solution)/shard_map/dot_general | solution.py:15
  474.2 13.9 %fusion.4 = f32[192,2048]{1,0:T(8,128)} fusion(bf16[192,3584]{1,0:T(8,128)(2,1)S(1)} %get-tuple-element.15, bf16[3584,2048]{1,0:T(8,128)(2,1)} %param.12, bf16[3584,2048]{1,0:T(8,128)(2,1)} %mul.96), kind=kOutput, calls=%fused_computation.7 | convolution fusion | flops 2825912320 | bytes 32309248 | tf_op jit(solution)/shard_map/dot_general | solution.py:37
  488.1 17.4 %fusion = bf16[2048,3584]{0,1:T(8,128)(2,1)} fusion(f32[2048,3584]{0,1:T(8,128)} %mul.107, bf16[192,3584]{1,0:T(8,128)(2,1)S(1)} %get-tuple-element.13, bf16[192,2048]{1,0:T(8,128)(2,1)S(1)} %copy-done.2), kind=kOutput, calls=%fused_computation.1 | convolution fusion | flops 2833252352 | bytes 46202880 | tf_op jit(solution)/shard_map/dot_general | solution.py:15
  505.5 17.7 %fusion.1 = bf16[2048,3584]{0,1:T(8,128)(2,1)} fusion(f32[2048,3584]{0,1:T(8,128)} %mul.104, bf16[192,3584]{1,0:T(8,128)(2,1)} %copy-done.3, bf16[192,2048]{1,0:T(8,128)(2,1)S(1)} %copy-done.2), kind=kOutput, calls=%fused_computation.3 | convolution fusion | flops 2833252352 | bytes 46202880 | tf_op jit(solution)/shard_map/dot_general | solution.py:15
  523.2 18.7 %copy.18 = bf16[2048,3584]{1,0:T(8,128)(2,1)} copy(bf16[2048,3584]{0,1:T(8,128)(2,1)} %fusion) | data formatting | bytes 29360128
  541.9 18.7 %copy.17 = bf16[2048,3584]{1,0:T(8,128)(2,1)} copy(bf16[2048,3584]{0,1:T(8,128)(2,1)} %fusion.1) | data formatting | bytes 29360128
  560.6 17.2 %multiply_convert_fusion = bf16[3584,2048]{1,0:T(8,128)(2,1)} fusion(f32[3584,2048]{1,0:T(8,128)} %mul.110, bf16[192,3584]{1,0:T(8,128)(2,1)S(1)} %get-tuple-element.15, bf16[192,2048]{1,0:T(8,128)(2,1)S(1)} %copy-done.5), kind=kOutput, calls=%fused_computation.4 | convolution fusion | flops 2833252352 | bytes 46202880 | tf_op jit(solution)/shard_map/dot_general | solution.py:15
  577.8 1.6 convert_element_type.49
  579.4 1.6 convert_element_type.46
  (25 shorter events, 2.1 us)
Async XLA Ops:
  7.2 440.1 %all-reduce.3.cloned.1.call-start = ((), (), s32[]{:S(2)}) async-start(), calls=%async_computation.4 | async-start | bytes 16515072 | tf_op jit(solution)/shard_map/psum | solution.py:33
  27.1 180.5 %copy-start.1 = (bf16[192,2048]{1,0:T(8,128)(2,1)}, bf16[192,2048]{1,0:T(8,128)(2,1)S(1)}, u32[]{:S(2)}) copy-start(bf16[192,2048]{1,0:T(8,128)(2,1)S(1)} %all_gather.6) | copy-start | bytes 2359300
  43.0 179.3 %copy-start.4 = (bf16[192,2048]{1,0:T(8,128)(2,1)}, bf16[192,2048]{1,0:T(8,128)(2,1)S(1)}, u32[]{:S(2)}) copy-start(bf16[192,2048]{1,0:T(8,128)(2,1)S(1)} %all_gather.7) | copy-start | bytes 2359300
  197.5 5.5 copy-start
  238.2 339.6 %reduce-scatter.5.cloned.1.call-start = ((), (), s32[]{:S(2)}) async-start(), calls=%async_computation.3 | async-start | bytes 1769472 | tf_op jit(solution)/shard_map/reduce_scatter | solution.py:53
  451.4 1.1 copy-start.3
  474.1 105.2 %reduce-scatter.3.cloned.1.call-start = ((), (), s32[]{:S(2)}) async-start(), calls=%async_computation.2 | async-start | bytes 1769472 | tf_op jit(solution)/shard_map/reduce_scatter | solution.py:38
  474.2 13.9 %copy-start.2 = (bf16[192,2048]{1,0:T(8,128)(2,1)S(1)}, bf16[192,2048]{1,0:T(8,128)(2,1)}, u32[]{:S(2)}) copy-start(bf16[192,2048]{1,0:T(8,128)(2,1)} %copy-done.1) | copy-start | bytes 2359300
  541.9 18.7 %copy-start.5 = (bf16[192,2048]{1,0:T(8,128)(2,1)S(1)}, bf16[192,2048]{1,0:T(8,128)(2,1)}, u32[]{:S(2)}) copy-start(bf16[192,2048]{1,0:T(8,128)(2,1)} %copy-done.4) | copy-start | bytes 2359300
Sparse Core Ops, SparseCore 0:
  238.3 172.3 all-reduce.2
  474.2 37.1 reduce-scatter.4
  513.9 32.0 reduce-scatter.2
where the time goes:
time: 597 us; the launch traced here: 587 us
  local copies, waits for them, and re-layouts  396 us (66%)
  matrix products  123 us (21%)
  blocking collectives  33.3 us (6%)
  other arithmetic  21.7 us (4%)
  between operations  13.8 us (2%)
    mul x12, local copies, waits for them, and re-layouts, expand_blocks(): shaped * blocks.astype(weight.dtype)[:, None, :, None]  351 us
    dot_general x6, matrix products, contract(): lax.dot_general(left_side, right_side, (((left_dim,), (right_dim,)), ((),...  89.6 us
    unnamed x14, local copies, waits for them, and re-layouts  44 us
    all_gather x1, blocking collectives, local(): lax.all_gather(tokens_in, 'col', axis=0, tiled=True)  17.4 us
    all_gather x1, blocking collectives, local(): lax.all_gather(grad_out, 'col', axis=0, tiled=True)  15.9 us
    dot_general x1, matrix products, local(): up_part = jnp.dot(all_tokens, up_kept, preferred_element_type=jnp.float32)  14.7 us
    dot_general x1, matrix products, local(): out_term = jnp.dot(hidden, down_kept, preferred_element_type=jnp.float32)  13.9 us
    mul x1, other arithmetic, expand_blocks(): shaped * blocks.astype(weight.dtype)[:, None, :, None]  12 us
  transfers between devices with their start and end apart: 3, of which 0 were waited for; matrix products, arithmetic and copies ran while one was open for 53% of the time, Pallas kernels for 0%

commit v1 on v0

v1 whole, which is shorter than its diff:
```python
import functools

import jax
import jax.numpy as jnp
from jax import lax
from jax.experimental import pallas as pl
from jax.experimental.pallas import tpu as pltpu
from jax.sharding import PartitionSpec as P

BF16 = jnp.bfloat16
F32 = jnp.float32
VMEM_LIMIT = 56 * 1024 * 1024
NT = (((1,), (1,)), ((), ()))


def dot(a, b):
    return jnp.dot(a, b, preferred_element_type=F32)


def spread(mask, first, width, block):
    count = mask.shape[-1]
    col = lax.broadcasted_iota(jnp.int32, (count, width), 1) // block + first
    row = lax.broadcasted_iota(jnp.int32, (count, width), 0)
    return dot(mask.astype(BF16), jnp.where(row == col, 1.0, 0.0).astype(BF16))


def masked_tile(w_ref, spread_mask, out_ref, block):
    width = w_ref.shape[1]
    for i in range(w_ref.shape[0] // block):
        keep = jnp.broadcast_to(spread_mask[i : i + 1, :], (block, width)).astype(BF16)
        out_ref[i * block : (i + 1) * block, :] = w_ref[i * block : (i + 1) * block, :] * keep


def load_quarters(refs, scratch):
    quarter = scratch.shape[0] // 4

    @pl.when(pl.program_id(0) == 0)
    def _():
        for j, ref in enumerate(refs):
            scratch[j * quarter : (j + 1) * quarter, :] = ref[0]


def quarter_specs(rows, width):
    return [
        pl.BlockSpec((1, rows, width), functools.partial(lambda i, me, j: (me[0] ^ j, 0, 0), j=j))
        for j in range(4)
    ]


def put_halves(part, send, keep, x_first):
    quarter = part.shape[0] // 4
    kept, sent = ((0, 2), (1, 3)) if x_first else ((0, 1), (2, 3))
    for slot in range(2):
        rows = slice(slot * quarter, (slot + 1) * quarter)
        keep[rows, :] = part[kept[slot] * quarter : (kept[slot] + 1) * quarter, :]
        send[rows, :] = part[sent[slot] * quarter : (sent[slot] + 1) * quarter, :].astype(BF16)


def join_halves(first, second, x_first):
    quarter = first.shape[0] // 2
    if not x_first:
        return jnp.concatenate([first[...], second[...]], axis=0)
    return jnp.concatenate(
        [first[:quarter, :], second[:quarter, :], first[quarter:, :], second[quarter:, :]], axis=0
    )


def params():
    return pltpu.CompilerParams(
        dimension_semantics=("arbitrary",), vmem_limit_bytes=VMEM_LIMIT
    )


def forward_part(me, tokens, weight, mask, tile, x_first):
    total, depth = tokens.shape
    quarter = total // 4
    width = weight.shape[1]
    block = depth // mask.shape[0]

    def body(me_ref, q0, q1, q2, q3, w_ref, m_ref, send, keep, x_s, w_s):
        load_quarters((q0, q1, q2, q3), x_s)
        m = spread(m_ref[...], pl.program_id(0) * (tile // block), tile, block)
        masked_tile(w_ref, m, w_s, block)
        put_halves(dot(x_s[...], w_s[...]), send, keep, x_first)

    split = tokens.reshape(4, quarter, depth)
    return pl.pallas_call(
        body,
        grid_spec=pltpu.PrefetchScalarGridSpec(
            num_scalar_prefetch=1,
            grid=(width // tile,),
            in_specs=quarter_specs(quarter, depth)
            + [
                pl.BlockSpec((depth, tile), lambda i, me: (0, i)),
                pl.BlockSpec(mask.shape, lambda i, me: (0, 0)),
            ],
            out_specs=[pl.BlockSpec((total // 2, tile), lambda i, me: (0, i))] * 2,
            scratch_shapes=[pltpu.VMEM((total, depth), BF16), pltpu.VMEM((depth, tile), BF16)],
        ),
        out_shape=[
            jax.ShapeDtypeStruct((total // 2, width), BF16),
            jax.ShapeDtypeStruct((total // 2, width), F32),
        ],
        compiler_params=params(),
        cost_estimate=pl.CostEstimate(
            flops=2 * total * depth * width,
            bytes_accessed=2 * depth * width + 3 * total * width,
            transcendentals=0,
        ),
        name="forward_part",
    )(me, split, split, split, split, weight, mask)


def hidden_part(me, grads, weight, mask, tile, first, steps, x_first):
    total, depth = grads.shape
    quarter = total // 4
    per = mask.shape[1]
    block = tile // per

    def body(me_ref, q0, q1, q2, q3, w_ref, m_ref, send, keep, x_s, w_s):
        load_quarters((q0, q1, q2, q3), x_s)
        m = spread(m_ref[0], 0, depth, block)
        masked_tile(w_ref, m, w_s, block)
        part = lax.dot_general(x_s[...], w_s[...], NT, preferred_element_type=F32)
        put_halves(part, send, keep, x_first)

    split = grads.reshape(4, quarter, depth)
    return pl.pallas_call(
        body,
        grid_spec=pltpu.PrefetchScalarGridSpec(
            num_scalar_prefetch=1,
            grid=(steps,),
            in_specs=quarter_specs(quarter, depth)
            + [
                pl.BlockSpec((tile, depth), lambda i, me: (i + first, 0)),
                pl.BlockSpec((1,) + mask.shape[1:], lambda i, me: (i + first, 0, 0)),
            ],
            out_specs=[pl.BlockSpec((total // 2, tile), lambda i, me: (0, i))] * 2,
            scratch_shapes=[pltpu.VMEM((total, depth), BF16), pltpu.VMEM((tile, depth), BF16)],
        ),
        out_shape=[
            jax.ShapeDtypeStruct((total // 2, steps * tile), BF16),
            jax.ShapeDtypeStruct((total // 2, steps * tile), F32),
        ],
        compiler_params=params(),
        cost_estimate=pl.CostEstimate(
            flops=2 * total * depth * steps * tile,
            bytes_accessed=2 * depth * steps * tile + 3 * total * steps * tile,
            transcendentals=0,
        ),
        name="hidden_part",
    )(me, split, split, split, split, weight, mask)


def put_owners(place, total, send, keep, owners):
    rows = total.shape[0] // owners
    per = owners // 4
    bits = owners.bit_length() - 1
    me, col = place[0], place[1]
    half = owners // 2
    for pair in range(owners // 2):
        pieces = []
        for spot in (2 * pair, 2 * pair + 1):
            step = sum(((spot >> b) & 1) << (bits - 1 - b) for b in range(bits))
            owner = col ^ step
            start = (((owner // per) ^ me) * per + owner % per) * rows
            pieces.append(total[pl.ds(pl.multiple_of(start, 8), rows), :])
        both = jnp.concatenate(pieces, axis=0)
        if pair < half // 2:
            keep[2 * pair * rows : (2 * pair + 2) * rows, :] = both
        else:
            at = 2 * pair - half
            send[at * rows : (at + 2) * rows, :] = both


def down_back(place, first_half, second_half, grads, weight, mask, tile, owners, x_first):
    total, depth = grads.shape
    quarter = total // 4
    width = weight.shape[0]
    per = mask.shape[1]
    block = tile // per

    def body(place_ref, q0, q1, q2, q3, h0, h1, w_ref, m_ref, gw, send, keep, g_s, w_s, acc):
        load_quarters((q0, q1, q2, q3), g_s)
        step = pl.program_id(0)
        m = spread(m_ref[0], 0, depth, block)
        masked_tile(w_ref, m, w_s, block)
        hid = join_halves(h0, h1, x_first)
        out = dot(hid, w_s[...])

        @pl.when(step == 0)
        def _():
            acc[...] = out

        @pl.when(step != 0)
        def _():
            acc[...] += out

        hid_t = hid.T
        for i in range(per):
            rows = slice(i * block, (i + 1) * block)
            gw[rows, :] = (dot(hid_t[rows, :], g_s[...]) * m[i : i + 1, :]).astype(BF16)

        @pl.when(step == pl.num_programs(0) - 1)
        def _():
            put_owners(place_ref, acc, send, keep, owners)

    split = grads.reshape(4, quarter, depth)
    return pl.pallas_call(
        body,
        grid_spec=pltpu.PrefetchScalarGridSpec(
            num_scalar_prefetch=1,
            grid=(width // tile,),
            in_specs=quarter_specs(quarter, depth)
            + [pl.BlockSpec((total // 2, tile), lambda i, me: (0, i))] * 2
            + [
                pl.BlockSpec((tile, depth), lambda i, me: (i, 0)),
                pl.BlockSpec((1,) + mask.shape[1:], lambda i, me: (i, 0, 0)),
            ],
            out_specs=[pl.BlockSpec((tile, depth), lambda i, me: (i, 0))]
            + [pl.BlockSpec((total // 2, depth), lambda i, me: (0, 0))] * 2,
            scratch_shapes=[
                pltpu.VMEM((total, depth), BF16),
                pltpu.VMEM((tile, depth), BF16),
                pltpu.VMEM((total, depth), F32),
            ],
        ),
        out_shape=[
            jax.ShapeDtypeStruct((width, depth), BF16),
            jax.ShapeDtypeStruct((total // 2, depth), F32),
            jax.ShapeDtypeStruct((total // 2, depth), F32),
        ],
        compiler_params=params(),
        cost_estimate=pl.CostEstimate(
            flops=4 * total * depth * width,
            bytes_accessed=4 * depth * width,
            transcendentals=0,
        ),
        name="down_back",
    )(place, split, split, split, split, first_half, second_half, weight, mask)


def input_back(place, gate_halves, up_halves, gate_w, up_w, gate_m, up_m, tile, owners):
    depth, width = gate_w.shape
    total = 2 * gate_halves[0].shape[0]
    block = depth // gate_m.shape[0]

    def body(place_ref, a0, a1, b0, b1, gw_ref, uw_ref, gm, um, send, keep, g_s, u_s, acc):
        step = pl.program_id(0)
        first = step * (tile // block)
        masked_tile(gw_ref, spread(gm[...], first, tile, block), g_s, block)
        masked_tile(uw_ref, spread(um[...], first, tile, block), u_s, block)
        out = lax.dot_general(
            join_halves(a0, a1, True), g_s[...], NT, preferred_element_type=F32
        ) + lax.dot_general(join_halves(b0, b1, False), u_s[...], NT, preferred_element_type=F32)

        @pl.when(step == 0)
        def _():
            acc[...] = out

        @pl.when(step != 0)
        def _():
            acc[...] += out

        @pl.when(step == pl.num_programs(0) - 1)
        def _():
            put_owners(place_ref, acc, send, keep, owners)

    return pl.pallas_call(
        body,
        grid_spec=pltpu.PrefetchScalarGridSpec(
            num_scalar_prefetch=1,
            grid=(width // tile,),
            in_specs=[pl.BlockSpec((total // 2, tile), lambda i, me: (0, i))] * 4
            + [pl.BlockSpec((depth, tile), lambda i, me: (0, i))] * 2
            + [pl.BlockSpec(gate_m.shape, lambda i, me: (0, 0))] * 2,
            out_specs=[pl.BlockSpec((total // 2, depth), lambda i, me: (0, 0))] * 2,
            scratch_shapes=[
                pltpu.VMEM((depth, tile), BF16),
                pltpu.VMEM((depth, tile), BF16),
                pltpu.VMEM((total, depth), F32),
            ],
        ),
        out_shape=[
            jax.ShapeDtypeStruct((total // 2, depth), F32),
            jax.ShapeDtypeStruct((total // 2, depth), F32),
        ],
        compiler_params=params(),
        cost_estimate=pl.CostEstimate(
            flops=4 * total * depth * width,
            bytes_accessed=4 * depth * width,
            transcendentals=0,
        ),
        name="input_back",
    )(place, *gate_halves, *up_halves, gate_w, up_w, gate_m, up_m)


def weight_back(me, gate_halves, up_halves, tokens, gate_m, up_m, tile):
    total, depth = tokens.shape
    quarter = total // 4
    width = gate_halves[0].shape[1]
    block = depth // gate_m.shape[0]
    rows_at_once = min(256, depth)

    def body(me_ref, q0, q1, q2, q3, a0, a1, b0, b1, gm, um, gg, gu, x_t):
        @pl.when(pl.program_id(0) == 0)
        def _():
            x_t[...] = jnp.concatenate([q0[0], q1[0], q2[0], q3[0]], axis=0).T

        first = pl.program_id(0) * (tile // block)
        for pre, mask, out in (
            (join_halves(a0, a1, True), gm, gg),
            (join_halves(b0, b1, False), um, gu),
        ):
            m = spread(mask[...], first, tile, block)
            for top in range(0, depth, rows_at_once):
                got = dot(x_t[top : top + rows_at_once, :], pre)
                for i in range(rows_at_once // block):
                    line = top // block + i
                    out[top + i * block : top + (i + 1) * block, :] = (
                        got[i * block : (i + 1) * block, :] * m[line : line + 1, :]
                    ).astype(BF16)

    split = tokens.reshape(4, quarter, depth)
    return pl.pallas_call(
        body,
        grid_spec=pltpu.PrefetchScalarGridSpec(
            num_scalar_prefetch=1,
            grid=(width // tile,),
            in_specs=quarter_specs(quarter, depth)
            + [pl.BlockSpec((total // 2, tile), lambda i, me: (0, i))] * 4
            + [pl.BlockSpec(gate_m.shape, lambda i, me: (0, 0))] * 2,
            out_specs=[pl.BlockSpec((depth, tile), lambda i, me: (0, i))] * 2,
            scratch_shapes=[pltpu.VMEM((depth, total), BF16)],
        ),
        out_shape=[jax.ShapeDtypeStruct((depth, width), BF16)] * 2,
        compiler_params=params(),
        cost_estimate=pl.CostEstimate(
            flops=4 * total * depth * width,
            bytes_accessed=4 * depth * width,
            transcendentals=0,
        ),
        name="weight_back",
    )(me, split, split, split, split, *gate_halves, *up_halves, gate_m, up_m)


def swap(value, axis, size, bit):
    return lax.ppermute(value, axis, [(i, i ^ bit) for i in range(size)])


def local(rows, cols, tokens_in, grad_out, gate_w, up_w, down_w, gate_mask, up_mask, down_mask):
    me = lax.axis_index("row").astype(jnp.int32)[None]
    place = jnp.stack([lax.axis_index("row"), lax.axis_index("col")]).astype(jnp.int32)
    width = gate_w.shape[1]
    tile = 256 if width % 256 == 0 else 128
    down_m = down_mask.reshape(width // tile, -1, down_mask.shape[1])

    def over_row(value, bit):
        return swap(value, "row", rows, bit)

    def leave(send, keep, x_first):
        first, second = (1, 2) if x_first else (2, 1)
        half = keep + over_row(send, first)
        quarter = half.shape[0] // 2
        return half[:quarter] + over_row(half[quarter:].astype(BF16), second)

    def collect(own, x_first):
        first, second = (2, 1) if x_first else (1, 2)
        near = jnp.concatenate([own, over_row(own, first)], axis=0)
        return near, over_row(near, second)

    def to_owner(send, keep):
        bit = 1
        while True:
            keep = keep + swap(send, "col", cols, bit)
            bit *= 2
            if bit == cols:
                return keep.astype(BF16)
            half = keep.shape[0] // 2
            keep, send = keep[:half], keep[half:].astype(BF16)

    tokens = lax.all_gather(tokens_in, "col", axis=0, tiled=True)
    gate_send, gate_keep = forward_part(me, tokens, gate_w, gate_mask, tile, True)
    up_send, up_keep = forward_part(me, tokens, up_w, up_mask, tile, False)
    up_send, grad_out = lax.optimization_barrier((up_send, grad_out))
    grads = lax.all_gather(grad_out, "col", axis=0, tiled=True)
    tiles = width // tile
    front = (tiles + 1) // 2
    part_a = hidden_part(me, grads, down_w, down_m, tile, 0, front, True)
    part_b = hidden_part(me, grads, down_w, down_m, tile, front, tiles - front, False)
    gate_pre = leave(gate_send, gate_keep, True)
    up_pre = leave(up_send, up_keep, False)
    sig = jax.nn.sigmoid(gate_pre)
    silu = gate_pre * sig
    hidden = collect((silu * up_pre).astype(BF16), False)
    grad_hidden = jnp.concatenate([leave(*part_a, True), leave(*part_b, False)], axis=1)
    grad_gate_pre = (grad_hidden * up_pre * sig * (1.0 + gate_pre * (1.0 - sig))).astype(BF16)
    grad_up_pre = (grad_hidden * silu).astype(BF16)
    gate_halves = collect(grad_gate_pre, True)
    up_halves = collect(grad_up_pre, False)
    grad_down, out_send, out_keep = down_back(
        place, *hidden, grads, down_w, down_m, tile, cols, False
    )
    in_send, in_keep = input_back(
        place, gate_halves, up_halves, gate_w, up_w, gate_mask, up_mask, tile, cols
    )
    grad_gate, grad_up = weight_back(me, gate_halves, up_halves, tokens, gate_mask, up_mask, tile)
    layer_out = to_owner(out_send, out_keep)
    grad_in = to_owner(in_send, in_keep)
    return (layer_out, grad_in, grad_gate, grad_up, grad_down)


def solution(mesh):
    by_row, by_col = P("row", "col"), P("col", "row")
    return jax.shard_map(
        functools.partial(local, mesh.shape["row"], mesh.shape["col"]),
        mesh=mesh,
        in_specs=(by_col, by_col, by_row, by_row, by_col, by_row, by_row, by_col),
        out_specs=(by_col, by_col, by_row, by_row, by_col),
        check_vma=False,
    )
```

time: 597 us -> 233 us (0.39); the launches traced: 587 us -> 230 us
  local copies, waits for them, and re-layouts: 396 us -> 3.05 us
  matrix products: 123 us -> 0 us
  Pallas kernels: 0 us -> 110 us
  waiting for transfers between devices: 0.05 us -> 56.8 us
  starting transfers between devices: 0.12 us -> 20.8 us
  other arithmetic: 21.7 us -> 3.34 us
  between operations: 13.8 us -> 0.9 us
    mul x12 -> x0, local copies, waits for them, and re-layouts: 351 us -> none  [expand_blocks(): shaped * blocks.astype(weight.dtype)[:, None, :, None]]
    dot_general x9 -> x0, matrix products: 123 us -> none  [the longest x6 89.6 us: contract(): lax.dot_general(left_side, right_side, (((left_dim,), (right_dim,)), ((),...]
    pallas_call x0 -> x7, Pallas kernels: none -> 110 us  [the longest x2 28.9 us: forward_part(): pl.pallas_call(body, grid_spec=pltpu.PrefetchScalarGridSpec(num_scalar_pr...]
    ppermute x0 -> x20, waiting for transfers between devices: none -> 56.8 us  [swap(): return lax.ppermute(value, axis, [(i, i ^ bit) for i in range(size)])]
    unnamed x14 -> x27, local copies, waits for them, and re-layouts: 44 us -> 2.87 us
    ppermute x0 -> x20, starting transfers between devices: none -> 20.8 us  [swap(): return lax.ppermute(value, axis, [(i, i ^ bit) for i in range(size)])]
    mul x1 -> x0, other arithmetic: 12 us -> none  [expand_blocks(): shaped * blocks.astype(weight.dtype)[:, None, :, None]]
    convert_element_type x6 -> x3, other arithmetic: 9.69 us -> 1.77 us  [the longest x2 1.32 us: to_owner(): return keep.astype(BF16)]
  transfers between devices with their start and end apart: 3 -> 20, of which waited for: 0 -> 11; matrix products, arithmetic and copies ran while one was open for 53% -> 1% of each run, Pallas kernels for 0% -> 38%
where the time goes in v1:
time: 233 us; the launch traced here: 230 us
  Pallas kernels  110 us (47%)
  waiting for transfers between devices  56.8 us (24%)
  blocking collectives  35.2 us (15%)
  starting transfers between devices  20.8 us (9%)
  other arithmetic  3.34 us (1%)
  local copies, waits for them, and re-layouts  3.05 us (1%)
    ppermute x20, waiting for transfers between devices, swap(): return lax.ppermute(value, axis, [(i, i ^ bit) for i in range(size)])  56.8 us
    pallas_call x2, Pallas kernels, forward_part(): pl.pallas_call(body, grid_spec=pltpu.PrefetchScalarGridSpec(num_scalar_pr...  28.9 us
    pallas_call x1, Pallas kernels, down_back(): pl.pallas_call(body, grid_spec=pltpu.PrefetchScalarGridSpec(num_scalar_pr...  25.3 us
    pallas_call x1, Pallas kernels, input_back(): pl.pallas_call(body, grid_spec=pltpu.PrefetchScalarGridSpec(num_scalar_pr...  23.1 us
    ppermute x20, starting transfers between devices, swap(): return lax.ppermute(value, axis, [(i, i ^ bit) for i in range(size)])  20.8 us
    all_gather x1, blocking collectives, local(): tokens = lax.all_gather(tokens_in, 'col', axis=0, tiled=True)  18.5 us
    pallas_call x2, Pallas kernels, hidden_part(): pl.pallas_call(body, grid_spec=pltpu.PrefetchScalarGridSpec(num_scalar_pr...  17.1 us
    all_gather x1, blocking collectives, local(): grads = lax.all_gather(grad_out, 'col', axis=0, tiled=True)  16.7 us
  transfers between devices with their start and end apart: 20, of which 11 were waited for; matrix products, arithmetic and copies ran while one was open for 1% of the time, Pallas kernels for 38%

profile of v1, /device:TPU:0, one launch (start us, length us, event | category | flops | bytes accessed | tf_op | source)
XLA Modules:
  0.0 230.1 jit_solution(10502105682363477553)
XLA Ops:
  0.6 1.4 copy.13
  2.0 18.5 %all_gather.6 = bf16[192,2048]{1,0:T(8,128)(2,1)} all-gather(bf16[24,2048]{1,0:T(8,128)(2,1)} %param.8), channel_id=1, replica_groups=mesh['row'=4,'col'=8] {'col'}, dimensions={0}, use_global_device_ids=true | all-gather | bytes 884736 | tf_op jit(solution)/shard_map/all_gather | solution.py:382
  20.6 14.4 %forward_part.2 = (bf16[96,3584]{1,0:T(8,128)(2,1)}, f32[96,3584]{1,0:T(8,128)}) custom-call(s32[1]{0:T(128)} %bitcast.me_ref, bf16[4,48,2048]{2,1,0:T(8,128)(2,1)} %bitcast.5, bf16[4,48,2048]{2,1,0:T(8,128)(2,1)} %bitcast.6, bf16[4,48,2048]{2,1,0:T(8,128)(2,1)} %bitcast.7, bf16[4,48,2048]{2,1,0:T(8,128)(2,1)} %bitcast.8, bf16[2048,3584]{1,0:T(8,128)(2,1)} %uw_ref.1, ...), custom_call_target="tpu_custom_call" | custom-call | flops 2818572288 | bytes 16744448 | tf_op jit(solution)/shard_map/forward_part/pallas_call | solution.py:87
  35.0 16.7 %all_gather.7 = bf16[192,2048]{1,0:T(8,128)(2,1)} all-gather(bf16[24,2048]{1,0:T(8,128)(2,1)S(1)} %copy-done.11), channel_id=1, replica_groups=mesh['row'=4,'col'=8] {'col'}, dimensions={0}, use_global_device_ids=true | all-gather | bytes 884736 | tf_op jit(solution)/shard_map/all_gather | solution.py:386
  51.6 8.5 %hidden_part.3 = (bf16[96,1792]{1,0:T(8,128)(2,1)}, f32[96,1792]{1,0:T(8,128)}) custom-call(s32[1]{0:T(128)} %bitcast.me_ref, bf16[4,48,2048]{2,1,0:T(8,128)(2,1)} %bitcast.17, bf16[4,48,2048]{2,1,0:T(8,128)(2,1)} %bitcast.18, bf16[4,48,2048]{2,1,0:T(8,128)(2,1)} %bitcast.19, bf16[4,48,2048]{2,1,0:T(8,128)(2,1)} %bitcast.20, bf16[3584,2048]{1,0:T(8,128)(2,1)} %w_ref.9, ...), custom_call_target="tpu_custom_call" | custom-call | flops 1409286144 | bytes 8372224 | tf_op jit(solution)/shard_map/hidden_part/pallas_call | solution.py:128
  60.2 1.6 collective-permute-start.11
  61.8 14.5 %forward_part.3 = (bf16[96,3584]{1,0:T(8,128)(2,1)}, f32[96,3584]{1,0:T(8,128)}) custom-call(s32[1]{0:T(128)} %bitcast.me_ref, bf16[4,48,2048]{2,1,0:T(8,128)(2,1)} %bitcast.9, bf16[4,48,2048]{2,1,0:T(8,128)(2,1)} %bitcast.10, bf16[4,48,2048]{2,1,0:T(8,128)(2,1)} %bitcast.11, bf16[4,48,2048]{2,1,0:T(8,128)(2,1)} %bitcast.12, bf16[2048,3584]{1,0:T(8,128)(2,1)} %gw_ref.1, ...), custom_call_target="tpu_custom_call" | custom-call | flops 2818572288 | bytes 16744448 | tf_op jit(solution)/shard_map/forward_part/pallas_call | solution.py:87
  76.3 1.5 collective-permute-start
  78.3 8.6 %hidden_part.2 = (bf16[96,1792]{1,0:T(8,128)(2,1)}, f32[96,1792]{1,0:T(8,128)}) custom-call(s32[1]{0:T(128)} %bitcast.me_ref, bf16[4,48,2048]{2,1,0:T(8,128)(2,1)} %bitcast.21, bf16[4,48,2048]{2,1,0:T(8,128)(2,1)} %bitcast.22, bf16[4,48,2048]{2,1,0:T(8,128)(2,1)} %bitcast.23, bf16[4,48,2048]{2,1,0:T(8,128)(2,1)} %bitcast.24, bf16[3584,2048]{1,0:T(8,128)(2,1)} %w_ref.9, ...), custom_call_target="tpu_custom_call" | custom-call | flops 1409286144 | bytes 8372224 | tf_op jit(solution)/shard_map/hidden_part/pallas_call | solution.py:128
  87.5 1.6 collective-permute-start.12
  89.1 13.0 %collective-permute-done.9 = bf16[96,1792]{1,0:T(8,128)(2,1)S(1)} collective-permute-done((bf16[96,1792]{1,0:T(8,128)(2,1)}, bf16[96,1792]{1,0:T(8,128)(2,1)S(1)}, u32[]{:S(2)}, u32[]{:S(2)}) %collective-permute-start.9) | collective-permute-done | bytes 344096 | tf_op jit(solution)/shard_map/ppermute | solution.py:348
  102.8 2.1 collective-permute-done.12
  106.6 1.6 collective-permute-start.3
  108.3 6.8 %collective-permute-done.1 = bf16[48,3584]{1,0:T(8,128)(2,1)S(1)} collective-permute-done((bf16[48,3584]{1,0:T(8,128)(2,1)S(1)}, bf16[48,3584]{1,0:T(8,128)(2,1)S(1)}, u32[]{:S(2)}, u32[]{:S(2)}) %collective-permute-start.1) | collective-permute-done | bytes 344096 | tf_op jit(solution)/shard_map/ppermute | solution.py:348
  115.1 0.8 collective-permute-done.3
  116.3 1.6 collective-permute-start.15
  119.1 8.3 %collective-permute-done.15 = bf16[48,3584]{1,0:T(8,128)(2,1)S(1)} collective-permute-done((bf16[48,3584]{1,0:T(8,128)(2,1)S(1)}, bf16[48,3584]{1,0:T(8,128)(2,1)S(1)}, u32[]{:S(2)}, u32[]{:S(2)}) %collective-permute-start.15) | collective-permute-done | bytes 344096 | tf_op jit(solution)/shard_map/ppermute | solution.py:348
  127.4 0.8 collective-permute-start.16
  128.2 1.6 collective-permute-start.14
  129.8 4.9 %collective-permute-done.4 = bf16[48,3584]{1,0:T(8,128)(2,1)S(1)} collective-permute-done((bf16[48,3584]{1,0:T(8,128)(2,1)S(1)}, bf16[48,3584]{1,0:T(8,128)(2,1)S(1)}, u32[]{:S(2)}, u32[]{:S(2)}) %collective-permute-start.4) | collective-permute-done | bytes 344096 | tf_op jit(solution)/shard_map/ppermute | solution.py:348
  134.8 0.8 collective-permute-start.5
  136.2 9.6 %collective-permute-done.16.b1 = bf16[96,3584]{1,0:T(8,128)(2,1)S(1)} collective-permute-done((bf16[96,3584]{1,0:T(8,128)(2,1)S(1)}, bf16[96,3584]{1,0:T(8,128)(2,1)S(1)}, u32[]{:S(2)}, u32[]{:S(2)}) %collective-permute-start.16) | collective-permute-done | bytes 688160 | tf_op jit(solution)/shard_map/ppermute | solution.py:348
  145.8 0.9 collective-permute-done.14.a1
  146.8 0.9 copy-done.7
  147.6 23.1 %input_back.1 = (f32[96,2048]{1,0:T(8,128)}, f32[96,2048]{1,0:T(8,128)}) custom-call(s32[2]{0:T(128)} %pad_add_fusion.place_ref, bf16[96,3584]{1,0:T(8,128)(2,1)} %copy-done.1, bf16[96,3584]{1,0:T(8,128)(2,1)} %copy-done.7, bf16[96,3584]{1,0:T(8,128)(2,1)} %copy-done, bf16[96,3584]{1,0:T(8,128)(2,1)} %copy-done.6, bf16[2048,3584]{1,0:T(8,128)(2,1)} %gw_ref.1, ...), custom_call_target="tpu_custom_call" | custom-call | flops 5637144576 | bytes 29360128 | tf_op jit(solution)/shard_map/input_back/pallas_call | solution.py:269
  170.8 25.3 %down_back.1 = (bf16[3584,2048]{1,0:T(8,128)(2,1)}, f32[96,2048]{1,0:T(8,128)}, f32[96,2048]{1,0:T(8,128)}) custom-call(s32[2]{0:T(128)} %pad_add_fusion.place_ref, bf16[4,48,2048]{2,1,0:T(8,128)(2,1)} %bitcast.25, bf16[4,48,2048]{2,1,0:T(8,128)(2,1)} %bitcast.26, bf16[4,48,2048]{2,1,0:T(8,128)(2,1)} %bitcast.27, bf16[4,48,2048]{2,1,0:T(8,128)(2,1)} %bitcast.28, ...), custom_call_target="tpu_custom_call" | custom-call | flops 5637144576 | bytes 29360128 | tf_op jit(solution)/shard_map/down_back/pallas_call | solution.py:209
  196.6 1.7 collective-permute-start.18
  198.4 15.7 %weight_back.1 = (bf16[2048,3584]{1,0:T(8,128)(2,1)}, bf16[2048,3584]{1,0:T(8,128)(2,1)}) custom-call(s32[1]{0:T(128)} %bitcast.me_ref, bf16[4,48,2048]{2,1,0:T(8,128)(2,1)} %bitcast.13, bf16[4,48,2048]{2,1,0:T(8,128)(2,1)} %bitcast.14, bf16[4,48,2048]{2,1,0:T(8,128)(2,1)} %bitcast.15, bf16[4,48,2048]{2,1,0:T(8,128)(2,1)} %bitcast.16, ...), custom_call_target="tpu_custom_call" | custom-call | flops 5637144576 | bytes 29360128 | tf_op jit(solution)/shard_map/weight_back/pallas_call | solution.py:325
  214.7 2.3 %collective-permute-start.19 = (bf16[24,2048]{1,0:T(8,128)(2,1)S(1)}, bf16[24,2048]{1,0:T(8,128)(2,1)S(1)}, u32[]{:S(2)}, u32[]{:S(2)}) collective-permute-start(bf16[24,2048]{1,0:T(8,128)(2,1)S(1)} %slice.126), channel_id=1, source_target_pairs={{0,4},{1,5},{2,6},{3,7},{4,0},{5,1},{6,2},{7,3},{8,12},{9,13},{10,... | collective-permute-start | bytes 294920 | tf_op jit(solution)/shard_map/ppermute | solution.py:348
  217.0 6.0 %collective-permute-done.7 = bf16[48,2048]{1,0:T(8,128)(2,1)S(1)} collective-permute-done((bf16[48,2048]{1,0:T(8,128)(2,1)S(1)}, bf16[48,2048]{1,0:T(8,128)(2,1)S(1)}, u32[]{:S(2)}, u32[]{:S(2)}) %collective-permute-start.7) | collective-permute-done | bytes 196640 | tf_op jit(solution)/shard_map/ppermute | solution.py:348
  223.1 1.5 collective-permute-start.8
  225.3 4.1 %collective-permute-done.8 = bf16[24,2048]{1,0:T(8,128)(2,1)S(1)} collective-permute-done((bf16[24,2048]{1,0:T(8,128)(2,1)S(1)}, bf16[24,2048]{1,0:T(8,128)(2,1)S(1)}, u32[]{:S(2)}, u32[]{:S(2)}) %collective-permute-start.8) | collective-permute-done | bytes 98336 | tf_op jit(solution)/shard_map/ppermute | solution.py:348
  (69 shorter events, 8.7 us)
Async XLA Ops:
  20.5 14.4 %copy-start.11 = (bf16[24,2048]{1,0:T(8,128)(2,1)S(1)}, bf16[24,2048]{1,0:T(8,128)(2,1)}, u32[]{:S(2)}) copy-start(bf16[24,2048]{1,0:T(8,128)(2,1)} %param.9) | copy-start | bytes 294916
  60.2 17.6 %copy-start.12 = (bf16[96,3584]{1,0:T(8,128)(2,1)S(1)}, bf16[96,3584]{1,0:T(8,128)(2,1)}, u32[]{:S(2)}) copy-start(bf16[96,3584]{1,0:T(8,128)(2,1)} %get-tuple-element.27) | copy-start | bytes 2064388
  60.2 27.3 %collective-permute-start.11 = (bf16[96,1792]{1,0:T(8,128)(2,1)}, bf16[96,1792]{1,0:T(8,128)(2,1)S(1)}, u32[]{:S(2)}, u32[]{:S(2)}) collective-permute-start(bf16[96,1792]{1,0:T(8,128)(2,1)} %get-tuple-element.33), channel_id=1, source_target_pairs={{0,16},{8,24},{16,0},{24,8},{1,17},{9,25},{17,1},{25,9},{2,18},{10... | collective-permute-start | bytes 1032200 | tf_op jit(solution)/shard_map/ppermute | solution.py:348
  76.3 11.2 %copy-start.9 = (f32[96,1792]{1,0:T(8,128)S(1)}, f32[96,1792]{1,0:T(8,128)}, u32[]{:S(2)}) copy-start(f32[96,1792]{1,0:T(8,128)} %get-tuple-element.32) | copy-start | bytes 2064388
  76.3 28.7 %collective-permute-start = (bf16[96,3584]{1,0:T(8,128)(2,1)}, bf16[96,3584]{1,0:T(8,128)(2,1)S(1)}, u32[]{:S(2)}, u32[]{:S(2)}) collective-permute-start(bf16[96,3584]{1,0:T(8,128)(2,1)} %get-tuple-element.25), channel_id=1, source_target_pairs={{0,8},{8,0},{16,24},{24,16},{1,9},{9,1},{17,25},{25,17},{2,10},{10... | collective-permute-start | bytes 2064392 | tf_op jit(solution)/shard_map/ppermute | solution.py:348
  77.7 28.1 %collective-permute-start.2 = (bf16[96,3584]{1,0:T(8,128)(2,1)S(1)}, bf16[96,3584]{1,0:T(8,128)(2,1)S(1)}, u32[]{:S(2)}, u32[]{:S(2)}) collective-permute-start(bf16[96,3584]{1,0:T(8,128)(2,1)S(1)} %copy-done.12), channel_id=1, source_target_pairs={{0,16},{8,24},{16,0},{24,8},{1,17},{9,25},{17,1},{25,9},{2,18},{10... | collective-permute-start | bytes 2064392 | tf_op jit(solution)/shard_map/ppermute | solution.py:348
  86.8 15.3 %copy-start.10 = (f32[96,1792]{1,0:T(8,128)S(1)}, f32[96,1792]{1,0:T(8,128)}, u32[]{:S(2)}) copy-start(f32[96,1792]{1,0:T(8,128)} %get-tuple-element.30) | copy-start | bytes 2064388
  86.9 15.3 %collective-permute-start.9 = (bf16[96,1792]{1,0:T(8,128)(2,1)}, bf16[96,1792]{1,0:T(8,128)(2,1)S(1)}, u32[]{:S(2)}, u32[]{:S(2)}) collective-permute-start(bf16[96,1792]{1,0:T(8,128)(2,1)} %get-tuple-element.31), channel_id=1, source_target_pairs={{0,8},{8,0},{16,24},{24,16},{1,9},{9,1},{17,25},{25,17},{2,10},{10... | collective-permute-start | bytes 1032200 | tf_op jit(solution)/shard_map/ppermute | solution.py:348
  87.5 17.4 %collective-permute-start.12 = (bf16[48,1792]{1,0:T(8,128)(2,1)S(1)}, bf16[48,1792]{1,0:T(8,128)(2,1)S(1)}, u32[]{:S(2)}, u32[]{:S(2)}) collective-permute-start(bf16[48,1792]{1,0:T(8,128)(2,1)S(1)} %slice.124), channel_id=1, source_target_pairs={{0,8},{8,0},{16,24},{24,16},{1,9},{9,1},{17,25},{25,17},{2,10},{10... | collective-permute-start | bytes 516104 | tf_op jit(solution)/shard_map/ppermute | solution.py:348
  102.1 2.9 %copy-start.3 = (f32[96,3584]{1,0:T(8,128)S(1)}, f32[96,3584]{1,0:T(8,128)}, u32[]{:S(2)}) copy-start(f32[96,3584]{1,0:T(8,128)} %get-tuple-element.24) | copy-start | bytes 4128772
  102.2 6.0 %collective-permute-start.10 = (bf16[48,1792]{1,0:T(8,128)(2,1)S(1)}, bf16[48,1792]{1,0:T(8,128)(2,1)S(1)}, u32[]{:S(2)}, u32[]{:S(2)}) collective-permute-start(bf16[48,1792]{1,0:T(8,128)(2,1)S(1)} %slice.125), channel_id=1, source_target_pairs={{0,16},{8,24},{16,0},{24,8},{1,17},{9,25},{17,1},{25,9},{2,18},{10... | collective-permute-start | bytes 516104 | tf_op jit(solution)/shard_map/ppermute | solution.py:348
  105.0 1.3 copy-start.2
  105.2 9.8 %collective-permute-start.1 = (bf16[48,3584]{1,0:T(8,128)(2,1)S(1)}, bf16[48,3584]{1,0:T(8,128)(2,1)S(1)}, u32[]{:S(2)}, u32[]{:S(2)}) collective-permute-start(bf16[48,3584]{1,0:T(8,128)(2,1)S(1)} %slice.121), channel_id=1, source_target_pairs={{0,16},{8,24},{16,0},{24,8},{1,17},{9,25},{17,1},{25,9},{2,18},{10... | collective-permute-start | bytes 1032200 | tf_op jit(solution)/shard_map/ppermute | solution.py:348
  106.6 9.3 %collective-permute-start.3 = (bf16[48,3584]{1,0:T(8,128)(2,1)S(1)}, bf16[48,3584]{1,0:T(8,128)(2,1)S(1)}, u32[]{:S(2)}, u32[]{:S(2)}) collective-permute-start(bf16[48,3584]{1,0:T(8,128)(2,1)S(1)} %slice.120), channel_id=1, source_target_pairs={{0,8},{8,0},{16,24},{24,16},{1,9},{9,1},{17,25},{25,17},{2,10},{10... | collective-permute-start | bytes 1032200 | tf_op jit(solution)/shard_map/ppermute | solution.py:348
  116.3 11.1 %collective-permute-start.15 = (bf16[48,3584]{1,0:T(8,128)(2,1)S(1)}, bf16[48,3584]{1,0:T(8,128)(2,1)S(1)}, u32[]{:S(2)}, u32[]{:S(2)}) collective-permute-start(bf16[48,3584]{1,0:T(8,128)(2,1)S(1)} %get-tuple-element.41), channel_id=1, source_target_pairs={{0,8},{8,0},{16,24},{24,16},{1,9},{9,1},{17,25},{25,17},{2,10},{10... | collective-permute-start | bytes 1032200 | tf_op jit(solution)/shard_map/ppermute | solution.py:348
  117.8 10.3 %collective-permute-start.13 = (bf16[48,3584]{1,0:T(8,128)(2,1)S(1)}, bf16[48,3584]{1,0:T(8,128)(2,1)S(1)}, u32[]{:S(2)}, u32[]{:S(2)}) collective-permute-start(bf16[48,3584]{1,0:T(8,128)(2,1)S(1)} %get-tuple-element.39), channel_id=1, source_target_pairs={{0,16},{8,24},{16,0},{24,8},{1,17},{9,25},{17,1},{25,9},{2,18},{10... | collective-permute-start | bytes 1032200 | tf_op jit(solution)/shard_map/ppermute | solution.py:348
  118.6 16.2 %collective-permute-start.4 = (bf16[48,3584]{1,0:T(8,128)(2,1)S(1)}, bf16[48,3584]{1,0:T(8,128)(2,1)S(1)}, u32[]{:S(2)}, u32[]{:S(2)}) collective-permute-start(bf16[48,3584]{1,0:T(8,128)(2,1)S(1)} %get-tuple-element.40), channel_id=1, source_target_pairs={{0,8},{8,0},{16,24},{24,16},{1,9},{9,1},{17,25},{25,17},{2,10},{10... | collective-permute-start | bytes 1032200 | tf_op jit(solution)/shard_map/ppermute | solution.py:348
  127.4 8.2 %copy-start = (bf16[96,3584]{1,0:T(8,128)(2,1)}, bf16[96,3584]{1,0:T(8,128)(2,1)S(1)}, u32[]{:S(2)}) copy-start(bf16[96,3584]{1,0:T(8,128)(2,1)S(1)} %pad_maximum_fusion.3.b0) | copy-start | bytes 2064388
  127.4 18.4 %collective-permute-start.16 = (bf16[96,3584]{1,0:T(8,128)(2,1)S(1)}, bf16[96,3584]{1,0:T(8,128)(2,1)S(1)}, u32[]{:S(2)}, u32[]{:S(2)}) collective-permute-start(bf16[96,3584]{1,0:T(8,128)(2,1)S(1)} %pad_maximum_fusion.3.b0), channel_id=1, source_target_pairs={{0,16},{8,24},{16,0},{24,8},{1,17},{9,25},{17,1},{25,9},{2,18},{10... | collective-permute-start | bytes 2064392 | tf_op jit(solution)/shard_map/ppermute | solution.py:348
  128.2 18.5 %copy-start.1 = (bf16[96,3584]{1,0:T(8,128)(2,1)}, bf16[96,3584]{1,0:T(8,128)(2,1)S(1)}, u32[]{:S(2)}) copy-start(bf16[96,3584]{1,0:T(8,128)(2,1)S(1)} %pad_maximum_fusion.2.a0) | copy-start | bytes 2064388
  128.2 18.5 %collective-permute-start.14 = (bf16[96,3584]{1,0:T(8,128)(2,1)S(1)}, bf16[96,3584]{1,0:T(8,128)(2,1)S(1)}, u32[]{:S(2)}, u32[]{:S(2)}) collective-permute-start(bf16[96,3584]{1,0:T(8,128)(2,1)S(1)} %pad_maximum_fusion.2.a0), channel_id=1, source_target_pairs={{0,8},{8,0},{16,24},{24,16},{1,9},{9,1},{17,25},{25,17},{2,10},{10... | collective-permute-start | bytes 2064392 | tf_op jit(solution)/shard_map/ppermute | solution.py:348
  134.8 35.9 %copy-start.8 = (bf16[96,3584]{1,0:T(8,128)(2,1)}, bf16[96,3584]{1,0:T(8,128)(2,1)S(1)}, u32[]{:S(2)}) copy-start(bf16[96,3584]{1,0:T(8,128)(2,1)S(1)} %pad_maximum_fusion.h0) | copy-start | bytes 2064388
  134.8 36.0 %collective-permute-start.5 = (bf16[96,3584]{1,0:T(8,128)(2,1)S(1)}, bf16[96,3584]{1,0:T(8,128)(2,1)}, u32[]{:S(2)}, u32[]{:S(2)}) collective-permute-start(bf16[96,3584]{1,0:T(8,128)(2,1)S(1)} %pad_maximum_fusion.h0), channel_id=1, source_target_pairs={{0,16},{8,24},{16,0},{24,8},{1,17},{9,25},{17,1},{25,9},{2,18},{10... | collective-permute-start | bytes 2064392 | tf_op jit(solution)/shard_map/ppermute | solution.py:348
  145.8 0.9 copy-start.6
  170.7 25.8 %copy-start.5 = (f32[96,2048]{1,0:T(8,128)S(1)}, f32[96,2048]{1,0:T(8,128)}, u32[]{:S(2)}) copy-start(f32[96,2048]{1,0:T(8,128)} %get-tuple-element.34) | copy-start | bytes 2359300
  170.7 25.8 %collective-permute-start.17 = (f32[96,2048]{1,0:T(8,128)}, f32[96,2048]{1,0:T(8,128)S(1)}, u32[]{:S(2)}, u32[]{:S(2)}) collective-permute-start(f32[96,2048]{1,0:T(8,128)} %get-tuple-element.35), channel_id=1, source_target_pairs={{0,1},{1,0},{2,3},{3,2},{4,5},{5,4},{6,7},{7,6},{8,9},{9,8},{10,11... | collective-permute-start | bytes 2359304 | tf_op jit(solution)/shard_map/ppermute | solution.py:348
  196.1 17.9 %collective-permute-start.6 = (f32[96,2048]{1,0:T(8,128)}, f32[96,2048]{1,0:T(8,128)S(1)}, u32[]{:S(2)}, u32[]{:S(2)}) collective-permute-start(f32[96,2048]{1,0:T(8,128)} %get-tuple-element.29), channel_id=1, source_target_pairs={{0,1},{1,0},{2,3},{3,2},{4,5},{5,4},{6,7},{7,6},{8,9},{9,8},{10,11... | collective-permute-start | bytes 2359304 | tf_op jit(solution)/shard_map/ppermute | solution.py:348
  196.6 17.4 %copy-start.4 = (f32[96,2048]{1,0:T(8,128)S(1)}, f32[96,2048]{1,0:T(8,128)}, u32[]{:S(2)}) copy-start(f32[96,2048]{1,0:T(8,128)} %get-tuple-element.28) | copy-start | bytes 2359300
  196.6 18.0 %collective-permute-start.18 = (bf16[48,2048]{1,0:T(8,128)(2,1)S(1)}, bf16[48,2048]{1,0:T(8,128)(2,1)S(1)}, u32[]{:S(2)}, u32[]{:S(2)}) collective-permute-start(bf16[48,2048]{1,0:T(8,128)(2,1)S(1)} %slice.122), channel_id=1, source_target_pairs={{0,2},{1,3},{2,0},{3,1},{4,6},{5,7},{6,4},{7,5},{8,10},{9,11},{10,... | collective-permute-start | bytes 589832 | tf_op jit(solution)/shard_map/ppermute | solution.py:348
  214.2 8.9 %collective-permute-start.7 = (bf16[48,2048]{1,0:T(8,128)(2,1)S(1)}, bf16[48,2048]{1,0:T(8,128)(2,1)S(1)}, u32[]{:S(2)}, u32[]{:S(2)}) collective-permute-start(bf16[48,2048]{1,0:T(8,128)(2,1)S(1)} %slice.123), channel_id=1, source_target_pairs={{0,2},{1,3},{2,0},{3,1},{4,6},{5,7},{6,4},{7,5},{8,10},{9,11},{10,... | collective-permute-start | bytes 589832 | tf_op jit(solution)/shard_map/ppermute | solution.py:348
  214.7 10.0 %collective-permute-start.19 = (bf16[24,2048]{1,0:T(8,128)(2,1)S(1)}, bf16[24,2048]{1,0:T(8,128)(2,1)S(1)}, u32[]{:S(2)}, u32[]{:S(2)}) collective-permute-start(bf16[24,2048]{1,0:T(8,128)(2,1)S(1)} %slice.126), channel_id=1, source_target_pairs={{0,4},{1,5},{2,6},{3,7},{4,0},{5,1},{6,2},{7,3},{8,12},{9,13},{10,... | collective-permute-start | bytes 294920 | tf_op jit(solution)/shard_map/ppermute | solution.py:348
  223.1 6.3 %collective-permute-start.8 = (bf16[24,2048]{1,0:T(8,128)(2,1)S(1)}, bf16[24,2048]{1,0:T(8,128)(2,1)S(1)}, u32[]{:S(2)}, u32[]{:S(2)}) collective-permute-start(bf16[24,2048]{1,0:T(8,128)(2,1)S(1)} %slice.127), channel_id=1, source_target_pairs={{0,4},{1,5},{2,6},{3,7},{4,0},{5,1},{6,2},{7,3},{8,12},{9,13},{10,... | collective-permute-start | bytes 294920 | tf_op jit(solution)/shard_map/ppermute | solution.py:348
  (1 other events, 0.9 us)

commit v2 on v0

v2 whole, which is shorter than its diff:
```python
import functools

import jax
import jax.numpy as jnp
from jax import lax
from jax.experimental import pallas as pl
from jax.experimental.pallas import tpu as pltpu
from jax.sharding import PartitionSpec as P

BF16 = jnp.bfloat16
F32 = jnp.float32
VMEM_LIMIT = 56 * 1024 * 1024
NT = (((1,), (1,)), ((), ()))
COST = pl.CostEstimate(flops=1000, bytes_accessed=1000, transcendentals=0)


def dot(a, b):
    return jnp.dot(a, b, preferred_element_type=F32)


def spread(mask, block):
    count = mask.shape[1]
    shape = (count, count * block)
    col = lax.broadcasted_iota(jnp.int32, shape, 1) // block
    row = lax.broadcasted_iota(jnp.int32, shape, 0)
    return dot(mask.astype(BF16), jnp.where(row == col, 1.0, 0.0).astype(BF16))


def masked(w, m, block):
    return jnp.concatenate(
        [
            w[i * block : (i + 1) * block, :]
            * jnp.broadcast_to(m[i : i + 1, :], (block, w.shape[1])).astype(BF16)
            for i in range(w.shape[0] // block)
        ],
        axis=0,
    )


def masked_product(left, right, m, out, block):
    height = left.shape[0]
    some = 256 if height % 256 == 0 else 128
    for top in range(0, height, some):
        got = dot(left[top : top + some, :], right)
        for i in range(some // block):
            line = top // block + i
            out[top + i * block : top + (i + 1) * block, :] = (
                got[i * block : (i + 1) * block, :] * m[line : line + 1, :]
            ).astype(BF16)


def fetches(pairs, columns, size):
    def copy(pair, i):
        source, held, sems = pair
        at = slice(i * size, (i + 1) * size)
        return pltpu.make_async_copy(
            source.at[:, at] if columns else source.at[at, :], held.at[i], sems.at[i]
        )

    def begin():
        for i in range(pairs[0][1].shape[0]):
            for pair in pairs:
                copy(pair, i).start()

    def arrived(i):
        for pair in pairs:
            copy(pair, i).wait()

    return begin, arrived


def at_step(pairs, columns, size, prepare):
    begin, arrived = fetches(pairs, columns, size)
    step = pl.program_id(0)

    @pl.when(step == 0)
    def _():
        begin()
        prepare()

    for i in range(pairs[0][1].shape[0]):
        pl.when(step == i)(functools.partial(arrived, i))
    return step


def spread_steps(mask, block, columns, out):
    full = spread(mask, block)
    steps, height, width = out.shape
    for i in range(steps):
        if columns:
            out[i] = full[:, i * width : (i + 1) * width]
        else:
            out[i] = full[i * height : (i + 1) * height, :]


def order_by_row(me, source, out):
    quarter = out.shape[0] // 4
    for j in range(4):
        at = pl.ds(pl.multiple_of((me ^ j) * quarter, 16), quarter)
        out[j * quarter : (j + 1) * quarter, :] = source[at, :]


def join_halves(me, pieces, out):
    quarter = out.shape[0] // 4
    left = 0
    for x_first, near, far in pieces:
        at = slice(left, left + near.shape[1])
        left += near.shape[1]
        for half, spots in (
            (near, (0, 2) if x_first else (0, 1)),
            (far, (1, 3) if x_first else (2, 3)),
        ):
            for slot, j in enumerate(spots):
                rows = pl.ds(pl.multiple_of((me ^ j) * quarter, 16), quarter)
                out[rows, at] = half[slot * quarter : (slot + 1) * quarter, :]


def put_halves(part, send, keep, at, x_first):
    quarter = part.shape[0] // 4
    kept, sent = ((0, 2), (1, 3)) if x_first else ((0, 1), (2, 3))
    for slot in range(2):
        rows = slice(slot * quarter, (slot + 1) * quarter)
        keep[rows, at] = part[kept[slot] * quarter : (kept[slot] + 1) * quarter, :]
        send[rows, at] = part[sent[slot] * quarter : (sent[slot] + 1) * quarter, :].astype(BF16)


def call(body, name, inputs, kinds, outs, out_kinds, scratch, steps=None, maps=None, aliases={}):
    spec = {
        "s": pl.BlockSpec(memory_space=pltpu.SMEM),
        "v": pl.BlockSpec(memory_space=pltpu.VMEM),
        "h": pl.BlockSpec(memory_space=pl.ANY),
    }
    out_specs = [spec[kind] for kind in out_kinds] if maps is None else maps
    grid = {} if steps is None else {"grid": (steps,)}
    return pl.pallas_call(
        body,
        in_specs=[spec[kind] for kind in kinds],
        out_specs=out_specs,
        out_shape=outs,
        scratch_shapes=scratch,
        input_output_aliases=aliases,
        compiler_params=pltpu.CompilerParams(vmem_limit_bytes=VMEM_LIMIT),
        cost_estimate=COST,
        name=name,
        **grid,
    )(*inputs)


def tiles_of(count, height, width):
    return [pltpu.VMEM((count, height, width), BF16), pltpu.SemaphoreType.DMA((count,))]


def shaped(*shape, kind=F32):
    return jax.ShapeDtypeStruct(shape, kind)


def parts_of(tile):
    some = min(tile, 256)
    return [slice(left, left + some) for left in range(0, tile, some)]


def forward_part(me, tokens, weight, mask, tile, x_first):
    total, depth = tokens.shape
    width = weight.shape[1]
    steps = width // tile
    block = depth // mask.shape[0]

    def body(me_ref, x_ref, w_hbm, m_ref, send, keep, x_s, m_s, held, sems):
        def prepare():
            order_by_row(me_ref[0], x_ref, x_s)
            spread_steps(m_ref[...], block, True, m_s)

        step = at_step([(w_hbm, held, sems)], True, tile, prepare)
        w, m = held.at[step], m_s[step]
        for at in parts_of(tile):
            part = dot(x_s[...], masked(w.at[:, at], m[:, at], block))
            put_halves(part, send, keep, at, x_first)

    return call(
        body,
        "forward_part",
        (me, tokens, weight, mask),
        "svhv",
        [shaped(total // 2, width, kind=BF16), shaped(total // 2, width)],
        None,
        [
            pltpu.VMEM((total, depth), BF16),
            pltpu.VMEM((steps, mask.shape[0], tile), F32),
            *tiles_of(steps, depth, tile),
        ],
        steps,
        [pl.BlockSpec((total // 2, tile), lambda i: (0, i))] * 2,
    )


def hidden_part(me, grads, weight, mask, tile):
    total, depth = grads.shape
    steps = weight.shape[0] // tile
    front = (steps + 1) // 2
    block = depth // mask.shape[1]
    per = tile // block

    def body(me_ref, x_ref, w_hbm, m_ref, a_send, a_keep, b_send, b_keep, x_s, m_s, held, sems):
        def prepare():
            order_by_row(me_ref[0], x_ref, x_s)
            spread_steps(m_ref[...], block, False, m_s)

        step = at_step([(w_hbm, held, sems)], False, tile, prepare)
        w, m = held.at[step], m_s[step]

        def put(send, keep, x_first):
            for at in parts_of(tile):
                rows = slice(at.start // block, at.stop // block)
                part = lax.dot_general(
                    x_s[...], masked(w.at[at, :], m[rows, :], block), NT, preferred_element_type=F32
                )
                put_halves(part, send, keep, at, x_first)

        pl.when(step < front)(functools.partial(put, a_send, a_keep, True))
        pl.when(step >= front)(functools.partial(put, b_send, b_keep, False))

    return call(
        body,
        "hidden_part",
        (me, grads, weight, mask),
        "svhv",
        [
            shaped(total // 2, count * tile, kind=kind)
            for count in (front, steps - front)
            for kind in (BF16, F32)
        ],
        None,
        [
            pltpu.VMEM((total, depth), BF16),
            pltpu.VMEM((steps, per, depth), F32),
            *tiles_of(steps, tile, depth),
        ],
        steps,
        [pl.BlockSpec((total // 2, tile), lambda i: (0, jnp.minimum(i, front - 1)))] * 2
        + [pl.BlockSpec((total // 2, tile), lambda i: (0, jnp.maximum(i - front, 0)))] * 2,
    )


def down_back(me, pieces, grads, weight, mask, tile):
    total, depth = grads.shape
    width = weight.shape[0]
    block = width // mask.shape[0]
    steps, slots = depth // tile, 4

    def body(me_ref, h0, h1, h2, h3, g_ref, w_hbm, m_ref, gw, send, keep, hid, hid_t, held, sems, stage, outs):
        begin, arrived = fetches([(w_hbm, held, sems)], True, tile)
        begin()
        join_halves(me_ref[0], ((True, h0, h1), (False, h2, h3)), hid)
        hid_t[...] = hid[...].T
        m = spread(m_ref[...], block)

        def leave(i):
            at = slice(i * tile, (i + 1) * tile)
            return pltpu.make_async_copy(stage.at[i % slots], gw.at[:, at], outs.at[i % slots])

        arrived(0)
        w = masked(held.at[0], m[:, :tile], block)
        for i in range(steps):
            at = slice(i * tile, (i + 1) * tile)
            now = w
            if i >= slots:
                leave(i - slots).wait()
            if i + 1 < steps:
                arrived(i + 1)
                w = masked(held.at[i + 1], m[:, (i + 1) * tile : (i + 2) * tile], block)
            out = dot(hid[...], now)
            keep[:, at] = out[: total // 2, :]
            send[:, at] = out[total // 2 :, :]
            masked_product(hid_t, g_ref[:, at], m[:, at], stage.at[i % slots], block)
            leave(i).start()
        for i in range(max(steps - slots, 0), steps):
            leave(i).wait()

    return call(
        body,
        "down_back",
        (me, *pieces, grads, weight, mask),
        "svvvvvhv",
        [shaped(width, depth, kind=BF16), shaped(total // 2, depth), shaped(total // 2, depth)],
        "hvv",
        [
            pltpu.VMEM((total, width), BF16),
            pltpu.VMEM((width, total), BF16),
            *tiles_of(steps, width, tile),
            pltpu.VMEM((slots, width, tile), BF16),
            pltpu.SemaphoreType.DMA((slots,)),
        ],
    )


def input_back(me, gate_pieces, up_pieces, gate_w, up_w, gate_m, up_m, tile):
    depth, width = gate_w.shape
    total = 2 * gate_pieces[0].shape[0]
    block = depth // gate_m.shape[0]
    steps, per = depth // tile, tile // block

    def body(me_ref, *refs):
        pieces, (gw, uw, gm, um, send, keep, a_s, b_s, gm_s, um_s, gh, gs, uh, us) = refs[:8], refs[8:]

        def prepare():
            join_halves(me_ref[0], ((True, *pieces[0:2]), (False, *pieces[2:4])), a_s)
            join_halves(me_ref[0], ((True, *pieces[4:6]), (False, *pieces[6:8])), b_s)
            spread_steps(gm[...], block, False, gm_s)
            spread_steps(um[...], block, False, um_s)

        step = at_step([(gw, gh, gs), (uw, uh, us)], False, tile, prepare)
        out = lax.dot_general(
            a_s[...], masked(gh.at[step], gm_s[step], block), NT, preferred_element_type=F32
        )
        out += lax.dot_general(
            b_s[...], masked(uh.at[step], um_s[step], block), NT, preferred_element_type=F32
        )
        keep[...] = out[: total // 2, :]
        send[...] = out[total // 2 :, :]

    return call(
        body,
        "input_back",
        (me, *gate_pieces, *up_pieces, gate_w, up_w, gate_m, up_m),
        "s" + "v" * 8 + "hhvv",
        [shaped(total // 2, depth), shaped(total // 2, depth)],
        None,
        [
            pltpu.VMEM((total, width), BF16),
            pltpu.VMEM((total, width), BF16),
            pltpu.VMEM((steps, per, width), F32),
            pltpu.VMEM((steps, per, width), F32),
            *tiles_of(steps, tile, width),
            *tiles_of(steps, tile, width),
        ],
        steps,
        [pl.BlockSpec((total // 2, tile), lambda i: (0, i))] * 2,
    )


def weight_back(me, pieces, tokens, mask, tile, left, right, earlier=None):
    total, depth = tokens.shape
    block = depth // mask.shape[0]
    width = mask.shape[1] * block
    steps, slots = (right - left) // tile, 6
    known = [] if earlier is None else [earlier]

    def body(me_ref, x_ref, m_ref, *refs):
        refs, (out, mark, x_t, a_s, stage, sems) = refs[:-6], refs[-6:]
        mark[...] = jnp.zeros_like(mark)

        def leave(i):
            at = slice(left + i * tile, left + (i + 1) * tile)
            return pltpu.make_async_copy(stage.at[i % slots], out.at[:, at], sems.at[i % slots])

        x_t[...] = x_ref[...].T
        ways = (True, False) if left == 0 else (False,)
        join_halves(me_ref[0], [(way, *refs[2 * n : 2 * n + 2]) for n, way in enumerate(ways[: len(pieces) // 2])], a_s)
        m = spread(m_ref[...], block)[:, left:right]
        for i in range(steps):
            at = slice(i * tile, (i + 1) * tile)
            if i >= slots:
                leave(i - slots).wait()
            masked_product(x_t, a_s[:, at], m[:, at], stage.at[i % slots], block)
            leave(i).start()
        for i in range(max(steps - slots, 0), steps):
            leave(i).wait()

    return call(
        body,
        "weight_back",
        (me, tokens, mask, *pieces, *known),
        "svv" + "v" * len(pieces) + "h" * len(known),
        [shaped(depth, width, kind=BF16), shaped(8, 128)],
        "hv",
        [
            pltpu.VMEM((depth, total), BF16),
            pltpu.VMEM((total, right - left), BF16),
            *tiles_of(slots, depth, tile),
        ],
        aliases={3 + len(pieces): 0} if known else {},
    )


def swap(value, axis, size, bit):
    return lax.ppermute(value, axis, [(i, i ^ bit) for i in range(size)])


def after(value, *earlier):
    return lax.optimization_barrier((value, *earlier))[0]


def local(rows, cols, tokens_in, grad_out, gate_w, up_w, down_w, gate_mask, up_mask, down_mask):
    me = lax.axis_index("row").astype(jnp.int32)[None]
    width = gate_w.shape[1]
    tile = 256 if width % 256 == 0 else 128
    wide = 512 if width % 512 == 0 else 128

    def over_row(value, bit):
        return swap(value, "row", rows, bit)

    def over_col(value, bit):
        return swap(value, "col", cols, bit)

    def halve(total):
        half = total.shape[0] // 2
        return total[:half], total[half:].astype(BF16)

    def gathering(own):
        bit = cols // 2
        while bit:
            got = over_col(own, bit)
            earlier = yield own
            got = got if earlier is None else after(got, earlier)
            own = jnp.concatenate([own, got], axis=0)
            bit //= 2
        yield own

    def leaving(send, keep):
        bit = 1
        while bit < cols:
            got = over_col(send, bit)
            earlier = yield send
            keep = keep + (got if earlier is None else after(got, earlier))
            bit *= 2
            if bit < cols:
                keep, send = halve(keep)
        yield keep.astype(BF16)

    def last(rounds):
        for value in rounds:
            pass
        return value

    rounds = gathering(tokens_in)
    near = tokens = next(rounds)
    for value in rounds:
        near, tokens = tokens, value
    rounds = gathering(after(grad_out, near))
    next(rounds)
    gate_send, gate_keep = forward_part(me, tokens, gate_w, gate_mask, wide, True)
    gate_got = over_row(gate_send, 1)
    rounds.send(gate_send)
    up_send, up_keep = forward_part(after(me, gate_send), tokens, up_w, up_mask, wide, False)
    up_got = over_row(up_send, 2)
    rounds.send(up_send)
    grads = last(rounds)
    a_send, a_keep, b_send, b_keep = hidden_part(
        after(me, up_send), grads, down_w, after(down_mask, gate_send), wide
    )
    a_got, b_got = over_row(a_send, 1), over_row(b_send, 2)
    gate_got, up_got, a_send = lax.optimization_barrier((gate_got, up_got, a_send))
    gate_keep, gate_send = halve(gate_keep + gate_got)
    up_keep, up_send = halve(up_keep + up_got)
    gate_got, up_got = over_row(gate_send, 2), over_row(up_send, 1)

    def near_halves(front, rest, *earlier):
        front, rest = lax.optimization_barrier((front, rest, *earlier))[:2]
        return front, over_row(front, 2), rest, over_row(rest, 1)

    def all_halves(front, front_got, rest, rest_got, *earlier):
        front_got, rest_got = lax.optimization_barrier((front_got, rest_got, *earlier))[:2]
        front = jnp.concatenate([front, front_got], axis=0)
        rest = jnp.concatenate([rest, rest_got], axis=0)
        return front, over_row(front, 1), rest, over_row(rest, 2)

    front = a_keep.shape[1]
    gate_pre, up_pre = gate_keep + gate_got, up_keep + up_got
    hidden = (jax.nn.sigmoid(gate_pre) * gate_pre * up_pre).astype(BF16)
    hidden_a, hidden_b, gate_pre, up_pre = lax.optimization_barrier(
        (hidden[:, :front], hidden[:, front:], gate_pre, up_pre)
    )
    hidden_all = all_halves(*near_halves(hidden_a, hidden_b))

    a_keep, a_send = halve(a_keep + after(a_got, gate_send, up_send))
    b_keep, b_send = halve(b_keep + after(b_got, gate_send, up_send))
    a_got, b_got = over_row(a_send, 2), over_row(b_send, 1)
    a_got, b_got = after(a_got, hidden_a), after(b_got, hidden_a)
    pre = []
    for at, grad_hidden in ((slice(None, front), a_keep + a_got), (slice(front, None), b_keep + b_got)):
        gate, up = gate_pre[:, at], up_pre[:, at]
        sig = jax.nn.sigmoid(gate)
        pre.append((grad_hidden * up * sig * (1.0 + gate * (1.0 - sig))).astype(BF16))
        pre.append((grad_hidden * (gate * sig)).astype(BF16))
    gate_near = near_halves(pre[0], pre[2], hidden_all[0], hidden_all[2])
    gate_all = all_halves(*gate_near, hidden_all[1], hidden_all[3])
    up_near = near_halves(pre[1], pre[3], gate_all[0], gate_all[2])
    grad_down, out_send, out_keep = down_back(
        after(me, gate_all[0], gate_all[2]), hidden_all, grads, down_w, down_mask, 256
    )
    up_all = all_halves(*up_near, out_send)
    gate_all = lax.optimization_barrier((*gate_all, out_send, up_all[0], up_all[2]))[:4]
    out_rounds = leaving(out_send, out_keep)
    next(out_rounds)
    grad_gate, mark = weight_back(
        after(me, out_send), gate_all, tokens, gate_mask, tile, 0, width
    )
    out_send = out_rounds.send(mark)
    up_all = lax.optimization_barrier((*up_all, mark))[:4]
    in_send, in_keep = input_back(
        after(me, mark, out_send), gate_all, up_all, gate_w, up_w, gate_mask, up_mask, 256
    )
    out_send = out_rounds.send(in_send)
    in_rounds = leaving(in_send, in_keep)
    next(in_rounds)
    in_send = in_rounds.send(None)
    grad_up, mark = weight_back(
        after(me, in_send, out_send), up_all[:2], tokens, up_mask, tile, 0, front
    )
    layer_out = out_rounds.send(mark)
    in_send = in_rounds.send(mark)
    grad_up, mark = weight_back(
        after(me, in_send), up_all[2:], tokens, up_mask, tile, front, width, grad_up
    )
    if cols > 8:
        layer_out = last(out_rounds)
    grad_in = in_rounds.send(mark)
    if cols > 8:
        grad_in = last(in_rounds)
    return (layer_out, grad_in, grad_gate, grad_up, grad_down)


def solution(mesh):
    by_row, by_col = P("row", "col"), P("col", "row")
    return jax.shard_map(
        functools.partial(local, mesh.shape["row"], mesh.shape["col"]),
        mesh=mesh,
        in_specs=(by_col, by_col, by_row, by_row, by_col, by_row, by_row, by_col),
        out_specs=(by_col, by_col, by_row, by_row, by_col),
        check_vma=False,
    )
```

time: 597 us -> 176 us (0.29); the launches traced: 587 us -> 176 us
  local copies, waits for them, and re-layouts: 396 us -> 6.77 us
  matrix products: 123 us -> 0 us
  Pallas kernels: 0 us -> 78.1 us
  waiting for transfers between devices: 0.05 us -> 51.9 us
  blocking collectives: 33.3 us -> 0 us
  starting transfers between devices: 0.12 us -> 33.3 us
  other arithmetic: 21.7 us -> 4.71 us
  between operations: 13.8 us -> 1.25 us
    mul x12 -> x0, local copies, waits for them, and re-layouts: 351 us -> none  [expand_blocks(): shaped * blocks.astype(weight.dtype)[:, None, :, None]]
    dot_general x9 -> x0, matrix products: 123 us -> none  [the longest x6 89.6 us: contract(): lax.dot_general(left_side, right_side, (((left_dim,), (right_dim,)), ((),...]
    pallas_call x0 -> x8, Pallas kernels: none -> 78.1 us  [call(): pl.pallas_call(body, in_specs=[spec[kind] for kind in kinds], out_specs=o...]
    ppermute x0 -> x32, waiting for transfers between devices: none -> 51.9 us  [swap(): return lax.ppermute(value, axis, [(i, i ^ bit) for i in range(size)])]
    unnamed x14 -> x54, local copies, waits for them, and re-layouts: 44 us -> 5.71 us
    all_gather x2 -> x0, blocking collectives: 33.3 us -> none  [the longest x1 17.4 us: local(): lax.all_gather(tokens_in, 'col', axis=0, tiled=True)]
    ppermute x0 -> x32, starting transfers between devices: none -> 33.3 us  [swap(): return lax.ppermute(value, axis, [(i, i ^ bit) for i in range(size)])]
    mul x1 -> x0, other arithmetic: 12 us -> none  [expand_blocks(): shaped * blocks.astype(weight.dtype)[:, None, :, None]]
  transfers between devices with their start and end apart: 3 -> 32, of which waited for: 0 -> 13; matrix products, arithmetic and copies ran while one was open for 53% -> 3% of each run, Pallas kernels for 0% -> 35%
where the time goes in v2:
time: 176 us
  Pallas kernels  78.1 us (44%)
  waiting for transfers between devices  51.9 us (29%)
  starting transfers between devices  33.3 us (19%)
  local copies, waits for them, and re-layouts  6.77 us (4%)
  other arithmetic  4.71 us (3%)
    pallas_call x8, Pallas kernels, call(): pl.pallas_call(body, in_specs=[spec[kind] for kind in kinds], out_specs=o...  78.1 us
    ppermute x32, waiting for transfers between devices, swap(): return lax.ppermute(value, axis, [(i, i ^ bit) for i in range(size)])  51.9 us
    ppermute x32, starting transfers between devices, swap(): return lax.ppermute(value, axis, [(i, i ^ bit) for i in range(size)])  33.3 us
    unnamed x54, local copies, waits for them, and re-layouts  5.71 us
  transfers between devices with their start and end apart: 32, of which 13 were waited for; matrix products, arithmetic and copies ran while one was open for 3% of the time, Pallas kernels for 35%

profile of v2, /device:TPU:0, one launch (start us, length us, event | category | flops | bytes accessed | tf_op | source)
XLA Modules:
  0.0 176.0 jit_solution(961191448887194005)
XLA Ops:
  0.7 4.1 %collective-permute-start = (bf16[24,2048]{1,0:T(8,128)(2,1)}, bf16[24,2048]{1,0:T(8,128)(2,1)S(1)}, u32[]{:S(2)}, u32[]{:S(2)}) collective-permute-start(bf16[24,2048]{1,0:T(8,128)(2,1)} %param.8), channel_id=1, source_target_pairs={{0,4},{1,5},{2,6},{3,7},{4,0},{5,1},{6,2},{7,3},{8,12},{9,13},{10,... | collective-permute-start | bytes 294920 | tf_op jit(solution)/shard_map/ppermute | solution.py:386
  5.7 4.2 %collective-permute-done = bf16[24,2048]{1,0:T(8,128)(2,1)S(1)} collective-permute-done((bf16[24,2048]{1,0:T(8,128)(2,1)}, bf16[24,2048]{1,0:T(8,128)(2,1)S(1)}, u32[]{:S(2)}, u32[]{:S(2)}) %collective-permute-start) | collective-permute-done | bytes 98336 | tf_op jit(solution)/shard_map/ppermute | solution.py:386
  11.7 5.2 %collective-permute-done.1 = bf16[48,2048]{1,0:T(8,128)(2,1)S(1)} collective-permute-done((bf16[48,2048]{1,0:T(8,128)(2,1)S(1)}, bf16[48,2048]{1,0:T(8,128)(2,1)S(1)}, u32[]{:S(2)}, u32[]{:S(2)}) %collective-permute-start.1) | collective-permute-done | bytes 196640 | tf_op jit(solution)/shard_map/ppermute | solution.py:386
  17.8 3.1 %collective-permute-start.3 = (bf16[24,2048]{1,0:T(8,128)(2,1)S(1)}, bf16[24,2048]{1,0:T(8,128)(2,1)S(1)}, u32[]{:S(2)}, u32[]{:S(2)}) collective-permute-start(bf16[24,2048]{1,0:T(8,128)(2,1)S(1)} %copy-done.12), channel_id=1, source_target_pairs={{0,4},{1,5},{2,6},{3,7},{4,0},{5,1},{6,2},{7,3},{8,12},{9,13},{10,... | collective-permute-start | bytes 294920 | tf_op jit(solution)/shard_map/ppermute | solution.py:386
  21.8 8.3 %forward_part.2 = (bf16[96,3584]{1,0:T(8,128)(2,1)}, f32[96,3584]{1,0:T(8,128)}) custom-call(s32[1]{0:T(128)} %bitcast.me_ref, bf16[192,2048]{1,0:T(8,128)(2,1)} %copy-done, bf16[2048,3584]{1,0:T(8,128)(2,1)} %refs_8_.1, s32[32,56]{1,0:T(8,128)} %refs_10_.1), custom_call_target="tpu_custom_call" | custom-call | flops 1000 | bytes 1000 | tf_op jit(solution)/shard_map/forward_part/pallas_call | solution.py:135
  30.1 1.8 %collective-permute-start.4 = (bf16[48,2048]{1,0:T(8,128)(2,1)S(1)}, bf16[48,2048]{1,0:T(8,128)(2,1)S(1)}, u32[]{:S(2)}, u32[]{:S(2)}) collective-permute-start(bf16[48,2048]{1,0:T(8,128)(2,1)S(1)} %pad_maximum_fusion.2), channel_id=1, source_target_pairs={{0,2},{1,3},{2,0},{3,1},{4,6},{5,7},{6,4},{7,5},{8,10},{9,11},{10,... | collective-permute-start | bytes 589832 | tf_op jit(solution)/shard_map/ppermute | solution.py:386
  32.0 1.5 collective-permute-start.7
  33.5 8.3 %forward_part.3 = (bf16[96,3584]{1,0:T(8,128)(2,1)}, f32[96,3584]{1,0:T(8,128)}) custom-call(s32[1]{0:T(128)} %bitcast.me_ref, bf16[192,2048]{1,0:T(8,128)(2,1)} %copy-done, bf16[2048,3584]{1,0:T(8,128)(2,1)} %refs_9_.1, s32[32,56]{1,0:T(8,128)} %m_ref.10), custom_call_target="tpu_custom_call" | custom-call | flops 1000 | bytes 1000 | tf_op jit(solution)/shard_map/forward_part/pallas_call | solution.py:135
  41.8 1.6 collective-permute-start.8
  44.2 1.7 collective-permute-done.5
  46.8 10.2 %hidden_part.1 = (bf16[96,2048]{1,0:T(8,128)(2,1)}, f32[96,2048]{1,0:T(8,128)}, bf16[96,1536]{1,0:T(8,128)(2,1)}, f32[96,1536]{1,0:T(8,128)}) custom-call(s32[1]{0:T(128)} %bitcast.me_ref, bf16[192,2048]{1,0:T(8,128)(2,1)} %copy-done.1, bf16[3584,2048]{1,0:T(8,128)(2,1)} %w_hbm.7, s32[56,32]{1,0:T(8,128)} %copy.14.m_ref), custom_call_target="tpu_custom_call" | custom-call | flops 1000 | bytes 1000 | tf_op jit(solution)/shard_map/hidden_part/pallas_call | solution.py:135
  59.3 1.6 collective-permute-start.10
  61.7 6.0 %collective-permute-done.12 = bf16[96,1536]{1,0:T(8,128)(2,1)S(1)} collective-permute-done((bf16[96,1536]{1,0:T(8,128)(2,1)}, bf16[96,1536]{1,0:T(8,128)(2,1)S(1)}, u32[]{:S(2)}, u32[]{:S(2)}) %collective-permute-start.12) | collective-permute-done | bytes 294944 | tf_op jit(solution)/shard_map/ppermute | solution.py:386
  67.8 1.6 collective-permute-start.13
  70.0 5.0 %collective-permute-done.10 = bf16[48,3584]{1,0:T(8,128)(2,1)S(1)} collective-permute-done((bf16[48,3584]{1,0:T(8,128)(2,1)S(1)}, bf16[48,3584]{1,0:T(8,128)(2,1)S(1)}, u32[]{:S(2)}, u32[]{:S(2)}) %collective-permute-start.10) | collective-permute-done | bytes 344096 | tf_op jit(solution)/shard_map/ppermute | solution.py:386
  75.1 1.5 collective-permute-done.11
  77.5 1.5 collective-permute-done.13
  79.9 4.2 %collective-permute-done.15 = bf16[48,1536]{1,0:T(8,128)(2,1)S(1)} collective-permute-done((bf16[48,1536]{1,0:T(8,128)(2,1)S(1)}, bf16[48,1536]{1,0:T(8,128)(2,1)S(1)}, u32[]{:S(2)}, u32[]{:S(2)}) %collective-permute-start.15) | collective-permute-done | bytes 147488 | tf_op jit(solution)/shard_map/ppermute | solution.py:386
  85.4 1.6 collective-permute-start.16
  86.9 1.5 collective-permute-start.17
  88.4 8.4 %collective-permute-done.17 = bf16[48,1536]{1,0:T(8,128)(2,1)S(1)} collective-permute-done((bf16[48,1536]{1,0:T(8,128)(2,1)S(1)}, bf16[48,1536]{1,0:T(8,128)(2,1)S(1)}, u32[]{:S(2)}, u32[]{:S(2)}) %collective-permute-start.17) | collective-permute-done | bytes 147488 | tf_op jit(solution)/shard_map/ppermute | solution.py:386
  98.3 1.6 collective-permute-start.23
  100.0 15.6 %down_back.1 = (bf16[3584,2048]{1,0:T(8,128)(2,1)}, f32[96,2048]{1,0:T(8,128)}, f32[96,2048]{1,0:T(8,128)}) custom-call(s32[1]{0:T(128)} %bitcast.me_ref, bf16[96,2048]{1,0:T(8,128)(2,1)} %copy-done.13, bf16[96,2048]{1,0:T(8,128)(2,1)} %copy-done.18, bf16[96,1536]{1,0:T(8,128)(2,1)} %copy-done.16, bf16[96,1536]{1,0:T(8,128)(2,1)} %copy-done.19, ...), custom_call_target="tpu_custom_call" | custom-call | flops 1000 | bytes 1000 | tf_op jit(solution)/shard_map/down_back/pallas_call | solution.py:135
  115.7 1.3 collective-permute-start.24
  117.0 4.9 %collective-permute-done.24 = bf16[48,1536]{1,0:T(8,128)(2,1)S(1)} collective-permute-done((bf16[48,1536]{1,0:T(8,128)(2,1)S(1)}, bf16[48,1536]{1,0:T(8,128)(2,1)S(1)}, u32[]{:S(2)}, u32[]{:S(2)}) %collective-permute-start.24) | collective-permute-done | bytes 147488 | tf_op jit(solution)/shard_map/ppermute | solution.py:386
  122.0 1.3 collective-permute-start.26
  125.3 8.6 %weight_back.3 = (bf16[2048,3584]{1,0:T(8,128)(2,1)}, f32[8,128]{1,0:T(8,128)}) custom-call(s32[1]{0:T(128)} %bitcast.me_ref, bf16[192,2048]{1,0:T(8,128)(2,1)} %copy-done, s32[32,56]{1,0:T(8,128)} %refs_10_.1, bf16[96,2048]{1,0:T(8,128)(2,1)} %copy-done.2, bf16[96,2048]{1,0:T(8,128)(2,1)} %copy-done.6, bf16[96,1536]{1,0:T(8,128)(2,1)} %copy-done.4, ...), custom_call_target="tpu_custom_call" | custom-call | flops 1000 | bytes 1000 | tf_op jit(solution)/shard_map/weight_back/pallas_call | solution.py:135
  134.8 16.1 %input_back.1 = (f32[96,2048]{1,0:T(8,128)}, f32[96,2048]{1,0:T(8,128)}) custom-call(s32[1]{0:T(128)} %bitcast.me_ref, bf16[96,2048]{1,0:T(8,128)(2,1)} %copy-done.2, bf16[96,2048]{1,0:T(8,128)(2,1)} %copy-done.6, bf16[96,1536]{1,0:T(8,128)(2,1)} %copy-done.4, bf16[96,1536]{1,0:T(8,128)(2,1)} %copy-done.10, bf16[96,2048]{1,0:T(8,128)(2,1)} %copy-done.3, ...), custom_call_target="tpu_custom_call" | custom-call | flops 1000 | bytes 1000 | tf_op jit(solution)/shard_map/input_back/pallas_call | solution.py:135
  151.4 7.0 %collective-permute-done.25 = bf16[48,2048]{1,0:T(8,128)(2,1)S(1)} collective-permute-done((bf16[48,2048]{1,0:T(8,128)(2,1)S(1)}, bf16[48,2048]{1,0:T(8,128)(2,1)S(1)}, u32[]{:S(2)}, u32[]{:S(2)}) %collective-permute-start.25) | collective-permute-done | bytes 196640 | tf_op jit(solution)/shard_map/ppermute | solution.py:386
  161.1 5.9 %weight_back.4 = (bf16[2048,3584]{1,0:T(8,128)(2,1)}, f32[8,128]{1,0:T(8,128)}) custom-call(s32[1]{0:T(128)} %bitcast.me_ref, bf16[192,2048]{1,0:T(8,128)(2,1)} %copy-done, s32[32,56]{1,0:T(8,128)} %m_ref.10, bf16[96,2048]{1,0:T(8,128)(2,1)} %copy-done.3, bf16[96,2048]{1,0:T(8,128)(2,1)} %copy-done.7), custom_call_target="tpu_custom_call" | custom-call | flops 1000 | bytes 1000 | tf_op jit(solution)/shard_map/weight_back/pallas_call | solution.py:135
  168.3 1.3 collective-permute-start.31
  170.2 5.2 %weight_back.5 = (bf16[2048,3584]{1,0:T(8,128)(2,1)}, f32[8,128]{1,0:T(8,128)}) custom-call(s32[1]{0:T(128)} %bitcast.me_ref, bf16[192,2048]{1,0:T(8,128)(2,1)} %copy-done, s32[32,56]{1,0:T(8,128)} %m_ref.10, bf16[96,1536]{1,0:T(8,128)(2,1)} %copy-done.5, bf16[96,1536]{1,0:T(8,128)(2,1)} %copy-done.11, ...), custom_call_target="tpu_custom_call", output_to_operand_aliasing={{0}: (5, {})} | custom-call | flops 1000 | bytes 1000 | tf_op jit(solution)/shard_map/weight_back/pallas_call | solution.py:135
  (130 shorter events, 23.2 us)
Async XLA Ops:
  0.7 9.2 %collective-permute-start = (bf16[24,2048]{1,0:T(8,128)(2,1)}, bf16[24,2048]{1,0:T(8,128)(2,1)S(1)}, u32[]{:S(2)}, u32[]{:S(2)}) collective-permute-start(bf16[24,2048]{1,0:T(8,128)(2,1)} %param.8), channel_id=1, source_target_pairs={{0,4},{1,5},{2,6},{3,7},{4,0},{5,1},{6,2},{7,3},{8,12},{9,13},{10,... | collective-permute-start | bytes 294920 | tf_op jit(solution)/shard_map/ppermute | solution.py:386
  10.8 6.2 %collective-permute-start.1 = (bf16[48,2048]{1,0:T(8,128)(2,1)S(1)}, bf16[48,2048]{1,0:T(8,128)(2,1)S(1)}, u32[]{:S(2)}, u32[]{:S(2)}) collective-permute-start(bf16[48,2048]{1,0:T(8,128)(2,1)S(1)} %pad_maximum_fusion.1), channel_id=1, source_target_pairs={{0,2},{1,3},{2,0},{3,1},{4,6},{5,7},{6,4},{7,5},{8,10},{9,11},{10,... | collective-permute-start | bytes 589832 | tf_op jit(solution)/shard_map/ppermute | solution.py:386
  17.0 3.9 %collective-permute-start.2 = (bf16[96,2048]{1,0:T(8,128)(2,1)S(1)}, bf16[96,2048]{1,0:T(8,128)(2,1)S(1)}, u32[]{:S(2)}, u32[]{:S(2)}) collective-permute-start(bf16[96,2048]{1,0:T(8,128)(2,1)S(1)} %get-tuple-element.138), channel_id=1, source_target_pairs={{0,1},{1,0},{2,3},{3,2},{4,5},{5,4},{6,7},{7,6},{8,9},{9,8},{10,11... | collective-permute-start | bytes 1179656 | tf_op jit(solution)/shard_map/ppermute | solution.py:386
  17.8 12.4 %collective-permute-start.3 = (bf16[24,2048]{1,0:T(8,128)(2,1)S(1)}, bf16[24,2048]{1,0:T(8,128)(2,1)S(1)}, u32[]{:S(2)}, u32[]{:S(2)}) collective-permute-start(bf16[24,2048]{1,0:T(8,128)(2,1)S(1)} %copy-done.12), channel_id=1, source_target_pairs={{0,4},{1,5},{2,6},{3,7},{4,0},{5,1},{6,2},{7,3},{8,12},{9,13},{10,... | collective-permute-start | bytes 294920 | tf_op jit(solution)/shard_map/ppermute | solution.py:386
  30.1 13.9 %collective-permute-start.4 = (bf16[48,2048]{1,0:T(8,128)(2,1)S(1)}, bf16[48,2048]{1,0:T(8,128)(2,1)S(1)}, u32[]{:S(2)}, u32[]{:S(2)}) collective-permute-start(bf16[48,2048]{1,0:T(8,128)(2,1)S(1)} %pad_maximum_fusion.2), channel_id=1, source_target_pairs={{0,2},{1,3},{2,0},{3,1},{4,6},{5,7},{6,4},{7,5},{8,10},{9,11},{10,... | collective-permute-start | bytes 589832 | tf_op jit(solution)/shard_map/ppermute | solution.py:386
  32.0 26.2 %collective-permute-start.7 = (bf16[96,3584]{1,0:T(8,128)(2,1)}, bf16[96,3584]{1,0:T(8,128)(2,1)S(1)}, u32[]{:S(2)}, u32[]{:S(2)}) collective-permute-start(bf16[96,3584]{1,0:T(8,128)(2,1)} %get-tuple-element.68), channel_id=1, source_target_pairs={{0,8},{8,0},{16,24},{24,16},{1,9},{9,1},{17,25},{25,17},{2,10},{10... | collective-permute-start | bytes 2064392 | tf_op jit(solution)/shard_map/ppermute | solution.py:386
  41.8 17.3 %collective-permute-start.8 = (bf16[96,3584]{1,0:T(8,128)(2,1)}, bf16[96,3584]{1,0:T(8,128)(2,1)S(1)}, u32[]{:S(2)}, u32[]{:S(2)}) collective-permute-start(bf16[96,3584]{1,0:T(8,128)(2,1)} %get-tuple-element.70), channel_id=1, source_target_pairs={{0,16},{8,24},{16,0},{24,8},{1,17},{9,25},{17,1},{25,9},{2,18},{10... | collective-permute-start | bytes 2064392 | tf_op jit(solution)/shard_map/ppermute | solution.py:386
  44.1 1.8 %collective-permute-start.5 = (bf16[96,2048]{1,0:T(8,128)(2,1)S(1)}, bf16[96,2048]{1,0:T(8,128)(2,1)S(1)}, u32[]{:S(2)}, u32[]{:S(2)}) collective-permute-start(bf16[96,2048]{1,0:T(8,128)(2,1)S(1)} %pad_maximum_fusion), channel_id=1, source_target_pairs={{0,1},{1,0},{2,3},{3,2},{4,5},{5,4},{6,7},{7,6},{8,9},{9,8},{10,11... | collective-permute-start | bytes 1179656 | tf_op jit(solution)/shard_map/ppermute | solution.py:386
  57.0 12.3 %collective-permute-start.6 = (bf16[96,2048]{1,0:T(8,128)(2,1)}, bf16[96,2048]{1,0:T(8,128)(2,1)S(1)}, u32[]{:S(2)}, u32[]{:S(2)}) collective-permute-start(bf16[96,2048]{1,0:T(8,128)(2,1)} %get-tuple-element.77), channel_id=1, source_target_pairs={{0,8},{8,0},{16,24},{24,16},{1,9},{9,1},{17,25},{25,17},{2,10},{10... | collective-permute-start | bytes 1179656 | tf_op jit(solution)/shard_map/ppermute | solution.py:386
  57.6 10.1 %collective-permute-start.12 = (bf16[96,1536]{1,0:T(8,128)(2,1)}, bf16[96,1536]{1,0:T(8,128)(2,1)S(1)}, u32[]{:S(2)}, u32[]{:S(2)}) collective-permute-start(bf16[96,1536]{1,0:T(8,128)(2,1)} %get-tuple-element.88), channel_id=1, source_target_pairs={{0,16},{8,24},{16,0},{24,8},{1,17},{9,25},{17,1},{25,9},{2,18},{10... | collective-permute-start | bytes 884744 | tf_op jit(solution)/shard_map/ppermute | solution.py:386
  59.3 15.8 %collective-permute-start.10 = (bf16[48,3584]{1,0:T(8,128)(2,1)S(1)}, bf16[48,3584]{1,0:T(8,128)(2,1)S(1)}, u32[]{:S(2)}, u32[]{:S(2)}) collective-permute-start(bf16[48,3584]{1,0:T(8,128)(2,1)S(1)} %slice.149), channel_id=1, source_target_pairs={{0,16},{8,24},{16,0},{24,8},{1,17},{9,25},{17,1},{25,9},{2,18},{10... | collective-permute-start | bytes 1032200 | tf_op jit(solution)/shard_map/ppermute | solution.py:386
  61.1 15.5 %collective-permute-start.11 = (bf16[48,3584]{1,0:T(8,128)(2,1)S(1)}, bf16[48,3584]{1,0:T(8,128)(2,1)S(1)}, u32[]{:S(2)}, u32[]{:S(2)}) collective-permute-start(bf16[48,3584]{1,0:T(8,128)(2,1)S(1)} %slice.148), channel_id=1, source_target_pairs={{0,8},{8,0},{16,24},{24,16},{1,9},{9,1},{17,25},{25,17},{2,10},{10... | collective-permute-start | bytes 1032200 | tf_op jit(solution)/shard_map/ppermute | solution.py:386
  67.8 11.2 %collective-permute-start.13 = (bf16[48,1536]{1,0:T(8,128)(2,1)S(1)}, bf16[48,1536]{1,0:T(8,128)(2,1)S(1)}, u32[]{:S(2)}, u32[]{:S(2)}) collective-permute-start(bf16[48,1536]{1,0:T(8,128)(2,1)S(1)} %slice.153), channel_id=1, source_target_pairs={{0,8},{8,0},{16,24},{24,16},{1,9},{9,1},{17,25},{25,17},{2,10},{10... | collective-permute-start | bytes 442376 | tf_op jit(solution)/shard_map/ppermute | solution.py:386
  69.5 10.2 %collective-permute-start.9 = (bf16[48,2048]{1,0:T(8,128)(2,1)S(1)}, bf16[48,2048]{1,0:T(8,128)(2,1)S(1)}, u32[]{:S(2)}, u32[]{:S(2)}) collective-permute-start(bf16[48,2048]{1,0:T(8,128)(2,1)S(1)} %slice.152), channel_id=1, source_target_pairs={{0,16},{8,24},{16,0},{24,8},{1,17},{9,25},{17,1},{25,9},{2,18},{10... | collective-permute-start | bytes 589832 | tf_op jit(solution)/shard_map/ppermute | solution.py:386
  76.9 7.2 %collective-permute-start.14 = (bf16[48,2048]{1,0:T(8,128)(2,1)S(1)}, bf16[48,2048]{1,0:T(8,128)(2,1)S(1)}, u32[]{:S(2)}, u32[]{:S(2)}) collective-permute-start(bf16[48,2048]{1,0:T(8,128)(2,1)S(1)} %slice.102), channel_id=1, source_target_pairs={{0,16},{8,24},{16,0},{24,8},{1,17},{9,25},{17,1},{25,9},{2,18},{10... | collective-permute-start | bytes 589832 | tf_op jit(solution)/shard_map/ppermute | solution.py:386
  79.0 5.1 %collective-permute-start.15 = (bf16[48,1536]{1,0:T(8,128)(2,1)S(1)}, bf16[48,1536]{1,0:T(8,128)(2,1)S(1)}, u32[]{:S(2)}, u32[]{:S(2)}) collective-permute-start(bf16[48,1536]{1,0:T(8,128)(2,1)S(1)} %slice.103), channel_id=1, source_target_pairs={{0,8},{8,0},{16,24},{24,16},{1,9},{9,1},{17,25},{25,17},{2,10},{10... | collective-permute-start | bytes 442376 | tf_op jit(solution)/shard_map/ppermute | solution.py:386
  84.1 12.7 %collective-permute-start.18 = (bf16[96,2048]{1,0:T(8,128)(2,1)S(1)}, bf16[96,2048]{1,0:T(8,128)(2,1)S(1)}, u32[]{:S(2)}, u32[]{:S(2)}) collective-permute-start(bf16[96,2048]{1,0:T(8,128)(2,1)S(1)} %constant_dynamic-update-slice_fusion.11.h0), channel_id=1, source_target_pairs={{0,8},{8,0},{16,24},{24,16},{1,9},{9,1},{17,25},{25,17},{2,10},{10... | collective-permute-start | bytes 1179656 | tf_op jit(solution)/shard_map/ppermute | solution.py:386
  84.8 12.1 %collective-permute-start.19 = (bf16[96,1536]{1,0:T(8,128)(2,1)S(1)}, bf16[96,1536]{1,0:T(8,128)(2,1)S(1)}, u32[]{:S(2)}, u32[]{:S(2)}) collective-permute-start(bf16[96,1536]{1,0:T(8,128)(2,1)S(1)} %constant_dynamic-update-slice_fusion.13.h2), channel_id=1, source_target_pairs={{0,16},{8,24},{16,0},{24,8},{1,17},{9,25},{17,1},{25,9},{2,18},{10... | collective-permute-start | bytes 884744 | tf_op jit(solution)/shard_map/ppermute | solution.py:386
  85.4 11.5 %collective-permute-start.16 = (bf16[48,2048]{1,0:T(8,128)(2,1)S(1)}, bf16[48,2048]{1,0:T(8,128)(2,1)S(1)}, u32[]{:S(2)}, u32[]{:S(2)}) collective-permute-start(bf16[48,2048]{1,0:T(8,128)(2,1)S(1)} %get-tuple-element.96), channel_id=1, source_target_pairs={{0,16},{8,24},{16,0},{24,8},{1,17},{9,25},{17,1},{25,9},{2,18},{10... | collective-permute-start | bytes 589832 | tf_op jit(solution)/shard_map/ppermute | solution.py:386
  86.9 9.9 %collective-permute-start.17 = (bf16[48,1536]{1,0:T(8,128)(2,1)S(1)}, bf16[48,1536]{1,0:T(8,128)(2,1)S(1)}, u32[]{:S(2)}, u32[]{:S(2)}) collective-permute-start(bf16[48,1536]{1,0:T(8,128)(2,1)S(1)} %get-tuple-element.97), channel_id=1, source_target_pairs={{0,8},{8,0},{16,24},{24,16},{1,9},{9,1},{17,25},{25,17},{2,10},{10... | collective-permute-start | bytes 442376 | tf_op jit(solution)/shard_map/ppermute | solution.py:386
  96.9 27.0 %collective-permute-start.21 = (bf16[96,2048]{1,0:T(8,128)(2,1)S(1)}, bf16[96,2048]{1,0:T(8,128)(2,1)S(1)}, u32[]{:S(2)}, u32[]{:S(2)}) collective-permute-start(bf16[96,2048]{1,0:T(8,128)(2,1)S(1)} %constant_dynamic-update-slice_fusion.15.refs_0_), channel_id=1, source_target_pairs={{0,8},{8,0},{16,24},{24,16},{1,9},{9,1},{17,25},{25,17},{2,10},{10... | collective-permute-start | bytes 1179656 | tf_op jit(solution)/shard_map/ppermute | solution.py:386
  97.8 26.1 %collective-permute-start.22 = (bf16[96,1536]{1,0:T(8,128)(2,1)S(1)}, bf16[96,1536]{1,0:T(8,128)(2,1)S(1)}, u32[]{:S(2)}, u32[]{:S(2)}) collective-permute-start(bf16[96,1536]{1,0:T(8,128)(2,1)S(1)} %constant_dynamic-update-slice_fusion.17.refs_2_), channel_id=1, source_target_pairs={{0,16},{8,24},{16,0},{24,8},{1,17},{9,25},{17,1},{25,9},{2,18},{10... | collective-permute-start | bytes 884744 | tf_op jit(solution)/shard_map/ppermute | solution.py:386
  98.3 23.6 %collective-permute-start.23 = (bf16[48,2048]{1,0:T(8,128)(2,1)S(1)}, bf16[48,2048]{1,0:T(8,128)(2,1)S(1)}, u32[]{:S(2)}, u32[]{:S(2)}) collective-permute-start(bf16[48,2048]{1,0:T(8,128)(2,1)S(1)} %get-tuple-element.104), channel_id=1, source_target_pairs={{0,16},{8,24},{16,0},{24,8},{1,17},{9,25},{17,1},{25,9},{2,18},{10... | collective-permute-start | bytes 589832 | tf_op jit(solution)/shard_map/ppermute | solution.py:386
  115.6 18.4 %collective-permute-start.20 = (f32[96,2048]{1,0:T(8,128)}, f32[96,2048]{1,0:T(8,128)S(1)}, u32[]{:S(2)}, u32[]{:S(2)}) collective-permute-start(f32[96,2048]{1,0:T(8,128)} %get-tuple-element.102), channel_id=1, source_target_pairs={{0,1},{1,0},{2,3},{3,2},{4,5},{5,4},{6,7},{7,6},{8,9},{9,8},{10,11... | collective-permute-start | bytes 2359304 | tf_op jit(solution)/shard_map/ppermute | solution.py:386
  115.7 6.3 %collective-permute-start.24 = (bf16[48,1536]{1,0:T(8,128)(2,1)S(1)}, bf16[48,1536]{1,0:T(8,128)(2,1)S(1)}, u32[]{:S(2)}, u32[]{:S(2)}) collective-permute-start(bf16[48,1536]{1,0:T(8,128)(2,1)S(1)} %get-tuple-element.105), channel_id=1, source_target_pairs={{0,8},{8,0},{16,24},{24,16},{1,9},{9,1},{17,25},{25,17},{2,10},{10... | collective-permute-start | bytes 442376 | tf_op jit(solution)/shard_map/ppermute | solution.py:386
  122.0 12.0 %collective-permute-start.26 = (bf16[96,2048]{1,0:T(8,128)(2,1)S(1)}, bf16[96,2048]{1,0:T(8,128)(2,1)S(1)}, u32[]{:S(2)}, u32[]{:S(2)}) collective-permute-start(bf16[96,2048]{1,0:T(8,128)(2,1)S(1)} %constant_dynamic-update-slice_fusion.19.refs_4_.refs_0_), channel_id=1, source_target_pairs={{0,8},{8,0},{16,24},{24,16},{1,9},{9,1},{17,25},{25,17},{2,10},{10... | collective-permute-start | bytes 1179656 | tf_op jit(solution)/shard_map/ppermute | solution.py:386
  123.3 10.6 %collective-permute-start.27 = (bf16[96,1536]{1,0:T(8,128)(2,1)S(1)}, bf16[96,1536]{1,0:T(8,128)(2,1)S(1)}, u32[]{:S(2)}, u32[]{:S(2)}) collective-permute-start(bf16[96,1536]{1,0:T(8,128)(2,1)S(1)} %constant_dynamic-update-slice_fusion.21.refs_6_.refs_0_), channel_id=1, source_target_pairs={{0,16},{8,24},{16,0},{24,8},{1,17},{9,25},{17,1},{25,9},{2,18},{10... | collective-permute-start | bytes 884744 | tf_op jit(solution)/shard_map/ppermute | solution.py:386
  150.9 7.4 %collective-permute-start.29 = (f32[96,2048]{1,0:T(8,128)}, f32[96,2048]{1,0:T(8,128)S(1)}, u32[]{:S(2)}, u32[]{:S(2)}) collective-permute-start(f32[96,2048]{1,0:T(8,128)} %get-tuple-element.119), channel_id=1, source_target_pairs={{0,1},{1,0},{2,3},{3,2},{4,5},{5,4},{6,7},{7,6},{8,9},{9,8},{10,11... | collective-permute-start | bytes 2359304 | tf_op jit(solution)/shard_map/ppermute | solution.py:386
  151.0 7.3 %collective-permute-start.25 = (bf16[48,2048]{1,0:T(8,128)(2,1)S(1)}, bf16[48,2048]{1,0:T(8,128)(2,1)S(1)}, u32[]{:S(2)}, u32[]{:S(2)}) collective-permute-start(bf16[48,2048]{1,0:T(8,128)(2,1)S(1)} %slice.151), channel_id=1, source_target_pairs={{0,2},{1,3},{2,0},{3,1},{4,6},{5,7},{6,4},{7,5},{8,10},{9,11},{10,... | collective-permute-start | bytes 589832 | tf_op jit(solution)/shard_map/ppermute | solution.py:386
  159.6 8.6 %collective-permute-start.30 = (bf16[48,2048]{1,0:T(8,128)(2,1)S(1)}, bf16[48,2048]{1,0:T(8,128)(2,1)S(1)}, u32[]{:S(2)}, u32[]{:S(2)}) collective-permute-start(bf16[48,2048]{1,0:T(8,128)(2,1)S(1)} %slice.150), channel_id=1, source_target_pairs={{0,2},{1,3},{2,0},{3,1},{4,6},{5,7},{6,4},{7,5},{8,10},{9,11},{10,... | collective-permute-start | bytes 589832 | tf_op jit(solution)/shard_map/ppermute | solution.py:386
  160.0 7.0 %collective-permute-start.28 = (bf16[24,2048]{1,0:T(8,128)(2,1)S(1)}, bf16[24,2048]{1,0:T(8,128)(2,1)S(1)}, u32[]{:S(2)}, u32[]{:S(2)}) collective-permute-start(bf16[24,2048]{1,0:T(8,128)(2,1)S(1)} %slice.155), channel_id=1, source_target_pairs={{0,4},{1,5},{2,6},{3,7},{4,0},{5,1},{6,2},{7,3},{8,12},{9,13},{10,... | collective-permute-start | bytes 294920 | tf_op jit(solution)/shard_map/ppermute | solution.py:386
  168.3 7.1 %collective-permute-start.31 = (bf16[24,2048]{1,0:T(8,128)(2,1)S(1)}, bf16[24,2048]{1,0:T(8,128)(2,1)S(1)}, u32[]{:S(2)}, u32[]{:S(2)}) collective-permute-start(bf16[24,2048]{1,0:T(8,128)(2,1)S(1)} %slice.154), channel_id=1, source_target_pairs={{0,4},{1,5},{2,6},{3,7},{4,0},{5,1},{6,2},{7,3},{8,12},{9,13},{10,... | collective-permute-start | bytes 294920 | tf_op jit(solution)/shard_map/ppermute | solution.py:386
  (21 other events, 181.2 us)

commit v3 on v2

--- a/solution.py
+++ b/solution.py
@@ -11,7 +11,6 @@
 F32 = jnp.float32
 VMEM_LIMIT = 56 * 1024 * 1024
 NT = (((1,), (1,)), ((), ()))
-COST = pl.CostEstimate(flops=1000, bytes_accessed=1000, transcendentals=0)
 
 
 def dot(a, b):
@@ -124,7 +123,7 @@
         send[rows, at] = part[sent[slot] * quarter : (sent[slot] + 1) * quarter, :].astype(BF16)
 
 
-def call(body, name, inputs, kinds, outs, out_kinds, scratch, steps=None, maps=None, aliases={}):
+def call(body, name, inputs, kinds, outs, out_kinds, scratch, steps=None, maps=None, aliases={}, macs=500, marks=()):
     spec = {
         "s": pl.BlockSpec(memory_space=pltpu.SMEM),
         "v": pl.BlockSpec(memory_space=pltpu.VMEM),
@@ -132,18 +131,22 @@
     }
     out_specs = [spec[kind] for kind in out_kinds] if maps is None else maps
     grid = {} if steps is None else {"grid": (steps,)}
+
+    def unmarked(*refs):
+        body(*refs[: len(inputs)], *refs[len(inputs) + len(marks) :])
+
     return pl.pallas_call(
-        body,
-        in_specs=[spec[kind] for kind in kinds],
+        unmarked,
+        in_specs=[spec[kind] for kind in (*kinds, *"h" * len(marks))],
         out_specs=out_specs,
         out_shape=outs,
         scratch_shapes=scratch,
         input_output_aliases=aliases,
         compiler_params=pltpu.CompilerParams(vmem_limit_bytes=VMEM_LIMIT),
-        cost_estimate=COST,
+        cost_estimate=pl.CostEstimate(flops=2 * macs, bytes_accessed=1000, transcendentals=0),
         name=name,
         **grid,
-    )(*inputs)
+    )(*inputs, *marks)
 
 
 def tiles_of(count, height, width):
@@ -290,10 +293,11 @@
             pltpu.VMEM((slots, width, tile), BF16),
             pltpu.SemaphoreType.DMA((slots,)),
         ],
-    )
-
-
-def input_back(me, gate_pieces, up_pieces, gate_w, up_w, gate_m, up_m, tile):
+        macs=2 * total * depth * width,
+    )
+
+
+def input_back(me, gate_pieces, up_pieces, gate_w, up_w, gate_m, up_m, tile, marks=()):
     depth, width = gate_w.shape
     total = 2 * gate_pieces[0].shape[0]
     block = depth // gate_m.shape[0]
@@ -335,33 +339,49 @@
         ],
         steps,
         [pl.BlockSpec((total // 2, tile), lambda i: (0, i))] * 2,
-    )
-
-
-def weight_back(me, pieces, tokens, mask, tile, left, right, earlier=None):
+        macs=2 * total * depth * width,
+        marks=marks,
+    )
+
+
+def weight_back(me, pieces, tokens, mask, tile, left, right, earlier=None, marks=()):
     total, depth = tokens.shape
     block = depth // mask.shape[0]
     width = mask.shape[1] * block
-    steps, slots = (right - left) // tile, 6
+    steps, slots = depth // tile, 6
     known = [] if earlier is None else [earlier]
 
     def body(me_ref, x_ref, m_ref, *refs):
-        refs, (out, mark, x_t, a_s, stage, sems) = refs[:-6], refs[-6:]
+        refs, (out, mark, a_s, stage, sems) = refs[:-5], refs[-5:]
         mark[...] = jnp.zeros_like(mark)
 
         def leave(i):
-            at = slice(left + i * tile, left + (i + 1) * tile)
-            return pltpu.make_async_copy(stage.at[i % slots], out.at[:, at], sems.at[i % slots])
-
-        x_t[...] = x_ref[...].T
+            rows = slice(i * tile, (i + 1) * tile)
+            return pltpu.make_async_copy(
+                stage.at[i % slots], out.at[rows, left:right], sems.at[i % slots]
+            )
+
         ways = (True, False) if left == 0 else (False,)
-        join_halves(me_ref[0], [(way, *refs[2 * n : 2 * n + 2]) for n, way in enumerate(ways[: len(pieces) // 2])], a_s)
+        join_halves(
+            me_ref[0],
+            [(way, *refs[2 * n : 2 * n + 2]) for n, way in enumerate(ways[: len(pieces) // 2])],
+            a_s,
+        )
         m = spread(m_ref[...], block)[:, left:right]
         for i in range(steps):
-            at = slice(i * tile, (i + 1) * tile)
             if i >= slots:
                 leave(i - slots).wait()
-            masked_product(x_t, a_s[:, at], m[:, at], stage.at[i % slots], block)
+            got = lax.dot_general(
+                x_ref[:, i * tile : (i + 1) * tile],
+                a_s[...],
+                (((0,), (0,)), ((), ())),
+                preferred_element_type=F32,
+            )
+            for j in range(tile // block):
+                line = i * (tile // block) + j
+                stage[i % slots, j * block : (j + 1) * block, :] = (
+                    got[j * block : (j + 1) * block, :] * m[line : line + 1, :]
+                ).astype(BF16)
             leave(i).start()
         for i in range(max(steps - slots, 0), steps):
             leave(i).wait()
@@ -373,12 +393,10 @@
         "svv" + "v" * len(pieces) + "h" * len(known),
         [shaped(depth, width, kind=BF16), shaped(8, 128)],
         "hv",
-        [
-            pltpu.VMEM((depth, total), BF16),
-            pltpu.VMEM((total, right - left), BF16),
-            *tiles_of(slots, depth, tile),
-        ],
+        [pltpu.VMEM((total, right - left), BF16), *tiles_of(slots, tile, right - left)],
         aliases={3 + len(pieces): 0} if known else {},
+        macs=total * depth * (right - left),
+        marks=marks,
     )
 
 
@@ -393,7 +411,6 @@
 def local(rows, cols, tokens_in, grad_out, gate_w, up_w, down_w, gate_mask, up_mask, down_mask):
     me = lax.axis_index("row").astype(jnp.int32)[None]
     width = gate_w.shape[1]
-    tile = 256 if width % 256 == 0 else 128
     wide = 512 if width % 512 == 0 else 128
 
     def over_row(value, bit):
@@ -417,15 +434,17 @@
         yield own
 
     def leaving(send, keep):
-        bit = 1
+        bit, earlier = 1, None
         while bit < cols:
             got = over_col(send, bit)
-            earlier = yield send
-            keep = keep + (got if earlier is None else after(got, earlier))
+            earlier = yield send, earlier
+            if earlier is not None:
+                got, earlier = lax.optimization_barrier((got, earlier))
+            keep = keep + got
             bit *= 2
             if bit < cols:
                 keep, send = halve(keep)
-        yield keep.astype(BF16)
+        yield keep.astype(BF16), earlier
 
     def last(rounds):
         for value in rounds:
@@ -488,35 +507,36 @@
     grad_down, out_send, out_keep = down_back(
         after(me, gate_all[0], gate_all[2]), hidden_all, grads, down_w, down_mask, 256
     )
-    up_all = all_halves(*up_near, out_send)
-    gate_all = lax.optimization_barrier((*gate_all, out_send, up_all[0], up_all[2]))[:4]
+    up_near = list(up_near)
+    up_near[1], up_near[3], out_send = lax.optimization_barrier((up_near[1], up_near[3], out_send))
+    up_all = all_halves(*up_near)
     out_rounds = leaving(out_send, out_keep)
     next(out_rounds)
     grad_gate, mark = weight_back(
-        after(me, out_send), gate_all, tokens, gate_mask, tile, 0, width
-    )
-    out_send = out_rounds.send(mark)
-    up_all = lax.optimization_barrier((*up_all, mark))[:4]
+        after(me, out_send), gate_all[:2], tokens, gate_mask, 256, 0, front
+    )
+    _, mark = out_rounds.send(mark)
+    grad_gate, mark = weight_back(
+        me, gate_all[2:], tokens, gate_mask, 256, front, width, grad_gate, [mark]
+    )
+    _, mark = out_rounds.send(mark)
     in_send, in_keep = input_back(
-        after(me, mark, out_send), gate_all, up_all, gate_w, up_w, gate_mask, up_mask, 256
-    )
-    out_send = out_rounds.send(in_send)
+        me, gate_all, up_all, gate_w, up_w, gate_mask, up_mask, 256, [mark]
+    )
+    layer_out, in_send = out_rounds.send(in_send)
     in_rounds = leaving(in_send, in_keep)
     next(in_rounds)
-    in_send = in_rounds.send(None)
+    in_send, _ = in_rounds.send(None)
     grad_up, mark = weight_back(
-        after(me, in_send, out_send), up_all[:2], tokens, up_mask, tile, 0, front
-    )
-    layer_out = out_rounds.send(mark)
-    in_send = in_rounds.send(mark)
+        after(me, in_send), up_all[:2], tokens, up_mask, 256, 0, front
+    )
+    in_send, mark = in_rounds.send(mark)
     grad_up, mark = weight_back(
-        after(me, in_send), up_all[2:], tokens, up_mask, tile, front, width, grad_up
-    )
+        after(me, in_send), up_all[2:], tokens, up_mask, 256, front, width, grad_up, [mark]
+    )
+    grad_in, _ = in_rounds.send(None)
     if cols > 8:
-        layer_out = last(out_rounds)
-    grad_in = in_rounds.send(mark)
-    if cols > 8:
-        grad_in = last(in_rounds)
+        (layer_out, _), (grad_in, _) = last(out_rounds), last(in_rounds)
     return (layer_out, grad_in, grad_gate, grad_up, grad_down)
 
 

time: 176 us -> 172 us (0.977)
  waiting for transfers between devices: 51.9 us -> 43.9 us
  Pallas kernels: 78.1 us -> 80.3 us
    ppermute x32, waiting for transfers between devices: 51.9 us -> 43.9 us  [swap(): return lax.ppermute(value, axis, [(i, i ^ bit) for i in range(size)])]
    pallas_call x8 -> x9, Pallas kernels: 78.1 us -> 80.3 us  [call(): pl.pallas_call(unmarked, in_specs=[spec[kind] for kind in (*kinds, *'h' *...]
  transfers between devices with their start and end apart: 32 -> 32, of which waited for: 13 -> 14; matrix products, arithmetic and copies ran while one was open for 3% -> 3% of each run, Pallas kernels for 35% -> 47%
where the time goes in v3:
time: 172 us
  Pallas kernels  80.3 us (47%)
  waiting for transfers between devices  43.9 us (26%)
  starting transfers between devices  33.9 us (20%)
  local copies, waits for them, and re-layouts  7.61 us (4%)
  other arithmetic  4.72 us (3%)
    pallas_call x9, Pallas kernels, call(): pl.pallas_call(unmarked, in_specs=[spec[kind] for kind in (*kinds, *'h' *...  80.3 us
    ppermute x32, waiting for transfers between devices, swap(): return lax.ppermute(value, axis, [(i, i ^ bit) for i in range(size)])  43.9 us
    ppermute x32, starting transfers between devices, swap(): return lax.ppermute(value, axis, [(i, i ^ bit) for i in range(size)])  33.9 us
    unnamed x54, local copies, waits for them, and re-layouts  6.55 us
  transfers between devices with their start and end apart: 32, of which 14 were waited for; matrix products, arithmetic and copies ran while one was open for 3% of the time, Pallas kernels for 47%

profile of v3, /device:TPU:0, one launch (start us, length us, event | category | flops | bytes accessed | tf_op | source)
XLA Modules:
  0.0 171.7 jit_solution(12764780026271014881)
XLA Ops:
  0.7 4.1 %collective-permute-start = (bf16[24,2048]{1,0:T(8,128)(2,1)}, bf16[24,2048]{1,0:T(8,128)(2,1)S(1)}, u32[]{:S(2)}, u32[]{:S(2)}) collective-permute-start(bf16[24,2048]{1,0:T(8,128)(2,1)} %param.8), channel_id=1, source_target_pairs={{0,4},{1,5},{2,6},{3,7},{4,0},{5,1},{6,2},{7,3},{8,12},{9,13},{10,... | collective-permute-start | bytes 294920 | tf_op jit(solution)/shard_map/ppermute | solution.py:404
  5.7 4.2 %collective-permute-done = bf16[24,2048]{1,0:T(8,128)(2,1)S(1)} collective-permute-done((bf16[24,2048]{1,0:T(8,128)(2,1)}, bf16[24,2048]{1,0:T(8,128)(2,1)S(1)}, u32[]{:S(2)}, u32[]{:S(2)}) %collective-permute-start) | collective-permute-done | bytes 98336 | tf_op jit(solution)/shard_map/ppermute | solution.py:404
  11.7 5.2 %collective-permute-done.1 = bf16[48,2048]{1,0:T(8,128)(2,1)S(1)} collective-permute-done((bf16[48,2048]{1,0:T(8,128)(2,1)S(1)}, bf16[48,2048]{1,0:T(8,128)(2,1)S(1)}, u32[]{:S(2)}, u32[]{:S(2)}) %collective-permute-start.1) | collective-permute-done | bytes 196640 | tf_op jit(solution)/shard_map/ppermute | solution.py:404
  17.8 3.1 %collective-permute-start.3 = (bf16[24,2048]{1,0:T(8,128)(2,1)S(1)}, bf16[24,2048]{1,0:T(8,128)(2,1)S(1)}, u32[]{:S(2)}, u32[]{:S(2)}) collective-permute-start(bf16[24,2048]{1,0:T(8,128)(2,1)S(1)} %copy-done.10), channel_id=1, source_target_pairs={{0,4},{1,5},{2,6},{3,7},{4,0},{5,1},{6,2},{7,3},{8,12},{9,13},{10,... | collective-permute-start | bytes 294920 | tf_op jit(solution)/shard_map/ppermute | solution.py:404
  21.8 8.3 %forward_part.2 = (bf16[96,3584]{1,0:T(8,128)(2,1)}, f32[96,3584]{1,0:T(8,128)}) custom-call(s32[1]{0:T(128)} %bitcast.refs_0_, bf16[192,2048]{1,0:T(8,128)(2,1)} %copy-done, bf16[2048,3584]{1,0:T(8,128)(2,1)} %refs_9_.1, s32[32,56]{1,0:T(8,128)} %refs_11_.1), custom_call_target="tpu_custom_call" | custom-call | flops 1000 | bytes 1000 | tf_op jit(solution)/shard_map/forward_part/pallas_call | solution.py:138
  30.1 1.8 %collective-permute-start.4 = (bf16[48,2048]{1,0:T(8,128)(2,1)S(1)}, bf16[48,2048]{1,0:T(8,128)(2,1)S(1)}, u32[]{:S(2)}, u32[]{:S(2)}) collective-permute-start(bf16[48,2048]{1,0:T(8,128)(2,1)S(1)} %pad_maximum_fusion.2), channel_id=1, source_target_pairs={{0,2},{1,3},{2,0},{3,1},{4,6},{5,7},{6,4},{7,5},{8,10},{9,11},{10,... | collective-permute-start | bytes 589832 | tf_op jit(solution)/shard_map/ppermute | solution.py:404
  31.9 1.6 collective-permute-start.7
  33.5 8.3 %forward_part.3 = (bf16[96,3584]{1,0:T(8,128)(2,1)}, f32[96,3584]{1,0:T(8,128)}) custom-call(s32[1]{0:T(128)} %bitcast.refs_0_, bf16[192,2048]{1,0:T(8,128)(2,1)} %copy-done, bf16[2048,3584]{1,0:T(8,128)(2,1)} %refs_10_.1, s32[32,56]{1,0:T(8,128)} %refs_2_.13), custom_call_target="tpu_custom_call" | custom-call | flops 1000 | bytes 1000 | tf_op jit(solution)/shard_map/forward_part/pallas_call | solution.py:138
  41.8 1.6 collective-permute-start.8
  44.3 1.7 collective-permute-done.5
  46.8 10.2 %hidden_part.1 = (bf16[96,2048]{1,0:T(8,128)(2,1)}, f32[96,2048]{1,0:T(8,128)}, bf16[96,1536]{1,0:T(8,128)(2,1)}, f32[96,1536]{1,0:T(8,128)}) custom-call(s32[1]{0:T(128)} %bitcast.refs_0_, bf16[192,2048]{1,0:T(8,128)(2,1)} %copy-done.7, bf16[3584,2048]{1,0:T(8,128)(2,1)} %refs_6_.1, s32[56,32]{1,0:T(8,128)} %copy.15.refs_3_), custom_call_target="tpu_custom_call" | custom-call | flops 1000 | bytes 1000 | tf_op jit(solution)/shard_map/hidden_part/pallas_call | solution.py:138
  59.3 1.6 collective-permute-start.10
  61.7 6.0 %collective-permute-done.12 = bf16[96,1536]{1,0:T(8,128)(2,1)S(1)} collective-permute-done((bf16[96,1536]{1,0:T(8,128)(2,1)}, bf16[96,1536]{1,0:T(8,128)(2,1)S(1)}, u32[]{:S(2)}, u32[]{:S(2)}) %collective-permute-start.12) | collective-permute-done | bytes 294944 | tf_op jit(solution)/shard_map/ppermute | solution.py:404
  67.8 1.6 collective-permute-start.13
  70.1 5.0 %collective-permute-done.10 = bf16[48,3584]{1,0:T(8,128)(2,1)S(1)} collective-permute-done((bf16[48,3584]{1,0:T(8,128)(2,1)S(1)}, bf16[48,3584]{1,0:T(8,128)(2,1)S(1)}, u32[]{:S(2)}, u32[]{:S(2)}) %collective-permute-start.10) | collective-permute-done | bytes 344096 | tf_op jit(solution)/shard_map/ppermute | solution.py:404
  75.1 1.5 collective-permute-done.11
  77.5 1.5 collective-permute-done.13
  79.9 4.2 %collective-permute-done.15 = bf16[48,1536]{1,0:T(8,128)(2,1)S(1)} collective-permute-done((bf16[48,1536]{1,0:T(8,128)(2,1)S(1)}, bf16[48,1536]{1,0:T(8,128)(2,1)S(1)}, u32[]{:S(2)}, u32[]{:S(2)}) %collective-permute-start.15) | collective-permute-done | bytes 147488 | tf_op jit(solution)/shard_map/ppermute | solution.py:404
  85.3 1.6 collective-permute-start.16
  86.9 1.5 collective-permute-start.17
  88.5 8.4 %collective-permute-done.17 = bf16[48,1536]{1,0:T(8,128)(2,1)S(1)} collective-permute-done((bf16[48,1536]{1,0:T(8,128)(2,1)S(1)}, bf16[48,1536]{1,0:T(8,128)(2,1)S(1)}, u32[]{:S(2)}, u32[]{:S(2)}) %collective-permute-start.17) | collective-permute-done | bytes 147488 | tf_op jit(solution)/shard_map/ppermute | solution.py:404
  98.3 1.5 collective-permute-start.20
  99.9 1.3 collective-permute-start.21
  101.1 15.6 %down_back.1 = (bf16[3584,2048]{1,0:T(8,128)(2,1)}, f32[96,2048]{1,0:T(8,128)}, f32[96,2048]{1,0:T(8,128)}) custom-call(s32[1]{0:T(128)} %bitcast.refs_0_, bf16[96,2048]{1,0:T(8,128)(2,1)} %copy-done.16, bf16[96,2048]{1,0:T(8,128)(2,1)} %copy-done.19, bf16[96,1536]{1,0:T(8,128)(2,1)} %copy-done.17, bf16[96,1536]{1,0:T(8,128)(2,1)} %copy-done.20, ...), custom_call_target="tpu_custom_call" | custom-call | flops 5637144576 | bytes 1000 | tf_op jit(solution)/shard_map/down_back/pallas_call | solution.py:138
  118.6 5.8 %weight_back.4 = (bf16[2048,3584]{1,0:T(8,128)(2,1)}, f32[8,128]{1,0:T(8,128)}) custom-call(s32[1]{0:T(128)} %bitcast.refs_0_, bf16[192,2048]{1,0:T(8,128)(2,1)} %copy-done, s32[32,56]{1,0:T(8,128)} %refs_11_.1, bf16[96,2048]{1,0:T(8,128)(2,1)} %copy-done.8, bf16[96,2048]{1,0:T(8,128)(2,1)} %copy-done.14), custom_call_target="tpu_custom_call" | custom-call | flops 1610612736 | bytes 1000 | tf_op jit(solution)/shard_map/weight_back/pallas_call | solution.py:138
  126.2 5.1 %weight_back.5 = (bf16[2048,3584]{1,0:T(8,128)(2,1)}, f32[8,128]{1,0:T(8,128)}) custom-call(s32[1]{0:T(128)} %bitcast.refs_0_, bf16[192,2048]{1,0:T(8,128)(2,1)} %copy-done, s32[32,56]{1,0:T(8,128)} %refs_11_.1, bf16[96,1536]{1,0:T(8,128)(2,1)} %copy-done.2, bf16[96,1536]{1,0:T(8,128)(2,1)} %copy-done.5, ...), custom_call_target="tpu_custom_call", output_to_operand_aliasing={{0}: (5, {})} | custom-call | flops 1207959552 | bytes 1000 | tf_op jit(solution)/shard_map/weight_back/pallas_call | solution.py:138
  135.3 16.1 %input_back.1 = (f32[96,2048]{1,0:T(8,128)}, f32[96,2048]{1,0:T(8,128)}) custom-call(s32[1]{0:T(128)} %bitcast.refs_0_, bf16[96,2048]{1,0:T(8,128)(2,1)} %copy-done.8, bf16[96,2048]{1,0:T(8,128)(2,1)} %copy-done.14, bf16[96,1536]{1,0:T(8,128)(2,1)} %copy-done.2, bf16[96,1536]{1,0:T(8,128)(2,1)} %copy-done.5, bf16[96,2048]{1,0:T(8,128)(2,1)} %copy-done.9, ...), custom_call_target="tpu_custom_call" | custom-call | flops 5637144576 | bytes 1000 | tf_op jit(solution)/shard_map/input_back/pallas_call | solution.py:138
  151.6 2.5 %collective-permute-done.29 = f32[96,2048]{1,0:T(8,128)S(1)} collective-permute-done((f32[96,2048]{1,0:T(8,128)}, f32[96,2048]{1,0:T(8,128)S(1)}, u32[]{:S(2)}, u32[]{:S(2)}) %collective-permute-start.29) | collective-permute-done | bytes 786464 | tf_op jit(solution)/shard_map/ppermute | solution.py:404
  155.3 1.8 %collective-permute-start.30 = (bf16[48,2048]{1,0:T(8,128)(2,1)S(1)}, bf16[48,2048]{1,0:T(8,128)(2,1)S(1)}, u32[]{:S(2)}, u32[]{:S(2)}) collective-permute-start(bf16[48,2048]{1,0:T(8,128)(2,1)S(1)} %slice.150), channel_id=1, source_target_pairs={{0,2},{1,3},{2,0},{3,1},{4,6},{5,7},{6,4},{7,5},{8,10},{9,11},{10,... | collective-permute-start | bytes 589832 | tf_op jit(solution)/shard_map/ppermute | solution.py:404
  157.7 5.8 %weight_back.6 = (bf16[2048,3584]{1,0:T(8,128)(2,1)}, f32[8,128]{1,0:T(8,128)}) custom-call(s32[1]{0:T(128)} %bitcast.refs_0_, bf16[192,2048]{1,0:T(8,128)(2,1)} %copy-done, s32[32,56]{1,0:T(8,128)} %refs_2_.13, bf16[96,2048]{1,0:T(8,128)(2,1)} %copy-done.9, bf16[96,2048]{1,0:T(8,128)(2,1)} %copy-done.15), custom_call_target="tpu_custom_call" | custom-call | flops 1610612736 | bytes 1000 | tf_op jit(solution)/shard_map/weight_back/pallas_call | solution.py:138
  164.7 5.1 %weight_back.7 = (bf16[2048,3584]{1,0:T(8,128)(2,1)}, f32[8,128]{1,0:T(8,128)}) custom-call(s32[1]{0:T(128)} %bitcast.refs_0_, bf16[192,2048]{1,0:T(8,128)(2,1)} %copy-done, s32[32,56]{1,0:T(8,128)} %refs_2_.13, bf16[96,1536]{1,0:T(8,128)(2,1)} %copy-done.1, bf16[96,1536]{1,0:T(8,128)(2,1)} %copy-done.6, ...), custom_call_target="tpu_custom_call", output_to_operand_aliasing={{0}: (5, {})} | custom-call | flops 1207959552 | bytes 1000 | tf_op jit(solution)/shard_map/weight_back/pallas_call | solution.py:138
  169.8 1.2 collective-permute-done.31
  (131 shorter events, 25.7 us)
Async XLA Ops:
  0.7 9.2 %collective-permute-start = (bf16[24,2048]{1,0:T(8,128)(2,1)}, bf16[24,2048]{1,0:T(8,128)(2,1)S(1)}, u32[]{:S(2)}, u32[]{:S(2)}) collective-permute-start(bf16[24,2048]{1,0:T(8,128)(2,1)} %param.8), channel_id=1, source_target_pairs={{0,4},{1,5},{2,6},{3,7},{4,0},{5,1},{6,2},{7,3},{8,12},{9,13},{10,... | collective-permute-start | bytes 294920 | tf_op jit(solution)/shard_map/ppermute | solution.py:404
  10.8 6.2 %collective-permute-start.1 = (bf16[48,2048]{1,0:T(8,128)(2,1)S(1)}, bf16[48,2048]{1,0:T(8,128)(2,1)S(1)}, u32[]{:S(2)}, u32[]{:S(2)}) collective-permute-start(bf16[48,2048]{1,0:T(8,128)(2,1)S(1)} %pad_maximum_fusion.1), channel_id=1, source_target_pairs={{0,2},{1,3},{2,0},{3,1},{4,6},{5,7},{6,4},{7,5},{8,10},{9,11},{10,... | collective-permute-start | bytes 589832 | tf_op jit(solution)/shard_map/ppermute | solution.py:404
  17.0 3.9 %collective-permute-start.2 = (bf16[96,2048]{1,0:T(8,128)(2,1)S(1)}, bf16[96,2048]{1,0:T(8,128)(2,1)S(1)}, u32[]{:S(2)}, u32[]{:S(2)}) collective-permute-start(bf16[96,2048]{1,0:T(8,128)(2,1)S(1)} %get-tuple-element.138), channel_id=1, source_target_pairs={{0,1},{1,0},{2,3},{3,2},{4,5},{5,4},{6,7},{7,6},{8,9},{9,8},{10,11... | collective-permute-start | bytes 1179656 | tf_op jit(solution)/shard_map/ppermute | solution.py:404
  17.8 12.4 %collective-permute-start.3 = (bf16[24,2048]{1,0:T(8,128)(2,1)S(1)}, bf16[24,2048]{1,0:T(8,128)(2,1)S(1)}, u32[]{:S(2)}, u32[]{:S(2)}) collective-permute-start(bf16[24,2048]{1,0:T(8,128)(2,1)S(1)} %copy-done.10), channel_id=1, source_target_pairs={{0,4},{1,5},{2,6},{3,7},{4,0},{5,1},{6,2},{7,3},{8,12},{9,13},{10,... | collective-permute-start | bytes 294920 | tf_op jit(solution)/shard_map/ppermute | solution.py:404
  30.1 14.0 %collective-permute-start.4 = (bf16[48,2048]{1,0:T(8,128)(2,1)S(1)}, bf16[48,2048]{1,0:T(8,128)(2,1)S(1)}, u32[]{:S(2)}, u32[]{:S(2)}) collective-permute-start(bf16[48,2048]{1,0:T(8,128)(2,1)S(1)} %pad_maximum_fusion.2), channel_id=1, source_target_pairs={{0,2},{1,3},{2,0},{3,1},{4,6},{5,7},{6,4},{7,5},{8,10},{9,11},{10,... | collective-permute-start | bytes 589832 | tf_op jit(solution)/shard_map/ppermute | solution.py:404
  31.9 26.1 %collective-permute-start.7 = (bf16[96,3584]{1,0:T(8,128)(2,1)}, bf16[96,3584]{1,0:T(8,128)(2,1)S(1)}, u32[]{:S(2)}, u32[]{:S(2)}) collective-permute-start(bf16[96,3584]{1,0:T(8,128)(2,1)} %get-tuple-element.68), channel_id=1, source_target_pairs={{0,8},{8,0},{16,24},{24,16},{1,9},{9,1},{17,25},{25,17},{2,10},{10... | collective-permute-start | bytes 2064392 | tf_op jit(solution)/shard_map/ppermute | solution.py:404
  41.8 17.3 %collective-permute-start.8 = (bf16[96,3584]{1,0:T(8,128)(2,1)}, bf16[96,3584]{1,0:T(8,128)(2,1)S(1)}, u32[]{:S(2)}, u32[]{:S(2)}) collective-permute-start(bf16[96,3584]{1,0:T(8,128)(2,1)} %get-tuple-element.70), channel_id=1, source_target_pairs={{0,16},{8,24},{16,0},{24,8},{1,17},{9,25},{17,1},{25,9},{2,18},{10... | collective-permute-start | bytes 2064392 | tf_op jit(solution)/shard_map/ppermute | solution.py:404
  44.1 1.8 %collective-permute-start.5 = (bf16[96,2048]{1,0:T(8,128)(2,1)S(1)}, bf16[96,2048]{1,0:T(8,128)(2,1)S(1)}, u32[]{:S(2)}, u32[]{:S(2)}) collective-permute-start(bf16[96,2048]{1,0:T(8,128)(2,1)S(1)} %pad_maximum_fusion), channel_id=1, source_target_pairs={{0,1},{1,0},{2,3},{3,2},{4,5},{5,4},{6,7},{7,6},{8,9},{9,8},{10,11... | collective-permute-start | bytes 1179656 | tf_op jit(solution)/shard_map/ppermute | solution.py:404
  57.0 12.3 %collective-permute-start.6 = (bf16[96,2048]{1,0:T(8,128)(2,1)}, bf16[96,2048]{1,0:T(8,128)(2,1)S(1)}, u32[]{:S(2)}, u32[]{:S(2)}) collective-permute-start(bf16[96,2048]{1,0:T(8,128)(2,1)} %get-tuple-element.77), channel_id=1, source_target_pairs={{0,8},{8,0},{16,24},{24,16},{1,9},{9,1},{17,25},{25,17},{2,10},{10... | collective-permute-start | bytes 1179656 | tf_op jit(solution)/shard_map/ppermute | solution.py:404
  57.6 10.1 %collective-permute-start.12 = (bf16[96,1536]{1,0:T(8,128)(2,1)}, bf16[96,1536]{1,0:T(8,128)(2,1)S(1)}, u32[]{:S(2)}, u32[]{:S(2)}) collective-permute-start(bf16[96,1536]{1,0:T(8,128)(2,1)} %get-tuple-element.88), channel_id=1, source_target_pairs={{0,16},{8,24},{16,0},{24,8},{1,17},{9,25},{17,1},{25,9},{2,18},{10... | collective-permute-start | bytes 884744 | tf_op jit(solution)/shard_map/ppermute | solution.py:404
  59.3 15.8 %collective-permute-start.10 = (bf16[48,3584]{1,0:T(8,128)(2,1)S(1)}, bf16[48,3584]{1,0:T(8,128)(2,1)S(1)}, u32[]{:S(2)}, u32[]{:S(2)}) collective-permute-start(bf16[48,3584]{1,0:T(8,128)(2,1)S(1)} %slice.149), channel_id=1, source_target_pairs={{0,16},{8,24},{16,0},{24,8},{1,17},{9,25},{17,1},{25,9},{2,18},{10... | collective-permute-start | bytes 1032200 | tf_op jit(solution)/shard_map/ppermute | solution.py:404
  61.1 15.5 %collective-permute-start.11 = (bf16[48,3584]{1,0:T(8,128)(2,1)S(1)}, bf16[48,3584]{1,0:T(8,128)(2,1)S(1)}, u32[]{:S(2)}, u32[]{:S(2)}) collective-permute-start(bf16[48,3584]{1,0:T(8,128)(2,1)S(1)} %slice.148), channel_id=1, source_target_pairs={{0,8},{8,0},{16,24},{24,16},{1,9},{9,1},{17,25},{25,17},{2,10},{10... | collective-permute-start | bytes 1032200 | tf_op jit(solution)/shard_map/ppermute | solution.py:404
  67.8 11.2 %collective-permute-start.13 = (bf16[48,1536]{1,0:T(8,128)(2,1)S(1)}, bf16[48,1536]{1,0:T(8,128)(2,1)S(1)}, u32[]{:S(2)}, u32[]{:S(2)}) collective-permute-start(bf16[48,1536]{1,0:T(8,128)(2,1)S(1)} %slice.153), channel_id=1, source_target_pairs={{0,8},{8,0},{16,24},{24,16},{1,9},{9,1},{17,25},{25,17},{2,10},{10... | collective-permute-start | bytes 442376 | tf_op jit(solution)/shard_map/ppermute | solution.py:404
  69.5 10.2 %collective-permute-start.9 = (bf16[48,2048]{1,0:T(8,128)(2,1)S(1)}, bf16[48,2048]{1,0:T(8,128)(2,1)S(1)}, u32[]{:S(2)}, u32[]{:S(2)}) collective-permute-start(bf16[48,2048]{1,0:T(8,128)(2,1)S(1)} %slice.152), channel_id=1, source_target_pairs={{0,16},{8,24},{16,0},{24,8},{1,17},{9,25},{17,1},{25,9},{2,18},{10... | collective-permute-start | bytes 589832 | tf_op jit(solution)/shard_map/ppermute | solution.py:404
  76.9 7.2 %collective-permute-start.14 = (bf16[48,2048]{1,0:T(8,128)(2,1)S(1)}, bf16[48,2048]{1,0:T(8,128)(2,1)S(1)}, u32[]{:S(2)}, u32[]{:S(2)}) collective-permute-start(bf16[48,2048]{1,0:T(8,128)(2,1)S(1)} %slice.102), channel_id=1, source_target_pairs={{0,16},{8,24},{16,0},{24,8},{1,17},{9,25},{17,1},{25,9},{2,18},{10... | collective-permute-start | bytes 589832 | tf_op jit(solution)/shard_map/ppermute | solution.py:404
  79.0 5.1 %collective-permute-start.15 = (bf16[48,1536]{1,0:T(8,128)(2,1)S(1)}, bf16[48,1536]{1,0:T(8,128)(2,1)S(1)}, u32[]{:S(2)}, u32[]{:S(2)}) collective-permute-start(bf16[48,1536]{1,0:T(8,128)(2,1)S(1)} %slice.103), channel_id=1, source_target_pairs={{0,8},{8,0},{16,24},{24,16},{1,9},{9,1},{17,25},{25,17},{2,10},{10... | collective-permute-start | bytes 442376 | tf_op jit(solution)/shard_map/ppermute | solution.py:404
  84.1 12.7 %collective-permute-start.18 = (bf16[96,2048]{1,0:T(8,128)(2,1)S(1)}, bf16[96,2048]{1,0:T(8,128)(2,1)S(1)}, u32[]{:S(2)}, u32[]{:S(2)}) collective-permute-start(bf16[96,2048]{1,0:T(8,128)(2,1)S(1)} %constant_dynamic-update-slice_fusion.11.refs_1_), channel_id=1, source_target_pairs={{0,8},{8,0},{16,24},{24,16},{1,9},{9,1},{17,25},{25,17},{2,10},{10... | collective-permute-start | bytes 1179656 | tf_op jit(solution)/shard_map/ppermute | solution.py:404
  84.8 12.1 %collective-permute-start.19 = (bf16[96,1536]{1,0:T(8,128)(2,1)S(1)}, bf16[96,1536]{1,0:T(8,128)(2,1)S(1)}, u32[]{:S(2)}, u32[]{:S(2)}) collective-permute-start(bf16[96,1536]{1,0:T(8,128)(2,1)S(1)} %constant_dynamic-update-slice_fusion.13.refs_3_), channel_id=1, source_target_pairs={{0,16},{8,24},{16,0},{24,8},{1,17},{9,25},{17,1},{25,9},{2,18},{10... | collective-permute-start | bytes 884744 | tf_op jit(solution)/shard_map/ppermute | solution.py:404
  85.3 11.5 %collective-permute-start.16 = (bf16[48,2048]{1,0:T(8,128)(2,1)S(1)}, bf16[48,2048]{1,0:T(8,128)(2,1)S(1)}, u32[]{:S(2)}, u32[]{:S(2)}) collective-permute-start(bf16[48,2048]{1,0:T(8,128)(2,1)S(1)} %get-tuple-element.96), channel_id=1, source_target_pairs={{0,16},{8,24},{16,0},{24,8},{1,17},{9,25},{17,1},{25,9},{2,18},{10... | collective-permute-start | bytes 589832 | tf_op jit(solution)/shard_map/ppermute | solution.py:404
  86.9 9.9 %collective-permute-start.17 = (bf16[48,1536]{1,0:T(8,128)(2,1)S(1)}, bf16[48,1536]{1,0:T(8,128)(2,1)S(1)}, u32[]{:S(2)}, u32[]{:S(2)}) collective-permute-start(bf16[48,1536]{1,0:T(8,128)(2,1)S(1)} %get-tuple-element.97), channel_id=1, source_target_pairs={{0,8},{8,0},{16,24},{24,16},{1,9},{9,1},{17,25},{25,17},{2,10},{10... | collective-permute-start | bytes 442376 | tf_op jit(solution)/shard_map/ppermute | solution.py:404
  96.9 20.9 %collective-permute-start.23 = (bf16[96,2048]{1,0:T(8,128)(2,1)S(1)}, bf16[96,2048]{1,0:T(8,128)(2,1)S(1)}, u32[]{:S(2)}, u32[]{:S(2)}) collective-permute-start(bf16[96,2048]{1,0:T(8,128)(2,1)S(1)} %constant_dynamic-update-slice_fusion.15.refs_3_.refs_1_), channel_id=1, source_target_pairs={{0,8},{8,0},{16,24},{24,16},{1,9},{9,1},{17,25},{25,17},{2,10},{10... | collective-permute-start | bytes 1179656 | tf_op jit(solution)/shard_map/ppermute | solution.py:404
  97.8 27.7 %collective-permute-start.25 = (bf16[96,1536]{1,0:T(8,128)(2,1)S(1)}, bf16[96,1536]{1,0:T(8,128)(2,1)S(1)}, u32[]{:S(2)}, u32[]{:S(2)}) collective-permute-start(bf16[96,1536]{1,0:T(8,128)(2,1)S(1)} %constant_dynamic-update-slice_fusion.17.refs_3_), channel_id=1, source_target_pairs={{0,16},{8,24},{16,0},{24,8},{1,17},{9,25},{17,1},{25,9},{2,18},{10... | collective-permute-start | bytes 884744 | tf_op jit(solution)/shard_map/ppermute | solution.py:404
  98.3 18.5 %collective-permute-start.20 = (bf16[48,2048]{1,0:T(8,128)(2,1)S(1)}, bf16[48,2048]{1,0:T(8,128)(2,1)S(1)}, u32[]{:S(2)}, u32[]{:S(2)}) collective-permute-start(bf16[48,2048]{1,0:T(8,128)(2,1)S(1)} %get-tuple-element.102), channel_id=1, source_target_pairs={{0,16},{8,24},{16,0},{24,8},{1,17},{9,25},{17,1},{25,9},{2,18},{10... | collective-permute-start | bytes 589832 | tf_op jit(solution)/shard_map/ppermute | solution.py:404
  99.9 16.9 %collective-permute-start.21 = (bf16[48,1536]{1,0:T(8,128)(2,1)S(1)}, bf16[48,1536]{1,0:T(8,128)(2,1)S(1)}, u32[]{:S(2)}, u32[]{:S(2)}) collective-permute-start(bf16[48,1536]{1,0:T(8,128)(2,1)S(1)} %get-tuple-element.103), channel_id=1, source_target_pairs={{0,8},{8,0},{16,24},{24,16},{1,9},{9,1},{17,25},{25,17},{2,10},{10... | collective-permute-start | bytes 442376 | tf_op jit(solution)/shard_map/ppermute | solution.py:404
  116.8 7.6 %collective-permute-start.22 = (f32[96,2048]{1,0:T(8,128)}, f32[96,2048]{1,0:T(8,128)S(1)}, u32[]{:S(2)}, u32[]{:S(2)}) collective-permute-start(f32[96,2048]{1,0:T(8,128)} %get-tuple-element.105), channel_id=1, source_target_pairs={{0,1},{1,0},{2,3},{3,2},{4,5},{5,4},{6,7},{7,6},{8,9},{9,8},{10,11... | collective-permute-start | bytes 2359304 | tf_op jit(solution)/shard_map/ppermute | solution.py:404
  117.0 16.9 %collective-permute-start.27 = (bf16[96,2048]{1,0:T(8,128)(2,1)S(1)}, bf16[96,2048]{1,0:T(8,128)(2,1)S(1)}, u32[]{:S(2)}, u32[]{:S(2)}) collective-permute-start(bf16[96,2048]{1,0:T(8,128)(2,1)S(1)} %constant_dynamic-update-slice_fusion.19.refs_5_.refs_3_), channel_id=1, source_target_pairs={{0,8},{8,0},{16,24},{24,16},{1,9},{9,1},{17,25},{25,17},{2,10},{10... | collective-permute-start | bytes 1179656 | tf_op jit(solution)/shard_map/ppermute | solution.py:404
  124.5 7.1 %collective-permute-start.24 = (bf16[48,2048]{1,0:T(8,128)(2,1)S(1)}, bf16[48,2048]{1,0:T(8,128)(2,1)S(1)}, u32[]{:S(2)}, u32[]{:S(2)}) collective-permute-start(bf16[48,2048]{1,0:T(8,128)(2,1)S(1)} %slice.151), channel_id=1, source_target_pairs={{0,2},{1,3},{2,0},{3,1},{4,6},{5,7},{6,4},{7,5},{8,10},{9,11},{10,... | collective-permute-start | bytes 589832 | tf_op jit(solution)/shard_map/ppermute | solution.py:404
  124.9 8.9 %collective-permute-start.28 = (bf16[96,1536]{1,0:T(8,128)(2,1)S(1)}, bf16[96,1536]{1,0:T(8,128)(2,1)S(1)}, u32[]{:S(2)}, u32[]{:S(2)}) collective-permute-start(bf16[96,1536]{1,0:T(8,128)(2,1)S(1)} %constant_dynamic-update-slice_fusion.21.refs_7_.refs_3_), channel_id=1, source_target_pairs={{0,16},{8,24},{16,0},{24,8},{1,17},{9,25},{17,1},{25,9},{2,18},{10... | collective-permute-start | bytes 884744 | tf_op jit(solution)/shard_map/ppermute | solution.py:404
  131.7 19.8 %collective-permute-start.26 = (bf16[24,2048]{1,0:T(8,128)(2,1)S(1)}, bf16[24,2048]{1,0:T(8,128)(2,1)S(1)}, u32[]{:S(2)}, u32[]{:S(2)}) collective-permute-start(bf16[24,2048]{1,0:T(8,128)(2,1)S(1)} %slice.155), channel_id=1, source_target_pairs={{0,4},{1,5},{2,6},{3,7},{4,0},{5,1},{6,2},{7,3},{8,12},{9,13},{10,... | collective-permute-start | bytes 294920 | tf_op jit(solution)/shard_map/ppermute | solution.py:404
  151.5 2.6 %collective-permute-start.29 = (f32[96,2048]{1,0:T(8,128)}, f32[96,2048]{1,0:T(8,128)S(1)}, u32[]{:S(2)}, u32[]{:S(2)}) collective-permute-start(f32[96,2048]{1,0:T(8,128)} %get-tuple-element.121), channel_id=1, source_target_pairs={{0,1},{1,0},{2,3},{3,2},{4,5},{5,4},{6,7},{7,6},{8,9},{9,8},{10,11... | collective-permute-start | bytes 2359304 | tf_op jit(solution)/shard_map/ppermute | solution.py:404
  155.3 8.3 %collective-permute-start.30 = (bf16[48,2048]{1,0:T(8,128)(2,1)S(1)}, bf16[48,2048]{1,0:T(8,128)(2,1)S(1)}, u32[]{:S(2)}, u32[]{:S(2)}) collective-permute-start(bf16[48,2048]{1,0:T(8,128)(2,1)S(1)} %slice.150), channel_id=1, source_target_pairs={{0,2},{1,3},{2,0},{3,1},{4,6},{5,7},{6,4},{7,5},{8,10},{9,11},{10,... | collective-permute-start | bytes 589832 | tf_op jit(solution)/shard_map/ppermute | solution.py:404
  163.7 7.4 %collective-permute-start.31 = (bf16[24,2048]{1,0:T(8,128)(2,1)S(1)}, bf16[24,2048]{1,0:T(8,128)(2,1)S(1)}, u32[]{:S(2)}, u32[]{:S(2)}) collective-permute-start(bf16[24,2048]{1,0:T(8,128)(2,1)S(1)} %slice.154), channel_id=1, source_target_pairs={{0,4},{1,5},{2,6},{3,7},{4,0},{5,1},{6,2},{7,3},{8,12},{9,13},{10,... | collective-permute-start | bytes 294920 | tf_op jit(solution)/shard_map/ppermute | solution.py:404
  (21 other events, 169.6 us)

commit v4 on v3

--- a/solution.py
+++ b/solution.py
@@ -10,6 +10,7 @@
 BF16 = jnp.bfloat16
 F32 = jnp.float32
 VMEM_LIMIT = 56 * 1024 * 1024
+AHEAD = 3
 NT = (((1,), (1,)), ((), ()))
 
 
@@ -56,10 +57,9 @@
             source.at[:, at] if columns else source.at[at, :], held.at[i], sems.at[i]
         )
 
-    def begin():
-        for i in range(pairs[0][1].shape[0]):
-            for pair in pairs:
-                copy(pair, i).start()
+    def begin(i):
+        for pair in pairs:
+            copy(pair, i).start()
 
     def arrived(i):
         for pair in pairs:
@@ -70,15 +70,22 @@
 
 def at_step(pairs, columns, size, prepare):
     begin, arrived = fetches(pairs, columns, size)
-    step = pl.program_id(0)
+    step, steps = pl.program_id(0), pairs[0][1].shape[0]
 
     @pl.when(step == 0)
     def _():
-        begin()
+        for i in range(min(AHEAD, steps)):
+            begin(i)
         prepare()
 
-    for i in range(pairs[0][1].shape[0]):
-        pl.when(step == i)(functools.partial(arrived, i))
+    for i in range(steps):
+
+        @pl.when(step == i)
+        def _(i=i):
+            if i + AHEAD < steps:
+                begin(i + AHEAD)
+            arrived(i)
+
     return step
 
 
@@ -252,7 +259,8 @@
 
     def body(me_ref, h0, h1, h2, h3, g_ref, w_hbm, m_ref, gw, send, keep, hid, hid_t, held, sems, stage, outs):
         begin, arrived = fetches([(w_hbm, held, sems)], True, tile)
-        begin()
+        for i in range(min(AHEAD, steps)):
+            begin(i)
         join_halves(me_ref[0], ((True, h0, h1), (False, h2, h3)), hid)
         hid_t[...] = hid[...].T
         m = spread(m_ref[...], block)
@@ -268,6 +276,8 @@
             now = w
             if i >= slots:
                 leave(i - slots).wait()
+            if i + AHEAD < steps:
+                begin(i + AHEAD)
             if i + 1 < steps:
                 arrived(i + 1)
                 w = masked(held.at[i + 1], m[:, (i + 1) * tile : (i + 2) * tile], block)

time: 172 us -> 173 us (level)
  no operation moved by 1% of the time
where the time goes in v4:
time: 173 us; the launch traced here: 172 us
  Pallas kernels  81 us (47%)
  waiting for transfers between devices  43.8 us (25%)
  starting transfers between devices  33.9 us (20%)
  local copies, waits for them, and re-layouts  7.61 us (4%)
  other arithmetic  4.72 us (3%)
    pallas_call x9, Pallas kernels, call(): pl.pallas_call(unmarked, in_specs=[spec[kind] for kind in (*kinds, *'h' *...  81 us
    ppermute x32, waiting for transfers between devices, swap(): return lax.ppermute(value, axis, [(i, i ^ bit) for i in range(size)])  43.8 us
    ppermute x32, starting transfers between devices, swap(): return lax.ppermute(value, axis, [(i, i ^ bit) for i in range(size)])  33.9 us
    unnamed x54, local copies, waits for them, and re-layouts  6.55 us
  transfers between devices with their start and end apart: 32, of which 14 were waited for; matrix products, arithmetic and copies ran while one was open for 3% of the time, Pallas kernels for 47%

profile of v4, /device:TPU:0, one launch (start us, length us, event | category | flops | bytes accessed | tf_op | source)
XLA Modules:
  0.0 172.4 jit_solution(3335729678451947430)
XLA Ops:
  0.7 4.1 %collective-permute-start = (bf16[24,2048]{1,0:T(8,128)(2,1)}, bf16[24,2048]{1,0:T(8,128)(2,1)S(1)}, u32[]{:S(2)}, u32[]{:S(2)}) collective-permute-start(bf16[24,2048]{1,0:T(8,128)(2,1)} %param.8), channel_id=1, source_target_pairs={{0,4},{1,5},{2,6},{3,7},{4,0},{5,1},{6,2},{7,3},{8,12},{9,13},{10,... | collective-permute-start | bytes 294920 | tf_op jit(solution)/shard_map/ppermute | solution.py:414
  5.7 4.2 %collective-permute-done = bf16[24,2048]{1,0:T(8,128)(2,1)S(1)} collective-permute-done((bf16[24,2048]{1,0:T(8,128)(2,1)}, bf16[24,2048]{1,0:T(8,128)(2,1)S(1)}, u32[]{:S(2)}, u32[]{:S(2)}) %collective-permute-start) | collective-permute-done | bytes 98336 | tf_op jit(solution)/shard_map/ppermute | solution.py:414
  11.7 5.2 %collective-permute-done.1 = bf16[48,2048]{1,0:T(8,128)(2,1)S(1)} collective-permute-done((bf16[48,2048]{1,0:T(8,128)(2,1)S(1)}, bf16[48,2048]{1,0:T(8,128)(2,1)S(1)}, u32[]{:S(2)}, u32[]{:S(2)}) %collective-permute-start.1) | collective-permute-done | bytes 196640 | tf_op jit(solution)/shard_map/ppermute | solution.py:414
  17.8 3.1 %collective-permute-start.3 = (bf16[24,2048]{1,0:T(8,128)(2,1)S(1)}, bf16[24,2048]{1,0:T(8,128)(2,1)S(1)}, u32[]{:S(2)}, u32[]{:S(2)}) collective-permute-start(bf16[24,2048]{1,0:T(8,128)(2,1)S(1)} %copy-done.10), channel_id=1, source_target_pairs={{0,4},{1,5},{2,6},{3,7},{4,0},{5,1},{6,2},{7,3},{8,12},{9,13},{10,... | collective-permute-start | bytes 294920 | tf_op jit(solution)/shard_map/ppermute | solution.py:414
  21.8 8.5 %forward_part.2 = (bf16[96,3584]{1,0:T(8,128)(2,1)}, f32[96,3584]{1,0:T(8,128)}) custom-call(s32[1]{0:T(128)} %bitcast.refs_0_, bf16[192,2048]{1,0:T(8,128)(2,1)} %copy-done, bf16[2048,3584]{1,0:T(8,128)(2,1)} %refs_9_.1, s32[32,56]{1,0:T(8,128)} %refs_11_.1), custom_call_target="tpu_custom_call" | custom-call | flops 1000 | bytes 1000 | tf_op jit(solution)/shard_map/forward_part/pallas_call | solution.py:145
  30.3 1.8 %collective-permute-start.4 = (bf16[48,2048]{1,0:T(8,128)(2,1)S(1)}, bf16[48,2048]{1,0:T(8,128)(2,1)S(1)}, u32[]{:S(2)}, u32[]{:S(2)}) collective-permute-start(bf16[48,2048]{1,0:T(8,128)(2,1)S(1)} %pad_maximum_fusion.2), channel_id=1, source_target_pairs={{0,2},{1,3},{2,0},{3,1},{4,6},{5,7},{6,4},{7,5},{8,10},{9,11},{10,... | collective-permute-start | bytes 589832 | tf_op jit(solution)/shard_map/ppermute | solution.py:414
  32.1 1.5 collective-permute-start.7
  33.7 8.5 %forward_part.3 = (bf16[96,3584]{1,0:T(8,128)(2,1)}, f32[96,3584]{1,0:T(8,128)}) custom-call(s32[1]{0:T(128)} %bitcast.refs_0_, bf16[192,2048]{1,0:T(8,128)(2,1)} %copy-done, bf16[2048,3584]{1,0:T(8,128)(2,1)} %refs_10_.1, s32[32,56]{1,0:T(8,128)} %refs_2_.13), custom_call_target="tpu_custom_call" | custom-call | flops 1000 | bytes 1000 | tf_op jit(solution)/shard_map/forward_part/pallas_call | solution.py:145
  42.1 1.6 collective-permute-start.8
  44.6 1.7 collective-permute-done.5
  47.1 10.2 %hidden_part.1 = (bf16[96,2048]{1,0:T(8,128)(2,1)}, f32[96,2048]{1,0:T(8,128)}, bf16[96,1536]{1,0:T(8,128)(2,1)}, f32[96,1536]{1,0:T(8,128)}) custom-call(s32[1]{0:T(128)} %bitcast.refs_0_, bf16[192,2048]{1,0:T(8,128)(2,1)} %copy-done.7, bf16[3584,2048]{1,0:T(8,128)(2,1)} %refs_6_.1, s32[56,32]{1,0:T(8,128)} %copy.15.refs_3_), custom_call_target="tpu_custom_call" | custom-call | flops 1000 | bytes 1000 | tf_op jit(solution)/shard_map/hidden_part/pallas_call | solution.py:145
  59.6 1.6 collective-permute-start.10
  62.0 6.0 %collective-permute-done.12 = bf16[96,1536]{1,0:T(8,128)(2,1)S(1)} collective-permute-done((bf16[96,1536]{1,0:T(8,128)(2,1)}, bf16[96,1536]{1,0:T(8,128)(2,1)S(1)}, u32[]{:S(2)}, u32[]{:S(2)}) %collective-permute-start.12) | collective-permute-done | bytes 294944 | tf_op jit(solution)/shard_map/ppermute | solution.py:414
  68.1 1.6 collective-permute-start.13
  70.4 5.0 %collective-permute-done.10 = bf16[48,3584]{1,0:T(8,128)(2,1)S(1)} collective-permute-done((bf16[48,3584]{1,0:T(8,128)(2,1)S(1)}, bf16[48,3584]{1,0:T(8,128)(2,1)S(1)}, u32[]{:S(2)}, u32[]{:S(2)}) %collective-permute-start.10) | collective-permute-done | bytes 344096 | tf_op jit(solution)/shard_map/ppermute | solution.py:414
  75.4 1.5 collective-permute-done.11
  77.8 1.5 collective-permute-done.13
  80.2 4.2 %collective-permute-done.15 = bf16[48,1536]{1,0:T(8,128)(2,1)S(1)} collective-permute-done((bf16[48,1536]{1,0:T(8,128)(2,1)S(1)}, bf16[48,1536]{1,0:T(8,128)(2,1)S(1)}, u32[]{:S(2)}, u32[]{:S(2)}) %collective-permute-start.15) | collective-permute-done | bytes 147488 | tf_op jit(solution)/shard_map/ppermute | solution.py:414
  85.7 1.6 collective-permute-start.16
  87.3 1.5 collective-permute-start.17
  88.8 8.4 %collective-permute-done.17 = bf16[48,1536]{1,0:T(8,128)(2,1)S(1)} collective-permute-done((bf16[48,1536]{1,0:T(8,128)(2,1)S(1)}, bf16[48,1536]{1,0:T(8,128)(2,1)S(1)}, u32[]{:S(2)}, u32[]{:S(2)}) %collective-permute-start.17) | collective-permute-done | bytes 147488 | tf_op jit(solution)/shard_map/ppermute | solution.py:414
  98.7 1.5 collective-permute-start.20
  100.2 1.3 collective-permute-start.21
  101.5 16.0 %down_back.1 = (bf16[3584,2048]{1,0:T(8,128)(2,1)}, f32[96,2048]{1,0:T(8,128)}, f32[96,2048]{1,0:T(8,128)}) custom-call(s32[1]{0:T(128)} %bitcast.refs_0_, bf16[96,2048]{1,0:T(8,128)(2,1)} %copy-done.16, bf16[96,2048]{1,0:T(8,128)(2,1)} %copy-done.19, bf16[96,1536]{1,0:T(8,128)(2,1)} %copy-done.17, bf16[96,1536]{1,0:T(8,128)(2,1)} %copy-done.20, ...), custom_call_target="tpu_custom_call" | custom-call | flops 5637144576 | bytes 1000 | tf_op jit(solution)/shard_map/down_back/pallas_call | solution.py:145
  119.2 5.8 %weight_back.4 = (bf16[2048,3584]{1,0:T(8,128)(2,1)}, f32[8,128]{1,0:T(8,128)}) custom-call(s32[1]{0:T(128)} %bitcast.refs_0_, bf16[192,2048]{1,0:T(8,128)(2,1)} %copy-done, s32[32,56]{1,0:T(8,128)} %refs_11_.1, bf16[96,2048]{1,0:T(8,128)(2,1)} %copy-done.8, bf16[96,2048]{1,0:T(8,128)(2,1)} %copy-done.14), custom_call_target="tpu_custom_call" | custom-call | flops 1610612736 | bytes 1000 | tf_op jit(solution)/shard_map/weight_back/pallas_call | solution.py:145
  126.9 5.1 %weight_back.5 = (bf16[2048,3584]{1,0:T(8,128)(2,1)}, f32[8,128]{1,0:T(8,128)}) custom-call(s32[1]{0:T(128)} %bitcast.refs_0_, bf16[192,2048]{1,0:T(8,128)(2,1)} %copy-done, s32[32,56]{1,0:T(8,128)} %refs_11_.1, bf16[96,1536]{1,0:T(8,128)(2,1)} %copy-done.2, bf16[96,1536]{1,0:T(8,128)(2,1)} %copy-done.5, ...), custom_call_target="tpu_custom_call", output_to_operand_aliasing={{0}: (5, {})} | custom-call | flops 1207959552 | bytes 1000 | tf_op jit(solution)/shard_map/weight_back/pallas_call | solution.py:145
  136.0 16.2 %input_back.1 = (f32[96,2048]{1,0:T(8,128)}, f32[96,2048]{1,0:T(8,128)}) custom-call(s32[1]{0:T(128)} %bitcast.refs_0_, bf16[96,2048]{1,0:T(8,128)(2,1)} %copy-done.8, bf16[96,2048]{1,0:T(8,128)(2,1)} %copy-done.14, bf16[96,1536]{1,0:T(8,128)(2,1)} %copy-done.2, bf16[96,1536]{1,0:T(8,128)(2,1)} %copy-done.5, bf16[96,2048]{1,0:T(8,128)(2,1)} %copy-done.9, ...), custom_call_target="tpu_custom_call" | custom-call | flops 5637144576 | bytes 1000 | tf_op jit(solution)/shard_map/input_back/pallas_call | solution.py:145
  152.3 2.5 %collective-permute-done.29 = f32[96,2048]{1,0:T(8,128)S(1)} collective-permute-done((f32[96,2048]{1,0:T(8,128)}, f32[96,2048]{1,0:T(8,128)S(1)}, u32[]{:S(2)}, u32[]{:S(2)}) %collective-permute-start.29) | collective-permute-done | bytes 786464 | tf_op jit(solution)/shard_map/ppermute | solution.py:414
  156.0 1.8 %collective-permute-start.30 = (bf16[48,2048]{1,0:T(8,128)(2,1)S(1)}, bf16[48,2048]{1,0:T(8,128)(2,1)S(1)}, u32[]{:S(2)}, u32[]{:S(2)}) collective-permute-start(bf16[48,2048]{1,0:T(8,128)(2,1)S(1)} %slice.150), channel_id=1, source_target_pairs={{0,2},{1,3},{2,0},{3,1},{4,6},{5,7},{6,4},{7,5},{8,10},{9,11},{10,... | collective-permute-start | bytes 589832 | tf_op jit(solution)/shard_map/ppermute | solution.py:414
  158.5 5.8 %weight_back.6 = (bf16[2048,3584]{1,0:T(8,128)(2,1)}, f32[8,128]{1,0:T(8,128)}) custom-call(s32[1]{0:T(128)} %bitcast.refs_0_, bf16[192,2048]{1,0:T(8,128)(2,1)} %copy-done, s32[32,56]{1,0:T(8,128)} %refs_2_.13, bf16[96,2048]{1,0:T(8,128)(2,1)} %copy-done.9, bf16[96,2048]{1,0:T(8,128)(2,1)} %copy-done.15), custom_call_target="tpu_custom_call" | custom-call | flops 1610612736 | bytes 1000 | tf_op jit(solution)/shard_map/weight_back/pallas_call | solution.py:145
  165.4 5.1 %weight_back.7 = (bf16[2048,3584]{1,0:T(8,128)(2,1)}, f32[8,128]{1,0:T(8,128)}) custom-call(s32[1]{0:T(128)} %bitcast.refs_0_, bf16[192,2048]{1,0:T(8,128)(2,1)} %copy-done, s32[32,56]{1,0:T(8,128)} %refs_2_.13, bf16[96,1536]{1,0:T(8,128)(2,1)} %copy-done.1, bf16[96,1536]{1,0:T(8,128)(2,1)} %copy-done.6, ...), custom_call_target="tpu_custom_call", output_to_operand_aliasing={{0}: (5, {})} | custom-call | flops 1207959552 | bytes 1000 | tf_op jit(solution)/shard_map/weight_back/pallas_call | solution.py:145
  170.5 1.2 collective-permute-done.31
  (131 shorter events, 25.7 us)
Async XLA Ops:
  0.7 9.2 %collective-permute-start = (bf16[24,2048]{1,0:T(8,128)(2,1)}, bf16[24,2048]{1,0:T(8,128)(2,1)S(1)}, u32[]{:S(2)}, u32[]{:S(2)}) collective-permute-start(bf16[24,2048]{1,0:T(8,128)(2,1)} %param.8), channel_id=1, source_target_pairs={{0,4},{1,5},{2,6},{3,7},{4,0},{5,1},{6,2},{7,3},{8,12},{9,13},{10,... | collective-permute-start | bytes 294920 | tf_op jit(solution)/shard_map/ppermute | solution.py:414
  10.8 6.2 %collective-permute-start.1 = (bf16[48,2048]{1,0:T(8,128)(2,1)S(1)}, bf16[48,2048]{1,0:T(8,128)(2,1)S(1)}, u32[]{:S(2)}, u32[]{:S(2)}) collective-permute-start(bf16[48,2048]{1,0:T(8,128)(2,1)S(1)} %pad_maximum_fusion.1), channel_id=1, source_target_pairs={{0,2},{1,3},{2,0},{3,1},{4,6},{5,7},{6,4},{7,5},{8,10},{9,11},{10,... | collective-permute-start | bytes 589832 | tf_op jit(solution)/shard_map/ppermute | solution.py:414
  17.0 3.9 %collective-permute-start.2 = (bf16[96,2048]{1,0:T(8,128)(2,1)S(1)}, bf16[96,2048]{1,0:T(8,128)(2,1)S(1)}, u32[]{:S(2)}, u32[]{:S(2)}) collective-permute-start(bf16[96,2048]{1,0:T(8,128)(2,1)S(1)} %get-tuple-element.138), channel_id=1, source_target_pairs={{0,1},{1,0},{2,3},{3,2},{4,5},{5,4},{6,7},{7,6},{8,9},{9,8},{10,11... | collective-permute-start | bytes 1179656 | tf_op jit(solution)/shard_map/ppermute | solution.py:414
  17.8 12.5 %collective-permute-start.3 = (bf16[24,2048]{1,0:T(8,128)(2,1)S(1)}, bf16[24,2048]{1,0:T(8,128)(2,1)S(1)}, u32[]{:S(2)}, u32[]{:S(2)}) collective-permute-start(bf16[24,2048]{1,0:T(8,128)(2,1)S(1)} %copy-done.10), channel_id=1, source_target_pairs={{0,4},{1,5},{2,6},{3,7},{4,0},{5,1},{6,2},{7,3},{8,12},{9,13},{10,... | collective-permute-start | bytes 294920 | tf_op jit(solution)/shard_map/ppermute | solution.py:414
  30.3 14.1 %collective-permute-start.4 = (bf16[48,2048]{1,0:T(8,128)(2,1)S(1)}, bf16[48,2048]{1,0:T(8,128)(2,1)S(1)}, u32[]{:S(2)}, u32[]{:S(2)}) collective-permute-start(bf16[48,2048]{1,0:T(8,128)(2,1)S(1)} %pad_maximum_fusion.2), channel_id=1, source_target_pairs={{0,2},{1,3},{2,0},{3,1},{4,6},{5,7},{6,4},{7,5},{8,10},{9,11},{10,... | collective-permute-start | bytes 589832 | tf_op jit(solution)/shard_map/ppermute | solution.py:414
  32.1 26.3 %collective-permute-start.7 = (bf16[96,3584]{1,0:T(8,128)(2,1)}, bf16[96,3584]{1,0:T(8,128)(2,1)S(1)}, u32[]{:S(2)}, u32[]{:S(2)}) collective-permute-start(bf16[96,3584]{1,0:T(8,128)(2,1)} %get-tuple-element.68), channel_id=1, source_target_pairs={{0,8},{8,0},{16,24},{24,16},{1,9},{9,1},{17,25},{25,17},{2,10},{10... | collective-permute-start | bytes 2064392 | tf_op jit(solution)/shard_map/ppermute | solution.py:414
  42.1 17.3 %collective-permute-start.8 = (bf16[96,3584]{1,0:T(8,128)(2,1)}, bf16[96,3584]{1,0:T(8,128)(2,1)S(1)}, u32[]{:S(2)}, u32[]{:S(2)}) collective-permute-start(bf16[96,3584]{1,0:T(8,128)(2,1)} %get-tuple-element.70), channel_id=1, source_target_pairs={{0,16},{8,24},{16,0},{24,8},{1,17},{9,25},{17,1},{25,9},{2,18},{10... | collective-permute-start | bytes 2064392 | tf_op jit(solution)/shard_map/ppermute | solution.py:414
  44.4 1.8 %collective-permute-start.5 = (bf16[96,2048]{1,0:T(8,128)(2,1)S(1)}, bf16[96,2048]{1,0:T(8,128)(2,1)S(1)}, u32[]{:S(2)}, u32[]{:S(2)}) collective-permute-start(bf16[96,2048]{1,0:T(8,128)(2,1)S(1)} %pad_maximum_fusion), channel_id=1, source_target_pairs={{0,1},{1,0},{2,3},{3,2},{4,5},{5,4},{6,7},{7,6},{8,9},{9,8},{10,11... | collective-permute-start | bytes 1179656 | tf_op jit(solution)/shard_map/ppermute | solution.py:414
  57.3 12.3 %collective-permute-start.6 = (bf16[96,2048]{1,0:T(8,128)(2,1)}, bf16[96,2048]{1,0:T(8,128)(2,1)S(1)}, u32[]{:S(2)}, u32[]{:S(2)}) collective-permute-start(bf16[96,2048]{1,0:T(8,128)(2,1)} %get-tuple-element.77), channel_id=1, source_target_pairs={{0,8},{8,0},{16,24},{24,16},{1,9},{9,1},{17,25},{25,17},{2,10},{10... | collective-permute-start | bytes 1179656 | tf_op jit(solution)/shard_map/ppermute | solution.py:414
  57.9 10.1 %collective-permute-start.12 = (bf16[96,1536]{1,0:T(8,128)(2,1)}, bf16[96,1536]{1,0:T(8,128)(2,1)S(1)}, u32[]{:S(2)}, u32[]{:S(2)}) collective-permute-start(bf16[96,1536]{1,0:T(8,128)(2,1)} %get-tuple-element.88), channel_id=1, source_target_pairs={{0,16},{8,24},{16,0},{24,8},{1,17},{9,25},{17,1},{25,9},{2,18},{10... | collective-permute-start | bytes 884744 | tf_op jit(solution)/shard_map/ppermute | solution.py:414
  59.6 15.8 %collective-permute-start.10 = (bf16[48,3584]{1,0:T(8,128)(2,1)S(1)}, bf16[48,3584]{1,0:T(8,128)(2,1)S(1)}, u32[]{:S(2)}, u32[]{:S(2)}) collective-permute-start(bf16[48,3584]{1,0:T(8,128)(2,1)S(1)} %slice.149), channel_id=1, source_target_pairs={{0,16},{8,24},{16,0},{24,8},{1,17},{9,25},{17,1},{25,9},{2,18},{10... | collective-permute-start | bytes 1032200 | tf_op jit(solution)/shard_map/ppermute | solution.py:414
  61.4 15.5 %collective-permute-start.11 = (bf16[48,3584]{1,0:T(8,128)(2,1)S(1)}, bf16[48,3584]{1,0:T(8,128)(2,1)S(1)}, u32[]{:S(2)}, u32[]{:S(2)}) collective-permute-start(bf16[48,3584]{1,0:T(8,128)(2,1)S(1)} %slice.148), channel_id=1, source_target_pairs={{0,8},{8,0},{16,24},{24,16},{1,9},{9,1},{17,25},{25,17},{2,10},{10... | collective-permute-start | bytes 1032200 | tf_op jit(solution)/shard_map/ppermute | solution.py:414
  68.1 11.2 %collective-permute-start.13 = (bf16[48,1536]{1,0:T(8,128)(2,1)S(1)}, bf16[48,1536]{1,0:T(8,128)(2,1)S(1)}, u32[]{:S(2)}, u32[]{:S(2)}) collective-permute-start(bf16[48,1536]{1,0:T(8,128)(2,1)S(1)} %slice.153), channel_id=1, source_target_pairs={{0,8},{8,0},{16,24},{24,16},{1,9},{9,1},{17,25},{25,17},{2,10},{10... | collective-permute-start | bytes 442376 | tf_op jit(solution)/shard_map/ppermute | solution.py:414
  69.8 10.2 %collective-permute-start.9 = (bf16[48,2048]{1,0:T(8,128)(2,1)S(1)}, bf16[48,2048]{1,0:T(8,128)(2,1)S(1)}, u32[]{:S(2)}, u32[]{:S(2)}) collective-permute-start(bf16[48,2048]{1,0:T(8,128)(2,1)S(1)} %slice.152), channel_id=1, source_target_pairs={{0,16},{8,24},{16,0},{24,8},{1,17},{9,25},{17,1},{25,9},{2,18},{10... | collective-permute-start | bytes 589832 | tf_op jit(solution)/shard_map/ppermute | solution.py:414
  77.2 7.2 %collective-permute-start.14 = (bf16[48,2048]{1,0:T(8,128)(2,1)S(1)}, bf16[48,2048]{1,0:T(8,128)(2,1)S(1)}, u32[]{:S(2)}, u32[]{:S(2)}) collective-permute-start(bf16[48,2048]{1,0:T(8,128)(2,1)S(1)} %slice.102), channel_id=1, source_target_pairs={{0,16},{8,24},{16,0},{24,8},{1,17},{9,25},{17,1},{25,9},{2,18},{10... | collective-permute-start | bytes 589832 | tf_op jit(solution)/shard_map/ppermute | solution.py:414
  79.3 5.1 %collective-permute-start.15 = (bf16[48,1536]{1,0:T(8,128)(2,1)S(1)}, bf16[48,1536]{1,0:T(8,128)(2,1)S(1)}, u32[]{:S(2)}, u32[]{:S(2)}) collective-permute-start(bf16[48,1536]{1,0:T(8,128)(2,1)S(1)} %slice.103), channel_id=1, source_target_pairs={{0,8},{8,0},{16,24},{24,16},{1,9},{9,1},{17,25},{25,17},{2,10},{10... | collective-permute-start | bytes 442376 | tf_op jit(solution)/shard_map/ppermute | solution.py:414
  84.5 12.7 %collective-permute-start.18 = (bf16[96,2048]{1,0:T(8,128)(2,1)S(1)}, bf16[96,2048]{1,0:T(8,128)(2,1)S(1)}, u32[]{:S(2)}, u32[]{:S(2)}) collective-permute-start(bf16[96,2048]{1,0:T(8,128)(2,1)S(1)} %constant_dynamic-update-slice_fusion.11.refs_1_), channel_id=1, source_target_pairs={{0,8},{8,0},{16,24},{24,16},{1,9},{9,1},{17,25},{25,17},{2,10},{10... | collective-permute-start | bytes 1179656 | tf_op jit(solution)/shard_map/ppermute | solution.py:414
  85.1 12.1 %collective-permute-start.19 = (bf16[96,1536]{1,0:T(8,128)(2,1)S(1)}, bf16[96,1536]{1,0:T(8,128)(2,1)S(1)}, u32[]{:S(2)}, u32[]{:S(2)}) collective-permute-start(bf16[96,1536]{1,0:T(8,128)(2,1)S(1)} %constant_dynamic-update-slice_fusion.13.refs_3_), channel_id=1, source_target_pairs={{0,16},{8,24},{16,0},{24,8},{1,17},{9,25},{17,1},{25,9},{2,18},{10... | collective-permute-start | bytes 884744 | tf_op jit(solution)/shard_map/ppermute | solution.py:414
  85.7 11.5 %collective-permute-start.16 = (bf16[48,2048]{1,0:T(8,128)(2,1)S(1)}, bf16[48,2048]{1,0:T(8,128)(2,1)S(1)}, u32[]{:S(2)}, u32[]{:S(2)}) collective-permute-start(bf16[48,2048]{1,0:T(8,128)(2,1)S(1)} %get-tuple-element.96), channel_id=1, source_target_pairs={{0,16},{8,24},{16,0},{24,8},{1,17},{9,25},{17,1},{25,9},{2,18},{10... | collective-permute-start | bytes 589832 | tf_op jit(solution)/shard_map/ppermute | solution.py:414
  87.3 9.9 %collective-permute-start.17 = (bf16[48,1536]{1,0:T(8,128)(2,1)S(1)}, bf16[48,1536]{1,0:T(8,128)(2,1)S(1)}, u32[]{:S(2)}, u32[]{:S(2)}) collective-permute-start(bf16[48,1536]{1,0:T(8,128)(2,1)S(1)} %get-tuple-element.97), channel_id=1, source_target_pairs={{0,8},{8,0},{16,24},{24,16},{1,9},{9,1},{17,25},{25,17},{2,10},{10... | collective-permute-start | bytes 442376 | tf_op jit(solution)/shard_map/ppermute | solution.py:414
  97.2 21.2 %collective-permute-start.23 = (bf16[96,2048]{1,0:T(8,128)(2,1)S(1)}, bf16[96,2048]{1,0:T(8,128)(2,1)S(1)}, u32[]{:S(2)}, u32[]{:S(2)}) collective-permute-start(bf16[96,2048]{1,0:T(8,128)(2,1)S(1)} %constant_dynamic-update-slice_fusion.15.refs_3_.refs_1_), channel_id=1, source_target_pairs={{0,8},{8,0},{16,24},{24,16},{1,9},{9,1},{17,25},{25,17},{2,10},{10... | collective-permute-start | bytes 1179656 | tf_op jit(solution)/shard_map/ppermute | solution.py:414
  98.1 28.1 %collective-permute-start.25 = (bf16[96,1536]{1,0:T(8,128)(2,1)S(1)}, bf16[96,1536]{1,0:T(8,128)(2,1)S(1)}, u32[]{:S(2)}, u32[]{:S(2)}) collective-permute-start(bf16[96,1536]{1,0:T(8,128)(2,1)S(1)} %constant_dynamic-update-slice_fusion.17.refs_3_), channel_id=1, source_target_pairs={{0,16},{8,24},{16,0},{24,8},{1,17},{9,25},{17,1},{25,9},{2,18},{10... | collective-permute-start | bytes 884744 | tf_op jit(solution)/shard_map/ppermute | solution.py:414
  98.7 18.8 %collective-permute-start.20 = (bf16[48,2048]{1,0:T(8,128)(2,1)S(1)}, bf16[48,2048]{1,0:T(8,128)(2,1)S(1)}, u32[]{:S(2)}, u32[]{:S(2)}) collective-permute-start(bf16[48,2048]{1,0:T(8,128)(2,1)S(1)} %get-tuple-element.102), channel_id=1, source_target_pairs={{0,16},{8,24},{16,0},{24,8},{1,17},{9,25},{17,1},{25,9},{2,18},{10... | collective-permute-start | bytes 589832 | tf_op jit(solution)/shard_map/ppermute | solution.py:414
  100.2 17.3 %collective-permute-start.21 = (bf16[48,1536]{1,0:T(8,128)(2,1)S(1)}, bf16[48,1536]{1,0:T(8,128)(2,1)S(1)}, u32[]{:S(2)}, u32[]{:S(2)}) collective-permute-start(bf16[48,1536]{1,0:T(8,128)(2,1)S(1)} %get-tuple-element.103), channel_id=1, source_target_pairs={{0,8},{8,0},{16,24},{24,16},{1,9},{9,1},{17,25},{25,17},{2,10},{10... | collective-permute-start | bytes 442376 | tf_op jit(solution)/shard_map/ppermute | solution.py:414
  117.5 7.6 %collective-permute-start.22 = (f32[96,2048]{1,0:T(8,128)}, f32[96,2048]{1,0:T(8,128)S(1)}, u32[]{:S(2)}, u32[]{:S(2)}) collective-permute-start(f32[96,2048]{1,0:T(8,128)} %get-tuple-element.105), channel_id=1, source_target_pairs={{0,1},{1,0},{2,3},{3,2},{4,5},{5,4},{6,7},{7,6},{8,9},{9,8},{10,11... | collective-permute-start | bytes 2359304 | tf_op jit(solution)/shard_map/ppermute | solution.py:414
  117.6 16.9 %collective-permute-start.27 = (bf16[96,2048]{1,0:T(8,128)(2,1)S(1)}, bf16[96,2048]{1,0:T(8,128)(2,1)S(1)}, u32[]{:S(2)}, u32[]{:S(2)}) collective-permute-start(bf16[96,2048]{1,0:T(8,128)(2,1)S(1)} %constant_dynamic-update-slice_fusion.19.refs_5_.refs_3_), channel_id=1, source_target_pairs={{0,8},{8,0},{16,24},{24,16},{1,9},{9,1},{17,25},{25,17},{2,10},{10... | collective-permute-start | bytes 1179656 | tf_op jit(solution)/shard_map/ppermute | solution.py:414
  125.2 7.1 %collective-permute-start.24 = (bf16[48,2048]{1,0:T(8,128)(2,1)S(1)}, bf16[48,2048]{1,0:T(8,128)(2,1)S(1)}, u32[]{:S(2)}, u32[]{:S(2)}) collective-permute-start(bf16[48,2048]{1,0:T(8,128)(2,1)S(1)} %slice.151), channel_id=1, source_target_pairs={{0,2},{1,3},{2,0},{3,1},{4,6},{5,7},{6,4},{7,5},{8,10},{9,11},{10,... | collective-permute-start | bytes 589832 | tf_op jit(solution)/shard_map/ppermute | solution.py:414
  125.6 8.9 %collective-permute-start.28 = (bf16[96,1536]{1,0:T(8,128)(2,1)S(1)}, bf16[96,1536]{1,0:T(8,128)(2,1)S(1)}, u32[]{:S(2)}, u32[]{:S(2)}) collective-permute-start(bf16[96,1536]{1,0:T(8,128)(2,1)S(1)} %constant_dynamic-update-slice_fusion.21.refs_7_.refs_3_), channel_id=1, source_target_pairs={{0,16},{8,24},{16,0},{24,8},{1,17},{9,25},{17,1},{25,9},{2,18},{10... | collective-permute-start | bytes 884744 | tf_op jit(solution)/shard_map/ppermute | solution.py:414
  132.4 19.8 %collective-permute-start.26 = (bf16[24,2048]{1,0:T(8,128)(2,1)S(1)}, bf16[24,2048]{1,0:T(8,128)(2,1)S(1)}, u32[]{:S(2)}, u32[]{:S(2)}) collective-permute-start(bf16[24,2048]{1,0:T(8,128)(2,1)S(1)} %slice.155), channel_id=1, source_target_pairs={{0,4},{1,5},{2,6},{3,7},{4,0},{5,1},{6,2},{7,3},{8,12},{9,13},{10,... | collective-permute-start | bytes 294920 | tf_op jit(solution)/shard_map/ppermute | solution.py:414
  152.2 2.6 %collective-permute-start.29 = (f32[96,2048]{1,0:T(8,128)}, f32[96,2048]{1,0:T(8,128)S(1)}, u32[]{:S(2)}, u32[]{:S(2)}) collective-permute-start(f32[96,2048]{1,0:T(8,128)} %get-tuple-element.121), channel_id=1, source_target_pairs={{0,1},{1,0},{2,3},{3,2},{4,5},{5,4},{6,7},{7,6},{8,9},{9,8},{10,11... | collective-permute-start | bytes 2359304 | tf_op jit(solution)/shard_map/ppermute | solution.py:414
  156.0 8.3 %collective-permute-start.30 = (bf16[48,2048]{1,0:T(8,128)(2,1)S(1)}, bf16[48,2048]{1,0:T(8,128)(2,1)S(1)}, u32[]{:S(2)}, u32[]{:S(2)}) collective-permute-start(bf16[48,2048]{1,0:T(8,128)(2,1)S(1)} %slice.150), channel_id=1, source_target_pairs={{0,2},{1,3},{2,0},{3,1},{4,6},{5,7},{6,4},{7,5},{8,10},{9,11},{10,... | collective-permute-start | bytes 589832 | tf_op jit(solution)/shard_map/ppermute | solution.py:414
  164.4 7.4 %collective-permute-start.31 = (bf16[24,2048]{1,0:T(8,128)(2,1)S(1)}, bf16[24,2048]{1,0:T(8,128)(2,1)S(1)}, u32[]{:S(2)}, u32[]{:S(2)}) collective-permute-start(bf16[24,2048]{1,0:T(8,128)(2,1)S(1)} %slice.154), channel_id=1, source_target_pairs={{0,4},{1,5},{2,6},{3,7},{4,0},{5,1},{6,2},{7,3},{8,12},{9,13},{10,... | collective-permute-start | bytes 294920 | tf_op jit(solution)/shard_map/ppermute | solution.py:414
  (21 other events, 170.3 us)

commit v5 on v3

--- a/solution.py
+++ b/solution.py
@@ -9,7 +9,7 @@
 
 BF16 = jnp.bfloat16
 F32 = jnp.float32
-VMEM_LIMIT = 56 * 1024 * 1024
+MIB = 1024 * 1024
 NT = (((1,), (1,)), ((), ()))
 
 
@@ -123,7 +123,7 @@
         send[rows, at] = part[sent[slot] * quarter : (sent[slot] + 1) * quarter, :].astype(BF16)
 
 
-def call(body, name, inputs, kinds, outs, out_kinds, scratch, steps=None, maps=None, aliases={}, macs=500, marks=()):
+def call(body, name, inputs, kinds, outs, out_kinds, scratch, steps=None, maps=None, aliases={}, macs=500, marks=(), mib=56):
     spec = {
         "s": pl.BlockSpec(memory_space=pltpu.SMEM),
         "v": pl.BlockSpec(memory_space=pltpu.VMEM),
@@ -142,7 +142,7 @@
         out_shape=outs,
         scratch_shapes=scratch,
         input_output_aliases=aliases,
-        compiler_params=pltpu.CompilerParams(vmem_limit_bytes=VMEM_LIMIT),
+        compiler_params=pltpu.CompilerParams(vmem_limit_bytes=mib * MIB),
         cost_estimate=pl.CostEstimate(flops=2 * macs, bytes_accessed=1000, transcendentals=0),
         name=name,
         **grid,
@@ -193,6 +193,7 @@
         ],
         steps,
         [pl.BlockSpec((total // 2, tile), lambda i: (0, i))] * 2,
+        mib=32,
     )
 
 
@@ -241,6 +242,7 @@
         steps,
         [pl.BlockSpec((total // 2, tile), lambda i: (0, jnp.minimum(i, front - 1)))] * 2
         + [pl.BlockSpec((total // 2, tile), lambda i: (0, jnp.maximum(i - front, 0)))] * 2,
+        mib=32,
     )
 
 
@@ -294,6 +296,7 @@
             pltpu.SemaphoreType.DMA((slots,)),
         ],
         macs=2 * total * depth * width,
+        mib=44,
     )
 
 
@@ -341,6 +344,7 @@
         [pl.BlockSpec((total // 2, tile), lambda i: (0, i))] * 2,
         macs=2 * total * depth * width,
         marks=marks,
+        mib=50,
     )
 
 
@@ -397,6 +401,7 @@
         aliases={3 + len(pieces): 0} if known else {},
         macs=total * depth * (right - left),
         marks=marks,
+        mib=26,
     )
 
 

time: 172 us -> 164 us (0.953)
  Pallas kernels: 80.3 us -> 61.7 us
  local copies, waits for them, and re-layouts: 7.61 us -> 14.1 us
  other arithmetic: 4.72 us -> 7.03 us
  starting transfers between devices: 33.9 us -> 36 us
    pallas_call x9, Pallas kernels: 80.3 us -> 61.7 us  [call(): pl.pallas_call(unmarked, in_specs=[spec[kind] for kind in (*kinds, *'h' *...]
    unnamed x54 -> x34, local copies, waits for them, and re-layouts: 6.55 us -> 13.6 us
    ppermute x32, starting transfers between devices: 33.9 us -> 36 us  [swap(): return lax.ppermute(value, axis, [(i, i ^ bit) for i in range(size)])]
  transfers between devices with their start and end apart: 32 -> 32, of which waited for: 14 -> 14; matrix products, arithmetic and copies ran while one was open for 3% -> 3% of each run, Pallas kernels for 47% -> 38%
where the time goes in v5:
time: 164 us
  Pallas kernels  61.7 us (38%)
  waiting for transfers between devices  43.5 us (27%)
  starting transfers between devices  36 us (22%)
  local copies, waits for them, and re-layouts  14.1 us (9%)
  other arithmetic  7.03 us (4%)
    pallas_call x9, Pallas kernels, call(): pl.pallas_call(unmarked, in_specs=[spec[kind] for kind in (*kinds, *'h' *...  61.7 us
    ppermute x32, waiting for transfers between devices, swap(): return lax.ppermute(value, axis, [(i, i ^ bit) for i in range(size)])  43.5 us
    ppermute x32, starting transfers between devices, swap(): return lax.ppermute(value, axis, [(i, i ^ bit) for i in range(size)])  36 us
    unnamed x34, local copies, waits for them, and re-layouts  13.6 us
  transfers between devices with their start and end apart: 32, of which 14 were waited for; matrix products, arithmetic and copies ran while one was open for 3% of the time, Pallas kernels for 38%

profile of v5, /device:TPU:0, one launch (start us, length us, event | category | flops | bytes accessed | tf_op | source)
XLA Modules:
  0.0 163.5 jit_solution(5133114163290225121)
XLA Ops:
  0.7 4.1 %collective-permute-start = (bf16[24,2048]{1,0:T(8,128)(2,1)}, bf16[24,2048]{1,0:T(8,128)(2,1)S(1)}, u32[]{:S(2)}, u32[]{:S(2)}) collective-permute-start(bf16[24,2048]{1,0:T(8,128)(2,1)} %param.8), channel_id=1, source_target_pairs={{0,4},{1,5},{2,6},{3,7},{4,0},{5,1},{6,2},{7,3},{8,12},{9,13},{10,... | collective-permute-start | bytes 294920 | tf_op jit(solution)/shard_map/ppermute | solution.py:409
  5.7 4.2 %collective-permute-done = bf16[24,2048]{1,0:T(8,128)(2,1)S(1)} collective-permute-done((bf16[24,2048]{1,0:T(8,128)(2,1)}, bf16[24,2048]{1,0:T(8,128)(2,1)S(1)}, u32[]{:S(2)}, u32[]{:S(2)}) %collective-permute-start) | collective-permute-done | bytes 98336 | tf_op jit(solution)/shard_map/ppermute | solution.py:409
  11.7 5.2 %collective-permute-done.1 = bf16[48,2048]{1,0:T(8,128)(2,1)S(1)} collective-permute-done((bf16[48,2048]{1,0:T(8,128)(2,1)S(1)}, bf16[48,2048]{1,0:T(8,128)(2,1)S(1)}, u32[]{:S(2)}, u32[]{:S(2)}) %collective-permute-start.1) | collective-permute-done | bytes 196640 | tf_op jit(solution)/shard_map/ppermute | solution.py:409
  17.2 3.2 %collective-permute-start.3 = (bf16[24,2048]{1,0:T(8,128)(2,1)S(1)}, bf16[24,2048]{1,0:T(8,128)(2,1)S(1)}, u32[]{:S(2)}, u32[]{:S(2)}) collective-permute-start(bf16[24,2048]{1,0:T(8,128)(2,1)S(1)} %copy-done.9), channel_id=1, source_target_pairs={{0,4},{1,5},{2,6},{3,7},{4,0},{5,1},{6,2},{7,3},{8,12},{9,13},{10,... | collective-permute-start | bytes 294920 | tf_op jit(solution)/shard_map/ppermute | solution.py:409
  20.4 5.2 %copy-done = bf16[2048,3584]{1,0:T(8,128)(2,1)S(1)} copy-done((bf16[2048,3584]{1,0:T(8,128)(2,1)S(1)}, bf16[2048,3584]{1,0:T(8,128)(2,1)}, u32[]{:S(2)}) %copy-start) | copy-done | bytes 14680088
  25.5 5.6 %forward_part.2 = (bf16[96,3584]{1,0:T(8,128)(2,1)S(1)}, f32[96,3584]{1,0:T(8,128)S(1)}) custom-call(s32[1]{0:T(128)} %bitcast.refs_0_, bf16[192,2048]{1,0:T(8,128)(2,1)S(1)} %constant_dynamic-update-slice_fusion.3.refs_1_, bf16[2048,3584]{1,0:T(8,128)(2,1)S(1)} %copy-done, s32[32,56]{1,0:T(8,128)S(1)} %copy-done.7), custom_call_target="tpu_custom_call" | custom-call | flops 1000 | bytes 1000 | tf_op jit(solution)/shard_map/forward_part/pallas_call | solution.py:138
  32.3 1.8 %collective-permute-start.4 = (bf16[48,2048]{1,0:T(8,128)(2,1)S(1)}, bf16[48,2048]{1,0:T(8,128)(2,1)S(1)}, u32[]{:S(2)}, u32[]{:S(2)}) collective-permute-start(bf16[48,2048]{1,0:T(8,128)(2,1)S(1)} %pad_maximum_fusion.2), channel_id=1, source_target_pairs={{0,2},{1,3},{2,0},{3,1},{4,6},{5,7},{6,4},{7,5},{8,10},{9,11},{10,... | collective-permute-start | bytes 589832 | tf_op jit(solution)/shard_map/ppermute | solution.py:409
  34.1 1.5 collective-permute-start.7
  35.6 6.2 %forward_part.3 = (bf16[96,3584]{1,0:T(8,128)(2,1)}, f32[96,3584]{1,0:T(8,128)S(1)}) custom-call(s32[1]{0:T(128)} %bitcast.refs_0_, bf16[192,2048]{1,0:T(8,128)(2,1)S(1)} %constant_dynamic-update-slice_fusion.3.refs_1_, bf16[2048,3584]{1,0:T(8,128)(2,1)S(1)} %copy-done.1, s32[32,56]{1,0:T(8,128)S(1)} %copy-done.8), custom_call_target="tpu_custom_call" | custom-call | flops 1000 | bytes 1000 | tf_op jit(solution)/shard_map/forward_part/pallas_call | solution.py:138
  44.7 1.7 %collective-permute-done.5 = bf16[96,2048]{1,0:T(8,128)(2,1)S(1)} collective-permute-done((bf16[96,2048]{1,0:T(8,128)(2,1)S(1)}, bf16[96,2048]{1,0:T(8,128)(2,1)S(1)}, u32[]{:S(2)}, u32[]{:S(2)}) %collective-permute-start.5) | collective-permute-done | bytes 393248 | tf_op jit(solution)/shard_map/ppermute | solution.py:409
  46.4 5.2 %copy-done.2 = bf16[3584,2048]{1,0:T(8,128)(2,1)S(1)} copy-done((bf16[3584,2048]{1,0:T(8,128)(2,1)S(1)}, bf16[3584,2048]{1,0:T(8,128)(2,1)}, u32[]{:S(2)}) %copy-start.2) | copy-done | bytes 14680088
  51.6 7.9 %hidden_part.1 = (bf16[96,2048]{1,0:T(8,128)(2,1)S(1)}, f32[96,2048]{1,0:T(8,128)S(1)}, bf16[96,1536]{1,0:T(8,128)(2,1)S(1)}, f32[96,1536]{1,0:T(8,128)S(1)}) custom-call(s32[1]{0:T(128)} %bitcast.refs_0_, bf16[192,2048]{1,0:T(8,128)(2,1)S(1)} %constant_dynamic-update-slice_fusion.7.refs_1_.refs_5_, bf16[3584,2048]{1,0:T(8,128)(2,1)S(1)} %copy-done.2, ...), custom_call_target="tpu_custom_call" | custom-call | flops 1000 | bytes 1000 | tf_op jit(solution)/shard_map/hidden_part/pallas_call | solution.py:138
  62.0 1.6 collective-permute-start.10
  64.9 1.5 collective-permute-start.11
  66.4 3.5 %collective-permute-done.12 = bf16[96,1536]{1,0:T(8,128)(2,1)S(1)} collective-permute-done((bf16[96,1536]{1,0:T(8,128)(2,1)S(1)}, bf16[96,1536]{1,0:T(8,128)(2,1)S(1)}, u32[]{:S(2)}, u32[]{:S(2)}) %collective-permute-start.12) | collective-permute-done | bytes 294944 | tf_op jit(solution)/shard_map/ppermute | solution.py:409
  70.0 1.5 collective-permute-start.13
  72.3 5.1 %collective-permute-done.10 = bf16[48,3584]{1,0:T(8,128)(2,1)S(1)} collective-permute-done((bf16[48,3584]{1,0:T(8,128)(2,1)S(1)}, bf16[48,3584]{1,0:T(8,128)(2,1)S(1)}, u32[]{:S(2)}, u32[]{:S(2)}) %collective-permute-start.10) | collective-permute-done | bytes 344096 | tf_op jit(solution)/shard_map/ppermute | solution.py:409
  82.2 4.2 %collective-permute-done.15 = bf16[48,1536]{1,0:T(8,128)(2,1)S(1)} collective-permute-done((bf16[48,1536]{1,0:T(8,128)(2,1)S(1)}, bf16[48,1536]{1,0:T(8,128)(2,1)S(1)}, u32[]{:S(2)}, u32[]{:S(2)}) %collective-permute-start.15) | collective-permute-done | bytes 147488 | tf_op jit(solution)/shard_map/ppermute | solution.py:409
  87.6 1.6 collective-permute-start.16
  90.7 8.4 %collective-permute-done.17 = bf16[48,1536]{1,0:T(8,128)(2,1)S(1)} collective-permute-done((bf16[48,1536]{1,0:T(8,128)(2,1)S(1)}, bf16[48,1536]{1,0:T(8,128)(2,1)S(1)}, u32[]{:S(2)}, u32[]{:S(2)}) %collective-permute-start.17) | collective-permute-done | bytes 147488 | tf_op jit(solution)/shard_map/ppermute | solution.py:409
  103.3 13.2 %down_back.1 = (bf16[3584,2048]{1,0:T(8,128)(2,1)}, f32[96,2048]{1,0:T(8,128)S(1)}, f32[96,2048]{1,0:T(8,128)S(1)}) custom-call(s32[1]{0:T(128)} %bitcast.refs_0_, bf16[96,2048]{1,0:T(8,128)(2,1)S(1)} %constant_dynamic-update-slice_fusion.11.refs_1_, bf16[96,2048]{1,0:T(8,128)(2,1)S(1)} %collective-permute-done.18.refs_2_, ...), custom_call_target="tpu_custom_call" | custom-call | flops 5637144576 | bytes 1000 | tf_op jit(solution)/shard_map/down_back/pallas_call | solution.py:138
  117.5 3.9 %weight_back.4 = (bf16[2048,3584]{1,0:T(8,128)(2,1)}, f32[8,128]{1,0:T(8,128)S(1)}) custom-call(s32[1]{0:T(128)} %bitcast.refs_0_, bf16[192,2048]{1,0:T(8,128)(2,1)S(1)} %constant_dynamic-update-slice_fusion.3.refs_1_, s32[32,56]{1,0:T(8,128)S(1)} %copy-done.7, bf16[96,2048]{1,0:T(8,128)(2,1)S(1)} %constant_dynamic-update-slice_fusion.15.refs_3_.refs_1_, ...), custom_call_target="tpu_custom_call" | custom-call | flops 1610612736 | bytes 1000 | tf_op jit(solution)/shard_map/weight_back/pallas_call | solution.py:138
  122.5 3.2 %weight_back.5 = (bf16[2048,3584]{1,0:T(8,128)(2,1)}, f32[8,128]{1,0:T(8,128)S(1)}) custom-call(s32[1]{0:T(128)} %bitcast.refs_0_, bf16[192,2048]{1,0:T(8,128)(2,1)S(1)} %constant_dynamic-update-slice_fusion.3.refs_1_, s32[32,56]{1,0:T(8,128)S(1)} %copy-done.7, ...), custom_call_target="tpu_custom_call", output_to_operand_aliasing={{0}: (5, {})} | custom-call | flops 1207959552 | bytes 1000 | tf_op jit(solution)/shard_map/weight_back/pallas_call | solution.py:138
  125.7 3.0 %collective-permute-done.24 = bf16[48,2048]{1,0:T(8,128)(2,1)S(1)} collective-permute-done((bf16[48,2048]{1,0:T(8,128)(2,1)S(1)}, bf16[48,2048]{1,0:T(8,128)(2,1)S(1)}, u32[]{:S(2)}, u32[]{:S(2)}) %collective-permute-start.24) | collective-permute-done | bytes 196640 | tf_op jit(solution)/shard_map/ppermute | solution.py:409
  128.7 1.6 collective-permute-start.26
  130.8 14.1 %input_back.1 = (f32[96,2048]{1,0:T(8,128)S(1)}, f32[96,2048]{1,0:T(8,128)}) custom-call(s32[1]{0:T(128)} %bitcast.refs_0_, bf16[96,2048]{1,0:T(8,128)(2,1)S(1)} %constant_dynamic-update-slice_fusion.15.refs_3_.refs_1_, bf16[96,2048]{1,0:T(8,128)(2,1)S(1)} %collective-permute-done.23.refs_4_.refs_2_, ...), custom_call_target="tpu_custom_call" | custom-call | flops 5637144576 | bytes 1000 | tf_op jit(solution)/shard_map/input_back/pallas_call | solution.py:138
  145.0 2.3 %collective-permute-done.29 = f32[96,2048]{1,0:T(8,128)S(1)} collective-permute-done((f32[96,2048]{1,0:T(8,128)S(1)}, f32[96,2048]{1,0:T(8,128)S(1)}, u32[]{:S(2)}, u32[]{:S(2)}) %collective-permute-start.29) | collective-permute-done | bytes 786464 | tf_op jit(solution)/shard_map/ppermute | solution.py:409
  148.6 1.8 %collective-permute-start.30 = (bf16[48,2048]{1,0:T(8,128)(2,1)S(1)}, bf16[48,2048]{1,0:T(8,128)(2,1)S(1)}, u32[]{:S(2)}, u32[]{:S(2)}) collective-permute-start(bf16[48,2048]{1,0:T(8,128)(2,1)S(1)} %slice.150), channel_id=1, source_target_pairs={{0,2},{1,3},{2,0},{3,1},{4,6},{5,7},{6,4},{7,5},{8,10},{9,11},{10,... | collective-permute-start | bytes 589832 | tf_op jit(solution)/shard_map/ppermute | solution.py:409
  151.0 3.9 %weight_back.6 = (bf16[2048,3584]{1,0:T(8,128)(2,1)}, f32[8,128]{1,0:T(8,128)S(1)}) custom-call(s32[1]{0:T(128)} %bitcast.refs_0_, bf16[192,2048]{1,0:T(8,128)(2,1)S(1)} %constant_dynamic-update-slice_fusion.3.refs_1_, s32[32,56]{1,0:T(8,128)S(1)} %copy-done.8, bf16[96,2048]{1,0:T(8,128)(2,1)S(1)} %constant_dynamic-update-slice_fusion.19.refs_5_.refs_3_, ...), custom_call_target="tpu_custom_call" | custom-call | flops 1610612736 | bytes 1000 | tf_op jit(solution)/shard_map/weight_back/pallas_call | solution.py:138
  155.7 1.6 collective-permute-start.31
  157.3 3.8 %weight_back.7 = (bf16[2048,3584]{1,0:T(8,128)(2,1)}, f32[8,128]{1,0:T(8,128)}) custom-call(s32[1]{0:T(128)} %bitcast.refs_0_, bf16[192,2048]{1,0:T(8,128)(2,1)S(1)} %constant_dynamic-update-slice_fusion.3.refs_1_, s32[32,56]{1,0:T(8,128)S(1)} %copy-done.8, ...), custom_call_target="tpu_custom_call", output_to_operand_aliasing={{0}: (5, {})} | custom-call | flops 1207959552 | bytes 1000 | tf_op jit(solution)/shard_map/weight_back/pallas_call | solution.py:138
  161.0 1.8 %collective-permute-done.31 = bf16[24,2048]{1,0:T(8,128)(2,1)S(1)} collective-permute-done((bf16[24,2048]{1,0:T(8,128)(2,1)S(1)}, bf16[24,2048]{1,0:T(8,128)(2,1)S(1)}, u32[]{:S(2)}, u32[]{:S(2)}) %collective-permute-start.31) | collective-permute-done | bytes 98336 | tf_op jit(solution)/shard_map/ppermute | solution.py:409
  (111 shorter events, 29.1 us)
Async XLA Ops:
  0.7 9.2 %collective-permute-start = (bf16[24,2048]{1,0:T(8,128)(2,1)}, bf16[24,2048]{1,0:T(8,128)(2,1)S(1)}, u32[]{:S(2)}, u32[]{:S(2)}) collective-permute-start(bf16[24,2048]{1,0:T(8,128)(2,1)} %param.8), channel_id=1, source_target_pairs={{0,4},{1,5},{2,6},{3,7},{4,0},{5,1},{6,2},{7,3},{8,12},{9,13},{10,... | collective-permute-start | bytes 294920 | tf_op jit(solution)/shard_map/ppermute | solution.py:409
  10.8 6.2 %collective-permute-start.1 = (bf16[48,2048]{1,0:T(8,128)(2,1)S(1)}, bf16[48,2048]{1,0:T(8,128)(2,1)S(1)}, u32[]{:S(2)}, u32[]{:S(2)}) collective-permute-start(bf16[48,2048]{1,0:T(8,128)(2,1)S(1)} %pad_maximum_fusion.1), channel_id=1, source_target_pairs={{0,2},{1,3},{2,0},{3,1},{4,6},{5,7},{6,4},{7,5},{8,10},{9,11},{10,... | collective-permute-start | bytes 589832 | tf_op jit(solution)/shard_map/ppermute | solution.py:409
  17.0 3.3 %collective-permute-start.2 = (bf16[96,2048]{1,0:T(8,128)(2,1)S(1)}, bf16[96,2048]{1,0:T(8,128)(2,1)S(1)}, u32[]{:S(2)}, u32[]{:S(2)}) collective-permute-start(bf16[96,2048]{1,0:T(8,128)(2,1)S(1)} %get-tuple-element.138), channel_id=1, source_target_pairs={{0,1},{1,0},{2,3},{3,2},{4,5},{5,4},{6,7},{7,6},{8,9},{9,8},{10,11... | collective-permute-start | bytes 1179656 | tf_op jit(solution)/shard_map/ppermute | solution.py:409
  17.2 15.1 %collective-permute-start.3 = (bf16[24,2048]{1,0:T(8,128)(2,1)S(1)}, bf16[24,2048]{1,0:T(8,128)(2,1)S(1)}, u32[]{:S(2)}, u32[]{:S(2)}) collective-permute-start(bf16[24,2048]{1,0:T(8,128)(2,1)S(1)} %copy-done.9), channel_id=1, source_target_pairs={{0,4},{1,5},{2,6},{3,7},{4,0},{5,1},{6,2},{7,3},{8,12},{9,13},{10,... | collective-permute-start | bytes 294920 | tf_op jit(solution)/shard_map/ppermute | solution.py:409
  32.3 12.2 %collective-permute-start.4 = (bf16[48,2048]{1,0:T(8,128)(2,1)S(1)}, bf16[48,2048]{1,0:T(8,128)(2,1)S(1)}, u32[]{:S(2)}, u32[]{:S(2)}) collective-permute-start(bf16[48,2048]{1,0:T(8,128)(2,1)S(1)} %pad_maximum_fusion.2), channel_id=1, source_target_pairs={{0,2},{1,3},{2,0},{3,1},{4,6},{5,7},{6,4},{7,5},{8,10},{9,11},{10,... | collective-permute-start | bytes 589832 | tf_op jit(solution)/shard_map/ppermute | solution.py:409
  34.1 26.5 %collective-permute-start.7 = (bf16[96,3584]{1,0:T(8,128)(2,1)S(1)}, bf16[96,3584]{1,0:T(8,128)(2,1)}, u32[]{:S(2)}, u32[]{:S(2)}) collective-permute-start(bf16[96,3584]{1,0:T(8,128)(2,1)S(1)} %get-tuple-element.68), channel_id=1, source_target_pairs={{0,8},{8,0},{16,24},{24,16},{1,9},{9,1},{17,25},{25,17},{2,10},{10... | collective-permute-start | bytes 2064392 | tf_op jit(solution)/shard_map/ppermute | solution.py:409
  42.9 17.7 %collective-permute-start.8 = (bf16[96,3584]{1,0:T(8,128)(2,1)}, bf16[96,3584]{1,0:T(8,128)(2,1)}, u32[]{:S(2)}, u32[]{:S(2)}) collective-permute-start(bf16[96,3584]{1,0:T(8,128)(2,1)} %get-tuple-element.70), channel_id=1, source_target_pairs={{0,16},{8,24},{16,0},{24,8},{1,17},{9,25},{17,1},{25,9},{2,18},{10... | collective-permute-start | bytes 2064392 | tf_op jit(solution)/shard_map/ppermute | solution.py:409
  44.6 1.8 %collective-permute-start.5 = (bf16[96,2048]{1,0:T(8,128)(2,1)S(1)}, bf16[96,2048]{1,0:T(8,128)(2,1)S(1)}, u32[]{:S(2)}, u32[]{:S(2)}) collective-permute-start(bf16[96,2048]{1,0:T(8,128)(2,1)S(1)} %pad_maximum_fusion), channel_id=1, source_target_pairs={{0,1},{1,0},{2,3},{3,2},{4,5},{5,4},{6,7},{7,6},{8,9},{9,8},{10,11... | collective-permute-start | bytes 1179656 | tf_op jit(solution)/shard_map/ppermute | solution.py:409
  59.5 12.1 %collective-permute-start.6 = (bf16[96,2048]{1,0:T(8,128)(2,1)S(1)}, bf16[96,2048]{1,0:T(8,128)(2,1)S(1)}, u32[]{:S(2)}, u32[]{:S(2)}) collective-permute-start(bf16[96,2048]{1,0:T(8,128)(2,1)S(1)} %get-tuple-element.77), channel_id=1, source_target_pairs={{0,8},{8,0},{16,24},{24,16},{1,9},{9,1},{17,25},{25,17},{2,10},{10... | collective-permute-start | bytes 1179656 | tf_op jit(solution)/shard_map/ppermute | solution.py:409
  60.1 9.9 %collective-permute-start.12 = (bf16[96,1536]{1,0:T(8,128)(2,1)S(1)}, bf16[96,1536]{1,0:T(8,128)(2,1)S(1)}, u32[]{:S(2)}, u32[]{:S(2)}) collective-permute-start(bf16[96,1536]{1,0:T(8,128)(2,1)S(1)} %get-tuple-element.88), channel_id=1, source_target_pairs={{0,16},{8,24},{16,0},{24,8},{1,17},{9,25},{17,1},{25,9},{2,18},{10... | collective-permute-start | bytes 884744 | tf_op jit(solution)/shard_map/ppermute | solution.py:409
  62.0 15.3 %collective-permute-start.10 = (bf16[48,3584]{1,0:T(8,128)(2,1)S(1)}, bf16[48,3584]{1,0:T(8,128)(2,1)S(1)}, u32[]{:S(2)}, u32[]{:S(2)}) collective-permute-start(bf16[48,3584]{1,0:T(8,128)(2,1)S(1)} %slice.149), channel_id=1, source_target_pairs={{0,16},{8,24},{16,0},{24,8},{1,17},{9,25},{17,1},{25,9},{2,18},{10... | collective-permute-start | bytes 1032200 | tf_op jit(solution)/shard_map/ppermute | solution.py:409
  64.9 14.0 %collective-permute-start.11 = (bf16[48,3584]{1,0:T(8,128)(2,1)S(1)}, bf16[48,3584]{1,0:T(8,128)(2,1)S(1)}, u32[]{:S(2)}, u32[]{:S(2)}) collective-permute-start(bf16[48,3584]{1,0:T(8,128)(2,1)S(1)} %slice.148), channel_id=1, source_target_pairs={{0,8},{8,0},{16,24},{24,16},{1,9},{9,1},{17,25},{25,17},{2,10},{10... | collective-permute-start | bytes 1032200 | tf_op jit(solution)/shard_map/ppermute | solution.py:409
  70.0 11.2 %collective-permute-start.13 = (bf16[48,1536]{1,0:T(8,128)(2,1)S(1)}, bf16[48,1536]{1,0:T(8,128)(2,1)S(1)}, u32[]{:S(2)}, u32[]{:S(2)}) collective-permute-start(bf16[48,1536]{1,0:T(8,128)(2,1)S(1)} %slice.153), channel_id=1, source_target_pairs={{0,8},{8,0},{16,24},{24,16},{1,9},{9,1},{17,25},{25,17},{2,10},{10... | collective-permute-start | bytes 442376 | tf_op jit(solution)/shard_map/ppermute | solution.py:409
  71.7 10.2 %collective-permute-start.9 = (bf16[48,2048]{1,0:T(8,128)(2,1)S(1)}, bf16[48,2048]{1,0:T(8,128)(2,1)S(1)}, u32[]{:S(2)}, u32[]{:S(2)}) collective-permute-start(bf16[48,2048]{1,0:T(8,128)(2,1)S(1)} %slice.152), channel_id=1, source_target_pairs={{0,16},{8,24},{16,0},{24,8},{1,17},{9,25},{17,1},{25,9},{2,18},{10... | collective-permute-start | bytes 589832 | tf_op jit(solution)/shard_map/ppermute | solution.py:409
  79.2 7.2 %collective-permute-start.14 = (bf16[48,2048]{1,0:T(8,128)(2,1)S(1)}, bf16[48,2048]{1,0:T(8,128)(2,1)S(1)}, u32[]{:S(2)}, u32[]{:S(2)}) collective-permute-start(bf16[48,2048]{1,0:T(8,128)(2,1)S(1)} %slice.102), channel_id=1, source_target_pairs={{0,16},{8,24},{16,0},{24,8},{1,17},{9,25},{17,1},{25,9},{2,18},{10... | collective-permute-start | bytes 589832 | tf_op jit(solution)/shard_map/ppermute | solution.py:409
  81.2 5.1 %collective-permute-start.15 = (bf16[48,1536]{1,0:T(8,128)(2,1)S(1)}, bf16[48,1536]{1,0:T(8,128)(2,1)S(1)}, u32[]{:S(2)}, u32[]{:S(2)}) collective-permute-start(bf16[48,1536]{1,0:T(8,128)(2,1)S(1)} %slice.103), channel_id=1, source_target_pairs={{0,8},{8,0},{16,24},{24,16},{1,9},{9,1},{17,25},{25,17},{2,10},{10... | collective-permute-start | bytes 442376 | tf_op jit(solution)/shard_map/ppermute | solution.py:409
  86.4 12.7 %collective-permute-start.18 = (bf16[96,2048]{1,0:T(8,128)(2,1)S(1)}, bf16[96,2048]{1,0:T(8,128)(2,1)S(1)}, u32[]{:S(2)}, u32[]{:S(2)}) collective-permute-start(bf16[96,2048]{1,0:T(8,128)(2,1)S(1)} %constant_dynamic-update-slice_fusion.11.refs_1_), channel_id=1, source_target_pairs={{0,8},{8,0},{16,24},{24,16},{1,9},{9,1},{17,25},{25,17},{2,10},{10... | collective-permute-start | bytes 1179656 | tf_op jit(solution)/shard_map/ppermute | solution.py:409
  87.0 12.1 %collective-permute-start.19 = (bf16[96,1536]{1,0:T(8,128)(2,1)S(1)}, bf16[96,1536]{1,0:T(8,128)(2,1)S(1)}, u32[]{:S(2)}, u32[]{:S(2)}) collective-permute-start(bf16[96,1536]{1,0:T(8,128)(2,1)S(1)} %constant_dynamic-update-slice_fusion.13.refs_3_), channel_id=1, source_target_pairs={{0,16},{8,24},{16,0},{24,8},{1,17},{9,25},{17,1},{25,9},{2,18},{10... | collective-permute-start | bytes 884744 | tf_op jit(solution)/shard_map/ppermute | solution.py:409
  87.6 11.5 %collective-permute-start.16 = (bf16[48,2048]{1,0:T(8,128)(2,1)S(1)}, bf16[48,2048]{1,0:T(8,128)(2,1)S(1)}, u32[]{:S(2)}, u32[]{:S(2)}) collective-permute-start(bf16[48,2048]{1,0:T(8,128)(2,1)S(1)} %get-tuple-element.96), channel_id=1, source_target_pairs={{0,16},{8,24},{16,0},{24,8},{1,17},{9,25},{17,1},{25,9},{2,18},{10... | collective-permute-start | bytes 589832 | tf_op jit(solution)/shard_map/ppermute | solution.py:409
  89.2 9.9 %collective-permute-start.17 = (bf16[48,1536]{1,0:T(8,128)(2,1)S(1)}, bf16[48,1536]{1,0:T(8,128)(2,1)S(1)}, u32[]{:S(2)}, u32[]{:S(2)}) collective-permute-start(bf16[48,1536]{1,0:T(8,128)(2,1)S(1)} %get-tuple-element.97), channel_id=1, source_target_pairs={{0,8},{8,0},{16,24},{24,16},{1,9},{9,1},{17,25},{25,17},{2,10},{10... | collective-permute-start | bytes 442376 | tf_op jit(solution)/shard_map/ppermute | solution.py:409
  99.1 18.4 %collective-permute-start.23 = (bf16[96,2048]{1,0:T(8,128)(2,1)S(1)}, bf16[96,2048]{1,0:T(8,128)(2,1)S(1)}, u32[]{:S(2)}, u32[]{:S(2)}) collective-permute-start(bf16[96,2048]{1,0:T(8,128)(2,1)S(1)} %constant_dynamic-update-slice_fusion.15.refs_3_.refs_1_), channel_id=1, source_target_pairs={{0,8},{8,0},{16,24},{24,16},{1,9},{9,1},{17,25},{25,17},{2,10},{10... | collective-permute-start | bytes 1179656 | tf_op jit(solution)/shard_map/ppermute | solution.py:409
  100.0 22.5 %collective-permute-start.25 = (bf16[96,1536]{1,0:T(8,128)(2,1)S(1)}, bf16[96,1536]{1,0:T(8,128)(2,1)S(1)}, u32[]{:S(2)}, u32[]{:S(2)}) collective-permute-start(bf16[96,1536]{1,0:T(8,128)(2,1)S(1)} %constant_dynamic-update-slice_fusion.17.refs_3_), channel_id=1, source_target_pairs={{0,16},{8,24},{16,0},{24,8},{1,17},{9,25},{17,1},{25,9},{2,18},{10... | collective-permute-start | bytes 884744 | tf_op jit(solution)/shard_map/ppermute | solution.py:409
  100.5 16.0 %collective-permute-start.20 = (bf16[48,2048]{1,0:T(8,128)(2,1)S(1)}, bf16[48,2048]{1,0:T(8,128)(2,1)S(1)}, u32[]{:S(2)}, u32[]{:S(2)}) collective-permute-start(bf16[48,2048]{1,0:T(8,128)(2,1)S(1)} %get-tuple-element.102), channel_id=1, source_target_pairs={{0,16},{8,24},{16,0},{24,8},{1,17},{9,25},{17,1},{25,9},{2,18},{10... | collective-permute-start | bytes 589832 | tf_op jit(solution)/shard_map/ppermute | solution.py:409
  102.1 14.5 %collective-permute-start.21 = (bf16[48,1536]{1,0:T(8,128)(2,1)S(1)}, bf16[48,1536]{1,0:T(8,128)(2,1)S(1)}, u32[]{:S(2)}, u32[]{:S(2)}) collective-permute-start(bf16[48,1536]{1,0:T(8,128)(2,1)S(1)} %get-tuple-element.103), channel_id=1, source_target_pairs={{0,8},{8,0},{16,24},{24,16},{1,9},{9,1},{17,25},{25,17},{2,10},{10... | collective-permute-start | bytes 442376 | tf_op jit(solution)/shard_map/ppermute | solution.py:409
  116.5 4.9 %collective-permute-start.22 = (f32[96,2048]{1,0:T(8,128)S(1)}, f32[96,2048]{1,0:T(8,128)S(1)}, u32[]{:S(2)}, u32[]{:S(2)}) collective-permute-start(f32[96,2048]{1,0:T(8,128)S(1)} %get-tuple-element.105), channel_id=1, source_target_pairs={{0,1},{1,0},{2,3},{3,2},{4,5},{5,4},{6,7},{7,6},{8,9},{9,8},{10,11... | collective-permute-start | bytes 2359304 | tf_op jit(solution)/shard_map/ppermute | solution.py:409
  116.7 14.1 %collective-permute-start.27 = (bf16[96,2048]{1,0:T(8,128)(2,1)S(1)}, bf16[96,2048]{1,0:T(8,128)(2,1)S(1)}, u32[]{:S(2)}, u32[]{:S(2)}) collective-permute-start(bf16[96,2048]{1,0:T(8,128)(2,1)S(1)} %constant_dynamic-update-slice_fusion.19.refs_5_.refs_3_), channel_id=1, source_target_pairs={{0,8},{8,0},{16,24},{24,16},{1,9},{9,1},{17,25},{25,17},{2,10},{10... | collective-permute-start | bytes 1179656 | tf_op jit(solution)/shard_map/ppermute | solution.py:409
  121.5 7.1 %collective-permute-start.24 = (bf16[48,2048]{1,0:T(8,128)(2,1)S(1)}, bf16[48,2048]{1,0:T(8,128)(2,1)S(1)}, u32[]{:S(2)}, u32[]{:S(2)}) collective-permute-start(bf16[48,2048]{1,0:T(8,128)(2,1)S(1)} %slice.151), channel_id=1, source_target_pairs={{0,2},{1,3},{2,0},{3,1},{4,6},{5,7},{6,4},{7,5},{8,10},{9,11},{10,... | collective-permute-start | bytes 589832 | tf_op jit(solution)/shard_map/ppermute | solution.py:409
  121.9 8.9 %collective-permute-start.28 = (bf16[96,1536]{1,0:T(8,128)(2,1)S(1)}, bf16[96,1536]{1,0:T(8,128)(2,1)S(1)}, u32[]{:S(2)}, u32[]{:S(2)}) collective-permute-start(bf16[96,1536]{1,0:T(8,128)(2,1)S(1)} %constant_dynamic-update-slice_fusion.21.refs_7_.refs_3_), channel_id=1, source_target_pairs={{0,16},{8,24},{16,0},{24,8},{1,17},{9,25},{17,1},{25,9},{2,18},{10... | collective-permute-start | bytes 884744 | tf_op jit(solution)/shard_map/ppermute | solution.py:409
  128.7 16.3 %collective-permute-start.26 = (bf16[24,2048]{1,0:T(8,128)(2,1)S(1)}, bf16[24,2048]{1,0:T(8,128)(2,1)S(1)}, u32[]{:S(2)}, u32[]{:S(2)}) collective-permute-start(bf16[24,2048]{1,0:T(8,128)(2,1)S(1)} %slice.155), channel_id=1, source_target_pairs={{0,4},{1,5},{2,6},{3,7},{4,0},{5,1},{6,2},{7,3},{8,12},{9,13},{10,... | collective-permute-start | bytes 294920 | tf_op jit(solution)/shard_map/ppermute | solution.py:409
  145.0 2.4 %collective-permute-start.29 = (f32[96,2048]{1,0:T(8,128)S(1)}, f32[96,2048]{1,0:T(8,128)S(1)}, u32[]{:S(2)}, u32[]{:S(2)}) collective-permute-start(f32[96,2048]{1,0:T(8,128)S(1)} %get-tuple-element.121), channel_id=1, source_target_pairs={{0,1},{1,0},{2,3},{3,2},{4,5},{5,4},{6,7},{7,6},{8,9},{9,8},{10,11... | collective-permute-start | bytes 2359304 | tf_op jit(solution)/shard_map/ppermute | solution.py:409
  148.6 7.0 %collective-permute-start.30 = (bf16[48,2048]{1,0:T(8,128)(2,1)S(1)}, bf16[48,2048]{1,0:T(8,128)(2,1)S(1)}, u32[]{:S(2)}, u32[]{:S(2)}) collective-permute-start(bf16[48,2048]{1,0:T(8,128)(2,1)S(1)} %slice.150), channel_id=1, source_target_pairs={{0,2},{1,3},{2,0},{3,1},{4,6},{5,7},{6,4},{7,5},{8,10},{9,11},{10,... | collective-permute-start | bytes 589832 | tf_op jit(solution)/shard_map/ppermute | solution.py:409
  155.7 7.2 %collective-permute-start.31 = (bf16[24,2048]{1,0:T(8,128)(2,1)S(1)}, bf16[24,2048]{1,0:T(8,128)(2,1)S(1)}, u32[]{:S(2)}, u32[]{:S(2)}) collective-permute-start(bf16[24,2048]{1,0:T(8,128)(2,1)S(1)} %slice.154), channel_id=1, source_target_pairs={{0,4},{1,5},{2,6},{3,7},{4,0},{5,1},{6,2},{7,3},{8,12},{9,13},{10,... | collective-permute-start | bytes 294920 | tf_op jit(solution)/shard_map/ppermute | solution.py:409
  (11 other events, 97.4 us)

commit v6 on v5

--- a/solution.py
+++ b/solution.py
@@ -193,7 +193,7 @@
         ],
         steps,
         [pl.BlockSpec((total // 2, tile), lambda i: (0, i))] * 2,
-        mib=32,
+        mib=51,
     )
 
 
@@ -242,7 +242,7 @@
         steps,
         [pl.BlockSpec((total // 2, tile), lambda i: (0, jnp.minimum(i, front - 1)))] * 2
         + [pl.BlockSpec((total // 2, tile), lambda i: (0, jnp.maximum(i - front, 0)))] * 2,
-        mib=32,
+        mib=51,
     )
 
 

time: 164 us -> 162 us (0.988)
  local copies, waits for them, and re-layouts: 14.1 us -> 9.21 us
  Pallas kernels: 61.7 us -> 64 us
    unnamed x34 -> x30, local copies, waits for them, and re-layouts: 13.6 us -> 6.7 us
    pallas_call x9, Pallas kernels: 61.7 us -> 64 us  [call(): pl.pallas_call(unmarked, in_specs=[spec[kind] for kind in (*kinds, *'h' *...]
    concatenate x3, other arithmetic: 0.95 us -> 2.67 us  [gathering(): own = jnp.concatenate([own, got], axis=0)]
  transfers between devices with their start and end apart: 32 -> 32, of which waited for: 14 -> 13; matrix products, arithmetic and copies ran while one was open for 3% -> 8% of each run, Pallas kernels for 38% -> 40%
where the time goes in v6:
time: 162 us
  Pallas kernels  64 us (40%)
  waiting for transfers between devices  44.3 us (27%)
  starting transfers between devices  34.7 us (21%)
  local copies, waits for them, and re-layouts  9.21 us (6%)
  other arithmetic  8.55 us (5%)
    pallas_call x9, Pallas kernels, call(): pl.pallas_call(unmarked, in_specs=[spec[kind] for kind in (*kinds, *'h' *...  64 us
    ppermute x32, waiting for transfers between devices, swap(): return lax.ppermute(value, axis, [(i, i ^ bit) for i in range(size)])  44.3 us
    ppermute x32, starting transfers between devices, swap(): return lax.ppermute(value, axis, [(i, i ^ bit) for i in range(size)])  34.7 us
    unnamed x30, local copies, waits for them, and re-layouts  6.7 us
  transfers between devices with their start and end apart: 32, of which 13 were waited for; matrix products, arithmetic and copies ran while one was open for 8% of the time, Pallas kernels for 40%

profile of v6, /device:TPU:0, one launch (start us, length us, event | category | flops | bytes accessed | tf_op | source)
XLA Modules:
  0.0 161.8 jit_solution(13993717302305925296)
XLA Ops:
  0.7 4.1 %collective-permute-start = (bf16[24,2048]{1,0:T(8,128)(2,1)}, bf16[24,2048]{1,0:T(8,128)(2,1)S(1)}, u32[]{:S(2)}, u32[]{:S(2)}) collective-permute-start(bf16[24,2048]{1,0:T(8,128)(2,1)} %param.8), channel_id=1, source_target_pairs={{0,4},{1,5},{2,6},{3,7},{4,0},{5,1},{6,2},{7,3},{8,12},{9,13},{10,... | collective-permute-start | bytes 294920 | tf_op jit(solution)/shard_map/ppermute | solution.py:409
  5.7 4.2 %collective-permute-done = bf16[24,2048]{1,0:T(8,128)(2,1)S(1)} collective-permute-done((bf16[24,2048]{1,0:T(8,128)(2,1)}, bf16[24,2048]{1,0:T(8,128)(2,1)S(1)}, u32[]{:S(2)}, u32[]{:S(2)}) %collective-permute-start) | collective-permute-done | bytes 98336 | tf_op jit(solution)/shard_map/ppermute | solution.py:409
  11.7 5.2 %collective-permute-done.1 = bf16[48,2048]{1,0:T(8,128)(2,1)S(1)} collective-permute-done((bf16[48,2048]{1,0:T(8,128)(2,1)S(1)}, bf16[48,2048]{1,0:T(8,128)(2,1)S(1)}, u32[]{:S(2)}, u32[]{:S(2)}) %collective-permute-start.1) | collective-permute-done | bytes 196640 | tf_op jit(solution)/shard_map/ppermute | solution.py:409
  17.8 3.1 %collective-permute-start.3 = (bf16[24,2048]{1,0:T(8,128)(2,1)S(1)}, bf16[24,2048]{1,0:T(8,128)(2,1)S(1)}, u32[]{:S(2)}, u32[]{:S(2)}) collective-permute-start(bf16[24,2048]{1,0:T(8,128)(2,1)S(1)} %copy-done.6), channel_id=1, source_target_pairs={{0,4},{1,5},{2,6},{3,7},{4,0},{5,1},{6,2},{7,3},{8,12},{9,13},{10,... | collective-permute-start | bytes 294920 | tf_op jit(solution)/shard_map/ppermute | solution.py:409
  20.9 6.9 %forward_part.2 = (bf16[96,3584]{1,0:T(8,128)(2,1)}, f32[96,3584]{1,0:T(8,128)S(1)}) custom-call(s32[1]{0:T(128)} %bitcast.refs_0_, bf16[192,2048]{1,0:T(8,128)(2,1)S(1)} %constant_dynamic-update-slice_fusion.3.refs_1_, bf16[2048,3584]{1,0:T(8,128)(2,1)} %refs_9_.1, s32[32,56]{1,0:T(8,128)S(1)} %copy-done.1), custom_call_target="tpu_custom_call" | custom-call | flops 1000 | bytes 1000 | tf_op jit(solution)/shard_map/forward_part/pallas_call | solution.py:138
  28.5 1.7 %collective-permute-start.4 = (bf16[48,2048]{1,0:T(8,128)(2,1)}, bf16[48,2048]{1,0:T(8,128)(2,1)}, u32[]{:S(2)}, u32[]{:S(2)}) collective-permute-start(bf16[48,2048]{1,0:T(8,128)(2,1)} %pad_maximum_fusion.2), channel_id=1, source_target_pairs={{0,2},{1,3},{2,0},{3,1},{4,6},{5,7},{6,4},{7,5},{8,10},{9,11},{10,... | collective-permute-start | bytes 589832 | tf_op jit(solution)/shard_map/ppermute | solution.py:409
  32.4 6.8 %forward_part.3 = (bf16[96,3584]{1,0:T(8,128)(2,1)}, f32[96,3584]{1,0:T(8,128)S(1)}) custom-call(s32[1]{0:T(128)} %bitcast.refs_0_, bf16[192,2048]{1,0:T(8,128)(2,1)S(1)} %constant_dynamic-update-slice_fusion.3.refs_1_, bf16[2048,3584]{1,0:T(8,128)(2,1)} %refs_10_.1, s32[32,56]{1,0:T(8,128)S(1)} %copy-done.2), custom_call_target="tpu_custom_call" | custom-call | flops 1000 | bytes 1000 | tf_op jit(solution)/shard_map/forward_part/pallas_call | solution.py:138
  39.2 1.6 collective-permute-start.8
  43.4 1.5 constant_dynamic-update-slice_fusion.9
  44.9 1.6 constant_dynamic-update-slice_fusion.8
  48.5 8.3 %hidden_part.1 = (bf16[96,2048]{1,0:T(8,128)(2,1)S(1)}, f32[96,2048]{1,0:T(8,128)S(1)}, bf16[96,1536]{1,0:T(8,128)(2,1)S(1)}, f32[96,1536]{1,0:T(8,128)S(1)}) custom-call(s32[1]{0:T(128)} %bitcast.refs_0_, bf16[192,2048]{1,0:T(8,128)(2,1)S(1)} %copy-done, bf16[3584,2048]{1,0:T(8,128)(2,1)} %refs_6_.1, s32[56,32]{1,0:T(8,128)S(1)} %copy-done.4), custom_call_target="tpu_custom_call" | custom-call | flops 1000 | bytes 1000 | tf_op jit(solution)/shard_map/hidden_part/pallas_call | solution.py:138
  59.1 1.6 collective-permute-start.10
  62.0 1.6 collective-permute-start.11
  63.5 3.6 %collective-permute-done.12 = bf16[96,1536]{1,0:T(8,128)(2,1)S(1)} collective-permute-done((bf16[96,1536]{1,0:T(8,128)(2,1)S(1)}, bf16[96,1536]{1,0:T(8,128)(2,1)S(1)}, u32[]{:S(2)}, u32[]{:S(2)}) %collective-permute-start.12) | collective-permute-done | bytes 294944 | tf_op jit(solution)/shard_map/ppermute | solution.py:409
  67.3 1.6 collective-permute-start.13
  69.5 5.1 %collective-permute-done.10 = bf16[48,3584]{1,0:T(8,128)(2,1)S(1)} collective-permute-done((bf16[48,3584]{1,0:T(8,128)(2,1)S(1)}, bf16[48,3584]{1,0:T(8,128)(2,1)S(1)}, u32[]{:S(2)}, u32[]{:S(2)}) %collective-permute-start.10) | collective-permute-done | bytes 344096 | tf_op jit(solution)/shard_map/ppermute | solution.py:409
  74.5 1.5 collective-permute-done.11
  77.0 1.9 %collective-permute-done.13 = bf16[48,1536]{1,0:T(8,128)(2,1)S(1)} collective-permute-done((bf16[48,1536]{1,0:T(8,128)(2,1)S(1)}, bf16[48,1536]{1,0:T(8,128)(2,1)S(1)}, u32[]{:S(2)}, u32[]{:S(2)}) %collective-permute-start.13) | collective-permute-done | bytes 147488 | tf_op jit(solution)/shard_map/ppermute | solution.py:409
  79.8 4.5 %collective-permute-done.15 = bf16[48,1536]{1,0:T(8,128)(2,1)S(1)} collective-permute-done((bf16[48,1536]{1,0:T(8,128)(2,1)S(1)}, bf16[48,1536]{1,0:T(8,128)(2,1)S(1)}, u32[]{:S(2)}, u32[]{:S(2)}) %collective-permute-start.15) | collective-permute-done | bytes 147488 | tf_op jit(solution)/shard_map/ppermute | solution.py:409
  85.5 1.6 collective-permute-start.16
  88.6 8.8 %collective-permute-done.17 = bf16[48,1536]{1,0:T(8,128)(2,1)S(1)} collective-permute-done((bf16[48,1536]{1,0:T(8,128)(2,1)S(1)}, bf16[48,1536]{1,0:T(8,128)(2,1)S(1)}, u32[]{:S(2)}, u32[]{:S(2)}) %collective-permute-start.17) | collective-permute-done | bytes 147488 | tf_op jit(solution)/shard_map/ppermute | solution.py:409
  98.9 1.5 collective-permute-start.20
  101.7 13.2 %down_back.1 = (bf16[3584,2048]{1,0:T(8,128)(2,1)}, f32[96,2048]{1,0:T(8,128)S(1)}, f32[96,2048]{1,0:T(8,128)S(1)}) custom-call(s32[1]{0:T(128)} %bitcast.refs_0_, bf16[96,2048]{1,0:T(8,128)(2,1)S(1)} %constant_dynamic-update-slice_fusion.11.refs_1_, bf16[96,2048]{1,0:T(8,128)(2,1)S(1)} %collective-permute-done.18.refs_2_, ...), custom_call_target="tpu_custom_call" | custom-call | flops 5637144576 | bytes 1000 | tf_op jit(solution)/shard_map/down_back/pallas_call | solution.py:138
  115.9 3.9 %weight_back.4 = (bf16[2048,3584]{1,0:T(8,128)(2,1)}, f32[8,128]{1,0:T(8,128)S(1)}) custom-call(s32[1]{0:T(128)} %bitcast.refs_0_, bf16[192,2048]{1,0:T(8,128)(2,1)S(1)} %constant_dynamic-update-slice_fusion.3.refs_1_, s32[32,56]{1,0:T(8,128)S(1)} %copy-done.1, bf16[96,2048]{1,0:T(8,128)(2,1)S(1)} %constant_dynamic-update-slice_fusion.15.refs_3_.refs_1_, ...), custom_call_target="tpu_custom_call" | custom-call | flops 1610612736 | bytes 1000 | tf_op jit(solution)/shard_map/weight_back/pallas_call | solution.py:138
  120.8 3.2 %weight_back.5 = (bf16[2048,3584]{1,0:T(8,128)(2,1)}, f32[8,128]{1,0:T(8,128)S(1)}) custom-call(s32[1]{0:T(128)} %bitcast.refs_0_, bf16[192,2048]{1,0:T(8,128)(2,1)S(1)} %constant_dynamic-update-slice_fusion.3.refs_1_, s32[32,56]{1,0:T(8,128)S(1)} %copy-done.1, ...), custom_call_target="tpu_custom_call", output_to_operand_aliasing={{0}: (5, {})} | custom-call | flops 1207959552 | bytes 1000 | tf_op jit(solution)/shard_map/weight_back/pallas_call | solution.py:138
  124.0 3.0 %collective-permute-done.24 = bf16[48,2048]{1,0:T(8,128)(2,1)S(1)} collective-permute-done((bf16[48,2048]{1,0:T(8,128)(2,1)S(1)}, bf16[48,2048]{1,0:T(8,128)(2,1)S(1)}, u32[]{:S(2)}, u32[]{:S(2)}) %collective-permute-start.24) | collective-permute-done | bytes 196640 | tf_op jit(solution)/shard_map/ppermute | solution.py:409
  129.2 14.1 %input_back.1 = (f32[96,2048]{1,0:T(8,128)S(1)}, f32[96,2048]{1,0:T(8,128)}) custom-call(s32[1]{0:T(128)} %bitcast.refs_0_, bf16[96,2048]{1,0:T(8,128)(2,1)S(1)} %constant_dynamic-update-slice_fusion.15.refs_3_.refs_1_, bf16[96,2048]{1,0:T(8,128)(2,1)S(1)} %collective-permute-done.23.refs_4_.refs_2_, ...), custom_call_target="tpu_custom_call" | custom-call | flops 5637144576 | bytes 1000 | tf_op jit(solution)/shard_map/input_back/pallas_call | solution.py:138
  143.4 2.3 %collective-permute-done.29 = f32[96,2048]{1,0:T(8,128)S(1)} collective-permute-done((f32[96,2048]{1,0:T(8,128)S(1)}, f32[96,2048]{1,0:T(8,128)S(1)}, u32[]{:S(2)}, u32[]{:S(2)}) %collective-permute-start.29) | collective-permute-done | bytes 786464 | tf_op jit(solution)/shard_map/ppermute | solution.py:409
  146.9 1.8 %collective-permute-start.30 = (bf16[48,2048]{1,0:T(8,128)(2,1)S(1)}, bf16[48,2048]{1,0:T(8,128)(2,1)S(1)}, u32[]{:S(2)}, u32[]{:S(2)}) collective-permute-start(bf16[48,2048]{1,0:T(8,128)(2,1)S(1)} %slice.150), channel_id=1, source_target_pairs={{0,2},{1,3},{2,0},{3,1},{4,6},{5,7},{6,4},{7,5},{8,10},{9,11},{10,... | collective-permute-start | bytes 589832 | tf_op jit(solution)/shard_map/ppermute | solution.py:409
  149.3 3.9 %weight_back.6 = (bf16[2048,3584]{1,0:T(8,128)(2,1)}, f32[8,128]{1,0:T(8,128)S(1)}) custom-call(s32[1]{0:T(128)} %bitcast.refs_0_, bf16[192,2048]{1,0:T(8,128)(2,1)S(1)} %constant_dynamic-update-slice_fusion.3.refs_1_, s32[32,56]{1,0:T(8,128)S(1)} %copy-done.3, bf16[96,2048]{1,0:T(8,128)(2,1)S(1)} %constant_dynamic-update-slice_fusion.19.refs_5_.refs_3_, ...), custom_call_target="tpu_custom_call" | custom-call | flops 1610612736 | bytes 1000 | tf_op jit(solution)/shard_map/weight_back/pallas_call | solution.py:138
  155.0 3.8 %weight_back.7 = (bf16[2048,3584]{1,0:T(8,128)(2,1)}, f32[8,128]{1,0:T(8,128)}) custom-call(s32[1]{0:T(128)} %bitcast.refs_0_, bf16[192,2048]{1,0:T(8,128)(2,1)S(1)} %constant_dynamic-update-slice_fusion.3.refs_1_, s32[32,56]{1,0:T(8,128)S(1)} %copy-done.3, ...), custom_call_target="tpu_custom_call", output_to_operand_aliasing={{0}: (5, {})} | custom-call | flops 1207959552 | bytes 1000 | tf_op jit(solution)/shard_map/weight_back/pallas_call | solution.py:138
  158.8 2.4 %collective-permute-done.31 = bf16[24,2048]{1,0:T(8,128)(2,1)S(1)} collective-permute-done((bf16[24,2048]{1,0:T(8,128)(2,1)S(1)}, bf16[24,2048]{1,0:T(8,128)(2,1)S(1)}, u32[]{:S(2)}, u32[]{:S(2)}) %collective-permute-start.31) | collective-permute-done | bytes 98336 | tf_op jit(solution)/shard_map/ppermute | solution.py:409
  (107 shorter events, 31.0 us)
Async XLA Ops:
  0.7 9.2 %collective-permute-start = (bf16[24,2048]{1,0:T(8,128)(2,1)}, bf16[24,2048]{1,0:T(8,128)(2,1)S(1)}, u32[]{:S(2)}, u32[]{:S(2)}) collective-permute-start(bf16[24,2048]{1,0:T(8,128)(2,1)} %param.8), channel_id=1, source_target_pairs={{0,4},{1,5},{2,6},{3,7},{4,0},{5,1},{6,2},{7,3},{8,12},{9,13},{10,... | collective-permute-start | bytes 294920 | tf_op jit(solution)/shard_map/ppermute | solution.py:409
  10.8 6.2 %collective-permute-start.1 = (bf16[48,2048]{1,0:T(8,128)(2,1)S(1)}, bf16[48,2048]{1,0:T(8,128)(2,1)S(1)}, u32[]{:S(2)}, u32[]{:S(2)}) collective-permute-start(bf16[48,2048]{1,0:T(8,128)(2,1)S(1)} %pad_maximum_fusion.1), channel_id=1, source_target_pairs={{0,2},{1,3},{2,0},{3,1},{4,6},{5,7},{6,4},{7,5},{8,10},{9,11},{10,... | collective-permute-start | bytes 589832 | tf_op jit(solution)/shard_map/ppermute | solution.py:409
  17.0 3.9 %collective-permute-start.2 = (bf16[96,2048]{1,0:T(8,128)(2,1)S(1)}, bf16[96,2048]{1,0:T(8,128)(2,1)S(1)}, u32[]{:S(2)}, u32[]{:S(2)}) collective-permute-start(bf16[96,2048]{1,0:T(8,128)(2,1)S(1)} %get-tuple-element.138), channel_id=1, source_target_pairs={{0,1},{1,0},{2,3},{3,2},{4,5},{5,4},{6,7},{7,6},{8,9},{9,8},{10,11... | collective-permute-start | bytes 1179656 | tf_op jit(solution)/shard_map/ppermute | solution.py:409
  17.8 10.0 %collective-permute-start.3 = (bf16[24,2048]{1,0:T(8,128)(2,1)S(1)}, bf16[24,2048]{1,0:T(8,128)(2,1)S(1)}, u32[]{:S(2)}, u32[]{:S(2)}) collective-permute-start(bf16[24,2048]{1,0:T(8,128)(2,1)S(1)} %copy-done.6), channel_id=1, source_target_pairs={{0,4},{1,5},{2,6},{3,7},{4,0},{5,1},{6,2},{7,3},{8,12},{9,13},{10,... | collective-permute-start | bytes 294920 | tf_op jit(solution)/shard_map/ppermute | solution.py:409
  28.5 13.7 %collective-permute-start.4 = (bf16[48,2048]{1,0:T(8,128)(2,1)}, bf16[48,2048]{1,0:T(8,128)(2,1)}, u32[]{:S(2)}, u32[]{:S(2)}) collective-permute-start(bf16[48,2048]{1,0:T(8,128)(2,1)} %pad_maximum_fusion.2), channel_id=1, source_target_pairs={{0,2},{1,3},{2,0},{3,1},{4,6},{5,7},{6,4},{7,5},{8,10},{9,11},{10,... | collective-permute-start | bytes 589832 | tf_op jit(solution)/shard_map/ppermute | solution.py:409
  30.9 26.9 %collective-permute-start.7 = (bf16[96,3584]{1,0:T(8,128)(2,1)}, bf16[96,3584]{1,0:T(8,128)(2,1)}, u32[]{:S(2)}, u32[]{:S(2)}) collective-permute-start(bf16[96,3584]{1,0:T(8,128)(2,1)} %get-tuple-element.68), channel_id=1, source_target_pairs={{0,8},{8,0},{16,24},{24,16},{1,9},{9,1},{17,25},{25,17},{2,10},{10... | collective-permute-start | bytes 2064392 | tf_op jit(solution)/shard_map/ppermute | solution.py:409
  39.2 18.6 %collective-permute-start.8 = (bf16[96,3584]{1,0:T(8,128)(2,1)}, bf16[96,3584]{1,0:T(8,128)(2,1)}, u32[]{:S(2)}, u32[]{:S(2)}) collective-permute-start(bf16[96,3584]{1,0:T(8,128)(2,1)} %get-tuple-element.70), channel_id=1, source_target_pairs={{0,16},{8,24},{16,0},{24,8},{1,17},{9,25},{17,1},{25,9},{2,18},{10... | collective-permute-start | bytes 2064392 | tf_op jit(solution)/shard_map/ppermute | solution.py:409
  43.3 3.2 %collective-permute-start.5 = (bf16[96,2048]{1,0:T(8,128)(2,1)S(1)}, bf16[96,2048]{1,0:T(8,128)(2,1)S(1)}, u32[]{:S(2)}, u32[]{:S(2)}) collective-permute-start(bf16[96,2048]{1,0:T(8,128)(2,1)S(1)} %pad_maximum_fusion), channel_id=1, source_target_pairs={{0,1},{1,0},{2,3},{3,2},{4,5},{5,4},{6,7},{7,6},{8,9},{9,8},{10,11... | collective-permute-start | bytes 1179656 | tf_op jit(solution)/shard_map/ppermute | solution.py:409
  56.7 12.1 %collective-permute-start.6 = (bf16[96,2048]{1,0:T(8,128)(2,1)S(1)}, bf16[96,2048]{1,0:T(8,128)(2,1)S(1)}, u32[]{:S(2)}, u32[]{:S(2)}) collective-permute-start(bf16[96,2048]{1,0:T(8,128)(2,1)S(1)} %get-tuple-element.77), channel_id=1, source_target_pairs={{0,8},{8,0},{16,24},{24,16},{1,9},{9,1},{17,25},{25,17},{2,10},{10... | collective-permute-start | bytes 1179656 | tf_op jit(solution)/shard_map/ppermute | solution.py:409
  57.3 9.8 %collective-permute-start.12 = (bf16[96,1536]{1,0:T(8,128)(2,1)S(1)}, bf16[96,1536]{1,0:T(8,128)(2,1)S(1)}, u32[]{:S(2)}, u32[]{:S(2)}) collective-permute-start(bf16[96,1536]{1,0:T(8,128)(2,1)S(1)} %get-tuple-element.88), channel_id=1, source_target_pairs={{0,16},{8,24},{16,0},{24,8},{1,17},{9,25},{17,1},{25,9},{2,18},{10... | collective-permute-start | bytes 884744 | tf_op jit(solution)/shard_map/ppermute | solution.py:409
  59.1 15.4 %collective-permute-start.10 = (bf16[48,3584]{1,0:T(8,128)(2,1)S(1)}, bf16[48,3584]{1,0:T(8,128)(2,1)S(1)}, u32[]{:S(2)}, u32[]{:S(2)}) collective-permute-start(bf16[48,3584]{1,0:T(8,128)(2,1)S(1)} %slice.149), channel_id=1, source_target_pairs={{0,16},{8,24},{16,0},{24,8},{1,17},{9,25},{17,1},{25,9},{2,18},{10... | collective-permute-start | bytes 1032200 | tf_op jit(solution)/shard_map/ppermute | solution.py:409
  62.0 14.1 %collective-permute-start.11 = (bf16[48,3584]{1,0:T(8,128)(2,1)S(1)}, bf16[48,3584]{1,0:T(8,128)(2,1)S(1)}, u32[]{:S(2)}, u32[]{:S(2)}) collective-permute-start(bf16[48,3584]{1,0:T(8,128)(2,1)S(1)} %slice.148), channel_id=1, source_target_pairs={{0,8},{8,0},{16,24},{24,16},{1,9},{9,1},{17,25},{25,17},{2,10},{10... | collective-permute-start | bytes 1032200 | tf_op jit(solution)/shard_map/ppermute | solution.py:409
  67.3 11.6 %collective-permute-start.13 = (bf16[48,1536]{1,0:T(8,128)(2,1)S(1)}, bf16[48,1536]{1,0:T(8,128)(2,1)S(1)}, u32[]{:S(2)}, u32[]{:S(2)}) collective-permute-start(bf16[48,1536]{1,0:T(8,128)(2,1)S(1)} %slice.153), channel_id=1, source_target_pairs={{0,8},{8,0},{16,24},{24,16},{1,9},{9,1},{17,25},{25,17},{2,10},{10... | collective-permute-start | bytes 442376 | tf_op jit(solution)/shard_map/ppermute | solution.py:409
  68.9 10.6 %collective-permute-start.9 = (bf16[48,2048]{1,0:T(8,128)(2,1)S(1)}, bf16[48,2048]{1,0:T(8,128)(2,1)S(1)}, u32[]{:S(2)}, u32[]{:S(2)}) collective-permute-start(bf16[48,2048]{1,0:T(8,128)(2,1)S(1)} %slice.152), channel_id=1, source_target_pairs={{0,16},{8,24},{16,0},{24,8},{1,17},{9,25},{17,1},{25,9},{2,18},{10... | collective-permute-start | bytes 589832 | tf_op jit(solution)/shard_map/ppermute | solution.py:409
  76.4 7.9 %collective-permute-start.14 = (bf16[48,2048]{1,0:T(8,128)(2,1)S(1)}, bf16[48,2048]{1,0:T(8,128)(2,1)S(1)}, u32[]{:S(2)}, u32[]{:S(2)}) collective-permute-start(bf16[48,2048]{1,0:T(8,128)(2,1)S(1)} %slice.102), channel_id=1, source_target_pairs={{0,16},{8,24},{16,0},{24,8},{1,17},{9,25},{17,1},{25,9},{2,18},{10... | collective-permute-start | bytes 589832 | tf_op jit(solution)/shard_map/ppermute | solution.py:409
  78.9 5.5 %collective-permute-start.15 = (bf16[48,1536]{1,0:T(8,128)(2,1)S(1)}, bf16[48,1536]{1,0:T(8,128)(2,1)S(1)}, u32[]{:S(2)}, u32[]{:S(2)}) collective-permute-start(bf16[48,1536]{1,0:T(8,128)(2,1)S(1)} %slice.103), channel_id=1, source_target_pairs={{0,8},{8,0},{16,24},{24,16},{1,9},{9,1},{17,25},{25,17},{2,10},{10... | collective-permute-start | bytes 442376 | tf_op jit(solution)/shard_map/ppermute | solution.py:409
  84.3 13.1 %collective-permute-start.18 = (bf16[96,2048]{1,0:T(8,128)(2,1)S(1)}, bf16[96,2048]{1,0:T(8,128)(2,1)S(1)}, u32[]{:S(2)}, u32[]{:S(2)}) collective-permute-start(bf16[96,2048]{1,0:T(8,128)(2,1)S(1)} %constant_dynamic-update-slice_fusion.11.refs_1_), channel_id=1, source_target_pairs={{0,8},{8,0},{16,24},{24,16},{1,9},{9,1},{17,25},{25,17},{2,10},{10... | collective-permute-start | bytes 1179656 | tf_op jit(solution)/shard_map/ppermute | solution.py:409
  84.9 12.5 %collective-permute-start.19 = (bf16[96,1536]{1,0:T(8,128)(2,1)S(1)}, bf16[96,1536]{1,0:T(8,128)(2,1)S(1)}, u32[]{:S(2)}, u32[]{:S(2)}) collective-permute-start(bf16[96,1536]{1,0:T(8,128)(2,1)S(1)} %constant_dynamic-update-slice_fusion.13.refs_3_), channel_id=1, source_target_pairs={{0,16},{8,24},{16,0},{24,8},{1,17},{9,25},{17,1},{25,9},{2,18},{10... | collective-permute-start | bytes 884744 | tf_op jit(solution)/shard_map/ppermute | solution.py:409
  85.5 11.9 %collective-permute-start.16 = (bf16[48,2048]{1,0:T(8,128)(2,1)S(1)}, bf16[48,2048]{1,0:T(8,128)(2,1)S(1)}, u32[]{:S(2)}, u32[]{:S(2)}) collective-permute-start(bf16[48,2048]{1,0:T(8,128)(2,1)S(1)} %get-tuple-element.96), channel_id=1, source_target_pairs={{0,16},{8,24},{16,0},{24,8},{1,17},{9,25},{17,1},{25,9},{2,18},{10... | collective-permute-start | bytes 589832 | tf_op jit(solution)/shard_map/ppermute | solution.py:409
  87.1 10.3 %collective-permute-start.17 = (bf16[48,1536]{1,0:T(8,128)(2,1)S(1)}, bf16[48,1536]{1,0:T(8,128)(2,1)S(1)}, u32[]{:S(2)}, u32[]{:S(2)}) collective-permute-start(bf16[48,1536]{1,0:T(8,128)(2,1)S(1)} %get-tuple-element.97), channel_id=1, source_target_pairs={{0,8},{8,0},{16,24},{24,16},{1,9},{9,1},{17,25},{25,17},{2,10},{10... | collective-permute-start | bytes 442376 | tf_op jit(solution)/shard_map/ppermute | solution.py:409
  97.5 18.4 %collective-permute-start.23 = (bf16[96,2048]{1,0:T(8,128)(2,1)S(1)}, bf16[96,2048]{1,0:T(8,128)(2,1)S(1)}, u32[]{:S(2)}, u32[]{:S(2)}) collective-permute-start(bf16[96,2048]{1,0:T(8,128)(2,1)S(1)} %constant_dynamic-update-slice_fusion.15.refs_3_.refs_1_), channel_id=1, source_target_pairs={{0,8},{8,0},{16,24},{24,16},{1,9},{9,1},{17,25},{25,17},{2,10},{10... | collective-permute-start | bytes 1179656 | tf_op jit(solution)/shard_map/ppermute | solution.py:409
  98.3 22.5 %collective-permute-start.25 = (bf16[96,1536]{1,0:T(8,128)(2,1)S(1)}, bf16[96,1536]{1,0:T(8,128)(2,1)S(1)}, u32[]{:S(2)}, u32[]{:S(2)}) collective-permute-start(bf16[96,1536]{1,0:T(8,128)(2,1)S(1)} %constant_dynamic-update-slice_fusion.17.refs_3_), channel_id=1, source_target_pairs={{0,16},{8,24},{16,0},{24,8},{1,17},{9,25},{17,1},{25,9},{2,18},{10... | collective-permute-start | bytes 884744 | tf_op jit(solution)/shard_map/ppermute | solution.py:409
  98.9 16.0 %collective-permute-start.20 = (bf16[48,2048]{1,0:T(8,128)(2,1)S(1)}, bf16[48,2048]{1,0:T(8,128)(2,1)S(1)}, u32[]{:S(2)}, u32[]{:S(2)}) collective-permute-start(bf16[48,2048]{1,0:T(8,128)(2,1)S(1)} %get-tuple-element.102), channel_id=1, source_target_pairs={{0,16},{8,24},{16,0},{24,8},{1,17},{9,25},{17,1},{25,9},{2,18},{10... | collective-permute-start | bytes 589832 | tf_op jit(solution)/shard_map/ppermute | solution.py:409
  100.4 14.5 %collective-permute-start.21 = (bf16[48,1536]{1,0:T(8,128)(2,1)S(1)}, bf16[48,1536]{1,0:T(8,128)(2,1)S(1)}, u32[]{:S(2)}, u32[]{:S(2)}) collective-permute-start(bf16[48,1536]{1,0:T(8,128)(2,1)S(1)} %get-tuple-element.103), channel_id=1, source_target_pairs={{0,8},{8,0},{16,24},{24,16},{1,9},{9,1},{17,25},{25,17},{2,10},{10... | collective-permute-start | bytes 442376 | tf_op jit(solution)/shard_map/ppermute | solution.py:409
  114.9 4.8 %collective-permute-start.22 = (f32[96,2048]{1,0:T(8,128)S(1)}, f32[96,2048]{1,0:T(8,128)S(1)}, u32[]{:S(2)}, u32[]{:S(2)}) collective-permute-start(f32[96,2048]{1,0:T(8,128)S(1)} %get-tuple-element.105), channel_id=1, source_target_pairs={{0,1},{1,0},{2,3},{3,2},{4,5},{5,4},{6,7},{7,6},{8,9},{9,8},{10,11... | collective-permute-start | bytes 2359304 | tf_op jit(solution)/shard_map/ppermute | solution.py:409
  115.0 14.1 %collective-permute-start.27 = (bf16[96,2048]{1,0:T(8,128)(2,1)S(1)}, bf16[96,2048]{1,0:T(8,128)(2,1)S(1)}, u32[]{:S(2)}, u32[]{:S(2)}) collective-permute-start(bf16[96,2048]{1,0:T(8,128)(2,1)S(1)} %constant_dynamic-update-slice_fusion.19.refs_5_.refs_3_), channel_id=1, source_target_pairs={{0,8},{8,0},{16,24},{24,16},{1,9},{9,1},{17,25},{25,17},{2,10},{10... | collective-permute-start | bytes 1179656 | tf_op jit(solution)/shard_map/ppermute | solution.py:409
  119.9 7.1 %collective-permute-start.24 = (bf16[48,2048]{1,0:T(8,128)(2,1)S(1)}, bf16[48,2048]{1,0:T(8,128)(2,1)S(1)}, u32[]{:S(2)}, u32[]{:S(2)}) collective-permute-start(bf16[48,2048]{1,0:T(8,128)(2,1)S(1)} %slice.151), channel_id=1, source_target_pairs={{0,2},{1,3},{2,0},{3,1},{4,6},{5,7},{6,4},{7,5},{8,10},{9,11},{10,... | collective-permute-start | bytes 589832 | tf_op jit(solution)/shard_map/ppermute | solution.py:409
  120.2 8.9 %collective-permute-start.28 = (bf16[96,1536]{1,0:T(8,128)(2,1)S(1)}, bf16[96,1536]{1,0:T(8,128)(2,1)S(1)}, u32[]{:S(2)}, u32[]{:S(2)}) collective-permute-start(bf16[96,1536]{1,0:T(8,128)(2,1)S(1)} %constant_dynamic-update-slice_fusion.21.refs_7_.refs_3_), channel_id=1, source_target_pairs={{0,16},{8,24},{16,0},{24,8},{1,17},{9,25},{17,1},{25,9},{2,18},{10... | collective-permute-start | bytes 884744 | tf_op jit(solution)/shard_map/ppermute | solution.py:409
  127.0 16.3 %collective-permute-start.26 = (bf16[24,2048]{1,0:T(8,128)(2,1)S(1)}, bf16[24,2048]{1,0:T(8,128)(2,1)S(1)}, u32[]{:S(2)}, u32[]{:S(2)}) collective-permute-start(bf16[24,2048]{1,0:T(8,128)(2,1)S(1)} %slice.155), channel_id=1, source_target_pairs={{0,4},{1,5},{2,6},{3,7},{4,0},{5,1},{6,2},{7,3},{8,12},{9,13},{10,... | collective-permute-start | bytes 294920 | tf_op jit(solution)/shard_map/ppermute | solution.py:409
  143.3 2.4 %collective-permute-start.29 = (f32[96,2048]{1,0:T(8,128)S(1)}, f32[96,2048]{1,0:T(8,128)S(1)}, u32[]{:S(2)}, u32[]{:S(2)}) collective-permute-start(f32[96,2048]{1,0:T(8,128)S(1)} %get-tuple-element.121), channel_id=1, source_target_pairs={{0,1},{1,0},{2,3},{3,2},{4,5},{5,4},{6,7},{7,6},{8,9},{9,8},{10,11... | collective-permute-start | bytes 2359304 | tf_op jit(solution)/shard_map/ppermute | solution.py:409
  146.9 7.0 %collective-permute-start.30 = (bf16[48,2048]{1,0:T(8,128)(2,1)S(1)}, bf16[48,2048]{1,0:T(8,128)(2,1)S(1)}, u32[]{:S(2)}, u32[]{:S(2)}) collective-permute-start(bf16[48,2048]{1,0:T(8,128)(2,1)S(1)} %slice.150), channel_id=1, source_target_pairs={{0,2},{1,3},{2,0},{3,1},{4,6},{5,7},{6,4},{7,5},{8,10},{9,11},{10,... | collective-permute-start | bytes 589832 | tf_op jit(solution)/shard_map/ppermute | solution.py:409
  154.0 7.2 %collective-permute-start.31 = (bf16[24,2048]{1,0:T(8,128)(2,1)S(1)}, bf16[24,2048]{1,0:T(8,128)(2,1)S(1)}, u32[]{:S(2)}, u32[]{:S(2)}) collective-permute-start(bf16[24,2048]{1,0:T(8,128)(2,1)S(1)} %slice.154), channel_id=1, source_target_pairs={{0,4},{1,5},{2,6},{3,7},{4,0},{5,1},{6,2},{7,3},{8,12},{9,13},{10,... | collective-permute-start | bytes 294920 | tf_op jit(solution)/shard_map/ppermute | solution.py:409
  (9 other events, 113.2 us)
